TPU v7x, 128 devices: a whole 4x4x4 slice. The times are simulated.
128 devices in a mesh: req: 16 (over z, y), mp: 8 (over x, core).
Axes of the slice: x: 4, y: 4, z: 4, core: 2. Of those that a mesh axis runs over, the one named last changes fastest.
Arguments:
- q_pre: bfloat16 [8192, 3072], P('req', 'mp'), may hold values from -64 to 64
- k_pre: bfloat16 [8192, 1024], P('req', 'mp'), may hold values from -64 to 64
- v_pre: bfloat16 [8192, 1024], P('req', 'mp'), may hold values from -12 to 12
- q_bias: float32 [3072], P('mp'), may hold values from -3 to 3
- k_bias: float32 [1024], P('mp'), may hold values from -3 to 3
- v_bias: float32 [1024], P('mp'), may hold values from -3 to 3
- segment_ids: int32 [8192], P('req'), may hold values from -1 to 63, as said below
- lengths: int32 [16, 4], replicated, may hold values from 64 to 128, as said below
- page_table: int32 [16, 4], replicated, may hold values from 0 to 63, as said below
- w_out: bfloat16 [3072, 5120], P('mp'), may hold values from -0.109375 to 0.109375
- residual: bfloat16 [8192, 5120], P('req'), may hold values from -4 to 4
- norm_gain: float32 [5120], replicated, may hold values from 0.1 to 1.9
- w_gate: bfloat16 [5120, 6912], P('req', 'mp'), may hold values from -0.078125 to 0.078125
- w_up: bfloat16 [5120, 6912], P('req', 'mp'), may hold values from -0.078125 to 0.078125
Outputs:
- hidden: bfloat16 [8192, 6912], P('req', 'mp')
- kv_cache: bfloat16 [64, 8, 128, 256], P('req', 'mp')
Inputs may be any that keep to these rules, and one draw needn't show every extreme that they name: Requests of block r lie in order from the block's first token, request j taking lengths[r, j] tokens; in every block one request has exactly 128 tokens. `segment_ids`: token t of block r carries r * 4 + j inside request j's run of tokens given by lengths, and -1 after the last request of its block. `page_table`: every page is named once; page p is held by req index p // 4; the requests of one block have pages held by different req indices.
All inputs are finite; a program needn't handle non-finite values.
Results may differ from a plain program's by a relative error of at most 0.019.
Values may be sent and summed in bfloat16 or wider, within the bound.
A program may use at most 128 MiB of HBM per device.

v0:
```python
import math

import jax
import jax.numpy as jnp
from jax import lax
from jax.sharding import PartitionSpec as P

HD = 128
PAGE = 128
REQS = 4


THETA = 1000000.0
EPS = 1e-06


def rotate(values, positions):
    half_dim = values.shape[-1] // 2
    frequencies = THETA ** (-jnp.arange(half_dim, dtype=jnp.float32) * (2.0 / values.shape[-1]))
    angles = positions[:, None] * frequencies[None, :]
    cosine = jnp.cos(angles)[:, None, :]
    sine_part = jnp.sin(angles)[:, None, :]
    first_half = values[..., :half_dim]
    second = values[..., half_dim:]
    return jnp.concatenate(
        [first_half * cosine - second * sine_part, second * cosine + first_half * sine_part],
        axis=-1,
    )


def attend(queries, keys, values, length):
    scale_factor = 1.0 / math.sqrt(queries.shape[-1])
    scores = (
        jnp.einsum("sqhge,skhe->shgqk", queries, keys, preferred_element_type=jnp.float32)
        * scale_factor
    )
    page_len = queries.shape[1]
    query_pos = jnp.arange(page_len)[:, None]
    key_pos = jnp.arange(page_len)[None, :]
    allowed = (key_pos <= query_pos)[None] & (key_pos[None] < length[:, None, None])
    allowed = allowed[:, None, None]
    row_max = jnp.max(jnp.where(allowed, scores, -1e30), axis=-1, keepdims=True)
    weights = jnp.where(allowed, jnp.exp(scores - row_max), 0.0)
    row_sum = jnp.sum(weights, axis=-1, keepdims=True)
    present = (jnp.arange(page_len)[None, :] < length[:, None])[:, None, None, :, None]
    row_probs = jnp.where(present, weights / jnp.where(present, row_sum, 1.0), 0.0).astype(
        jnp.bfloat16
    )
    mixed_rows = jnp.einsum(
        "shgqk,skhe->sqhge", row_probs, values, preferred_element_type=jnp.float32
    )
    return mixed_rows.astype(jnp.bfloat16)


def normalize(resid_rows, summed, gain_row):
    state = resid_rows.astype(jnp.float32) + summed
    scale_row = lax.rsqrt(jnp.mean(state * state, axis=-1, keepdims=True) + EPS)
    return (state * scale_row * gain_row).astype(jnp.bfloat16)


def shards(
    q_pre,
    k_pre,
    v_pre,
    q_bias,
    k_bias,
    v_bias,
    segment_ids,
    lengths,
    page_table,
    w_out,
    residual,
    norm_gain,
    w_gate,
    w_up,
):
    me_req = lax.axis_index("req")
    groups_all = lax.axis_size("req")
    block_rows = q_pre.shape[0]
    kv_heads = k_pre.shape[1] // HD
    q_heads = q_pre.shape[1] // HD
    group_size = q_heads // kv_heads
    own_lens = lax.dynamic_index_in_dim(lengths, me_req, 0, keepdims=False)
    own_pages = lax.dynamic_index_in_dim(page_table, me_req, 0, keepdims=False)
    own_owner = own_pages // REQS
    starts = jnp.cumsum(own_lens) - own_lens
    offsets = jnp.arange(PAGE, dtype=jnp.int32)
    row_index = jnp.clip(starts[:, None] + offsets[None, :], 0, block_rows - 1)
    flat_index = row_index.reshape(-1)
    request_ids = me_req * REQS + jnp.arange(REQS, dtype=jnp.int32)[:, None]
    inside = (offsets[None, :] < own_lens[:, None]) & (
        jnp.take(segment_ids, flat_index).reshape(REQS, PAGE) == request_ids
    )
    keep_mask = inside[:, :, None, None]
    positions = offsets.astype(jnp.float32)

    def prepare(source, bias_row, head_count):
        picked = jnp.take(source, flat_index, axis=0).astype(jnp.float32) + bias_row
        return picked.reshape(REQS, PAGE, head_count, HD)

    query_req = jnp.where(
        keep_mask, rotate(prepare(q_pre, q_bias, q_heads), positions), 0.0
    ).astype(jnp.bfloat16)
    key_req = jnp.where(keep_mask, rotate(prepare(k_pre, k_bias, kv_heads), positions), 0.0).astype(
        jnp.bfloat16
    )
    value_req = jnp.where(keep_mask, prepare(v_pre, v_bias, kv_heads), 0.0).astype(jnp.bfloat16)
    to_owner = (own_owner[None, :] == jnp.arange(groups_all)[:, None]).astype(jnp.bfloat16)
    alive_rows = segment_ids >= 0
    req_idx = jnp.clip(segment_ids - me_req * REQS, 0, REQS - 1)
    req_hit = req_idx[:, None] == jnp.arange(REQS)[None, :]
    row_start = jnp.sum(jnp.where(req_hit, starts[None, :], 0), axis=1)
    row_pos = jnp.clip(jnp.arange(block_rows, dtype=jnp.int32) - row_start, 0, PAGE - 1)
    hits = (
        page_table[None, :, :] == (me_req * REQS + jnp.arange(REQS, dtype=jnp.int32))[:, None, None]
    )
    page_select = jnp.sum(hits.astype(jnp.int32), axis=2).astype(jnp.bfloat16)
    q_send = jnp.einsum(
        "gj,jpc->gpc",
        to_owner,
        query_req.reshape(REQS, PAGE, q_heads * HD),
        preferred_element_type=jnp.float32,
    ).astype(jnp.bfloat16)
    k_send = jnp.einsum(
        "gj,jpc->gpc",
        to_owner,
        key_req.reshape(REQS, PAGE, kv_heads * HD),
        preferred_element_type=jnp.float32,
    ).astype(jnp.bfloat16)
    v_send = jnp.einsum(
        "gj,jpc->gpc",
        to_owner,
        value_req.reshape(REQS, PAGE, kv_heads * HD),
        preferred_element_type=jnp.float32,
    ).astype(jnp.bfloat16)
    q_in, k_in, v_in = (
        lax.all_to_all(q_send, "req", split_axis=0, concat_axis=0, tiled=True),
        lax.all_to_all(k_send, "req", split_axis=0, concat_axis=0, tiled=True),
        lax.all_to_all(v_send, "req", split_axis=0, concat_axis=0, tiled=True),
    )
    in_len = jnp.sum(jnp.where(page_table // REQS == me_req, lengths, 0), axis=1)
    q_groups = q_in.reshape(groups_all, PAGE, kv_heads, group_size, HD)
    k_groups = k_in.reshape(groups_all, PAGE, kv_heads, HD)
    v_groups = v_in.reshape(groups_all, PAGE, kv_heads, HD)
    pages_in = jnp.concatenate([k_groups, v_groups], axis=-1).transpose(0, 2, 1, 3)
    attended = attend(q_groups, k_groups, v_groups, in_len)
    returned = lax.all_to_all(
        attended.reshape(groups_all, PAGE, q_heads * HD),
        "req",
        split_axis=0,
        concat_axis=0,
        tiled=True,
    )
    row_group = jnp.sum(jnp.where(req_hit, own_owner[None, :], 0), axis=1)
    source_rows = jnp.take(
        returned.reshape(groups_all * PAGE, q_heads * HD), row_group * PAGE + row_pos, axis=0
    )
    cache_out = jnp.einsum(
        "ls,shpc->lhpc", page_select, pages_in, preferred_element_type=jnp.float32
    ).astype(jnp.bfloat16)
    attn_rows = jnp.where(alive_rows[:, None], source_rows, jnp.zeros((), jnp.bfloat16))
    summed = lax.psum(
        jnp.dot(attn_rows, w_out, preferred_element_type=jnp.float32).astype(jnp.bfloat16), "mp"
    ).astype(jnp.float32)
    normed = normalize(residual, summed, norm_gain)
    gate_acc = jnp.dot(
        normed,
        lax.all_gather(w_gate, "req", axis=0, tiled=True),
        preferred_element_type=jnp.float32,
    )
    up_acc = jnp.dot(
        normed, lax.all_gather(w_up, "req", axis=0, tiled=True), preferred_element_type=jnp.float32
    )
    hidden = (jax.nn.silu(gate_acc) * up_acc).astype(jnp.bfloat16)
    return (hidden, cache_out)


def solution(mesh):
    in_specs = (
        P("req", "mp"),
        P("req", "mp"),
        P("req", "mp"),
        P("mp"),
        P("mp"),
        P("mp"),
        P("req"),
        P(),
        P(),
        P("mp", None),
        P("req", None),
        P(),
        P("req", "mp"),
        P("req", "mp"),
    )
    out_specs = (P("req", "mp"), P("req", "mp", None, None))
    return jax.shard_map(shards, mesh=mesh, in_specs=in_specs, out_specs=out_specs, check_vma=False)
```

profile of v0, /device:TPU:0, one launch (start us, length us, event | category | flops | bytes accessed | tf_op | source)
XLA Modules:
  0.0 290.2 jit_solution(10564905103255792273)
XLA Ops:
  9.8 3.6 %gather_fusion = s32[512]{0:T(512)S(1)} fusion(s32[512]{0:T(512)} %param.22, s32[1024]{0:T(1024)S(1)} %pad_clamp_fusion.2), kind=kCustom, calls=%fused_computation.2 | custom fusion | bytes 6144 | tf_op jit(solution)/shard_map/jit(_take)/gather | solution.py:92
  13.4 1.9 gather_fusion.1
  18.1 1.5 copy.81
  19.6 8.1 %all-to-all-start.2 = ((bf16[16,128,384]{2,1,0:T(8,128)(2,1)}), bf16[16,128,384]{2,1,0:T(8,128)(2,1)S(1)}, u32[]{:S(2)}, u32[]{:S(2)}) async-start(bf16[16,128,384]{2,1,0:T(8,128)(2,1)} %copy.81), calls=%async_computation.2 | async-start | bytes 3145728 | tf_op jit(solution)/shard_map/all_to_all | solution.py:137
  28.3 1.3 gather_fusion.4
  31.9 1.3 gather_fusion.3
  34.0 18.2 %all-to-all-done.2 = bf16[16,128,384]{2,1,0:T(8,128)(2,1)S(1)} async-done(((bf16[16,128,384]{2,1,0:T(8,128)(2,1)}), bf16[16,128,384]{2,1,0:T(8,128)(2,1)S(1)}, u32[]{:S(2)}, u32[]{:S(2)}) %all-to-all-start.2) | async-done | bytes 1572896 | tf_op jit(solution)/shard_map/all_to_all | solution.py:137
  52.2 3.6 %all-to-all-start.1 = ((bf16[16,128,128]{2,1,0:T(8,128)(2,1)}), bf16[16,128,128]{2,1,0:T(8,128)(2,1)S(1)}, u32[]{:S(2)}, u32[]{:S(2)}) async-start(bf16[16,128,128]{2,1,0:T(8,128)(2,1)} %copy.77), calls=%async_computation.1 | async-start | bytes 1048576 | tf_op jit(solution)/shard_map/all_to_all | solution.py:138
  57.2 1.7 copy.82
  58.8 7.9 %all-to-all-done.1 = bf16[16,128,128]{2,1,0:T(8,128)(2,1)S(1)} async-done(((bf16[16,128,128]{2,1,0:T(8,128)(2,1)}), bf16[16,128,128]{2,1,0:T(8,128)(2,1)S(1)}, u32[]{:S(2)}, u32[]{:S(2)}) %all-to-all-start.1) | async-done | bytes 524320 | tf_op jit(solution)/shard_map/all_to_all | solution.py:138
  66.7 4.2 %all-to-all-start = ((bf16[16,128,128]{2,1,0:T(8,128)(2,1)}), bf16[16,128,128]{2,1,0:T(8,128)(2,1)}, u32[]{:S(2)}, u32[]{:S(2)}) async-start(bf16[16,128,128]{2,1,0:T(8,128)(2,1)} %copy.72), calls=%async_computation | async-start | bytes 1048576 | tf_op jit(solution)/shard_map/all_to_all | solution.py:139
  71.0 2.2 fusion
  74.1 7.0 %all-to-all-done = bf16[16,128,128]{2,1,0:T(8,128)(2,1)} async-done(((bf16[16,128,128]{2,1,0:T(8,128)(2,1)}), bf16[16,128,128]{2,1,0:T(8,128)(2,1)}, u32[]{:S(2)}, u32[]{:S(2)}) %all-to-all-start) | async-done | bytes 524320 | tf_op jit(solution)/shard_map/all_to_all | solution.py:139
  81.1 3.3 %convolution_convert_fusion.1 = bf16[16,128,3,128]{3,1,2,0:T(8,128)(2,1)} fusion(f32[16,128,128,3]{2,1,3,0:T(8,128)S(1)} %get-tuple-element.24, f32[16,3,128]{2,1,0:T(4,128)S(1)} %broadcast_select_fusion, f32[16,3,128]{2,1,0:T(4,128)S(1)} %get-tuple-element.23, pred[16,128,128]{1,2,0:T(8,128)(4,1)S(1)} %broadcast_and_fusion, ...), kind=kOutput, calls=%fused_computation.17 | convolution fusion | flops 206831616 | bytes 5556224 | tf_op jit(solution)/shard_map/shgqk,skhe->sqhge/dot_general | solution.py:49
  84.5 4.0 %all-to-all-start.3 = ((bf16[16,128,384]{1,2,0:T(8,128)(2,1)}), bf16[16,128,384]{1,2,0:T(8,128)(2,1)S(1)}, u32[]{:S(2)}, u32[]{:S(2)}) async-start(bf16[16,128,384]{1,2,0:T(8,128)(2,1)} %bitcast.106), calls=%async_computation.3 | async-start | bytes 3145728 | tf_op jit(solution)/shard_map/all_to_all | solution.py:147
  89.3 20.9 %all-to-all-done.3 = bf16[16,128,384]{1,2,0:T(8,128)(2,1)S(1)} async-done(((bf16[16,128,384]{1,2,0:T(8,128)(2,1)}), bf16[16,128,384]{1,2,0:T(8,128)(2,1)S(1)}, u32[]{:S(2)}, u32[]{:S(2)}) %all-to-all-start.3) | async-done | bytes 1572896 | tf_op jit(solution)/shard_map/all_to_all | solution.py:147
  111.0 1.9 gather_fusion.2
  113.0 6.9 %convolution_convert_fusion = bf16[512,5120]{1,0:T(8,128)(2,1)} fusion(bf16[384,5120]{1,0:T(8,128)(2,1)} %param.25, bf16[512,384]{1,0:T(8,128)(2,1)S(1)} %gather_fusion.2, pred[512]{0:T(512)(128)(4,1)S(1)} %copy-done.12, pred[512]{0:T(512)(128)(4,1)S(1)} %broadcast_compare_fusion), kind=kOutput, calls=%fused_computation.8 | convolution fusion | flops 2016280576 | bytes 9569280 | tf_op jit(solution)/shard_map/dot_general | solution.py:163
  121.5 1.4 copy.109
  124.0 71.2 %all-reduce.2.cloned.1.call-done = bf16[512,5120]{1,0:T(8,128)(2,1)} async-done(((bf16[512,5120]{1,0:T(8,128)(2,1)}), bf16[512,5120]{1,0:T(8,128)(2,1)}) %all-reduce.2.cloned.1.call-update) | async-done | bytes 5242896 | tf_op jit(solution)/shard_map/psum | solution.py:162
  195.1 5.8 %multiply_reduce_fusion = f32[512]{0:T(512)S(1)} fusion(bf16[512,5120]{1,0:T(8,128)(2,1)} %all-reduce.2.cloned.1.call-done, bf16[512,5120]{1,0:T(8,128)(2,1)} %param.26), kind=kLoop, calls=%fused_computation.6 | loop fusion | flops 13106688 | bytes 10487808 | tf_op jit(solution)/shard_map/reduce_sum | solution.py:57
  201.0 12.5 %fusion.51 = f32[512,864]{0,1:T(8,128)S(1)} fusion(bf16[5120,864]{1,0:T(8,128)(2,1)} %all-gather.3.cloned.1.call-done, bf16[512,5120]{1,0:T(8,128)(2,1)} %all-reduce.2.cloned.1.call-done, bf16[512,5120]{1,0:T(8,128)(2,1)} %param.26, f32[5120]{0:T(1024)S(1)} %copy-done.13, f32[512]{0:T(512)S(1)} %add_rsqrt_fusion), kind=kOutput, calls=%fused_computation.124 | convolution fusion | flops 4545576960 | bytes 21125120 | tf_op jit(solution)/shard_map/dot_general | solution.py:166
  213.4 56.5 %all-gather.5.cloned.1.call-done = bf16[5120,864]{1,0:T(8,128)(2,1)} async-done(((bf16[320,864]{1,0:T(8,128)(2,1)}), bf16[5120,864]{1,0:T(8,128)(2,1)}) %all-gather.5.cloned.1.call-update) | async-done | bytes 8847376 | tf_op jit(solution)/shard_map/all_gather | solution.py:172
  269.9 12.8 %multiply_convert_fusion.1 = bf16[512,864]{0,1:T(8,128)(2,1)} fusion(f32[512,864]{0,1:T(8,128)S(1)} %fusion.51, bf16[5120,864]{1,0:T(8,128)(2,1)} %all-gather.5.cloned.1.call-done, bf16[512,5120]{1,0:T(8,128)(2,1)} %all-reduce.2.cloned.1.call-done, bf16[512,5120]{1,0:T(8,128)(2,1)} %param.26, f32[5120]{0:T(1024)S(1)} %copy-done.13, f32[512]{0:T(512)S(1)} %add_rsqrt_fusion), kind=kOutput, calls=%fused_computation.16 | convolution fusion | flops 4548231168 | bytes 22009856 | tf_op jit(solution)/shard_map/dot_general | solution.py:171
  (94 shorter events, 14.3 us)
Async XLA Ops:
  8.0 5.4 %copy-start = (bf16[512,384]{1,0:T(8,128)(2,1)S(1)}, bf16[512,384]{1,0:T(8,128)(2,1)}, u32[]{:S(2)}) copy-start(bf16[512,384]{1,0:T(8,128)(2,1)} %param.16) | copy-start | bytes 1179652
  9.3 0.5 copy-start.14
  9.8 6.2 %copy-start.9 = (f32[384]{0:T(512)S(1)}, f32[384]{0:T(512)}, u32[]{:S(2)}) copy-start(f32[384]{0:T(512)} %param.19) | copy-start | bytes 4612
  18.1 10.2 %copy-start.3 = (bf16[512,128]{1,0:T(8,128)(2,1)S(1)}, bf16[512,128]{1,0:T(8,128)(2,1)}, u32[]{:S(2)}) copy-start(bf16[512,128]{1,0:T(8,128)(2,1)} %param.17) | copy-start | bytes 393220
  18.1 11.6 %copy-start.10 = (f32[128]{0:T(128)S(1)}, f32[128]{0:T(128)}, u32[]{:S(2)}) copy-start(f32[128]{0:T(128)} %param.20) | copy-start | bytes 1540
  19.6 32.6 %all-to-all-start.2 = ((bf16[16,128,384]{2,1,0:T(8,128)(2,1)}), bf16[16,128,384]{2,1,0:T(8,128)(2,1)S(1)}, u32[]{:S(2)}, u32[]{:S(2)}) async-start(bf16[16,128,384]{2,1,0:T(8,128)(2,1)} %copy.81), calls=%async_computation.2 | async-start | bytes 3145728 | tf_op jit(solution)/shard_map/all_to_all | solution.py:137
  27.8 4.2 %copy-start.4 = (bf16[512,128]{1,0:T(8,128)(2,1)S(1)}, bf16[512,128]{1,0:T(8,128)(2,1)}, u32[]{:S(2)}) copy-start(bf16[512,128]{1,0:T(8,128)(2,1)} %param.18) | copy-start | bytes 393220
  28.3 5.0 %copy-start.7 = (s32[16,4]{0,1:T(4,128)S(1)}, s32[16,4]{0,1:T(4,128)}, u32[]{:S(2)}) copy-start(s32[16,4]{0,1:T(4,128)} %param.24) | copy-start | bytes 772
  28.3 5.0 %copy-start.8 = (s32[16,4]{0,1:T(4,128)S(1)}, s32[16,4]{0,1:T(4,128)}, u32[]{:S(2)}) copy-start(s32[16,4]{0,1:T(4,128)} %param.23) | copy-start | bytes 772
  28.3 5.0 %copy-start.11 = (f32[128]{0:T(128)S(1)}, f32[128]{0:T(128)}, u32[]{:S(2)}) copy-start(f32[128]{0:T(128)} %param.21) | copy-start | bytes 1540
  52.2 14.5 %all-to-all-start.1 = ((bf16[16,128,128]{2,1,0:T(8,128)(2,1)}), bf16[16,128,128]{2,1,0:T(8,128)(2,1)S(1)}, u32[]{:S(2)}, u32[]{:S(2)}) async-start(bf16[16,128,128]{2,1,0:T(8,128)(2,1)} %copy.77), calls=%async_computation.1 | async-start | bytes 1048576 | tf_op jit(solution)/shard_map/all_to_all | solution.py:138
  66.7 4.2 %copy-start.5 = (bf16[16,128,128]{2,1,0:T(8,128)(2,1)}, bf16[16,128,128]{2,1,0:T(8,128)(2,1)S(1)}, u32[]{:S(2)}) copy-start(bf16[16,128,128]{2,1,0:T(8,128)(2,1)S(1)} %all-to-all-done.1) | copy-start | bytes 1572868
  66.7 14.4 %all-to-all-start = ((bf16[16,128,128]{2,1,0:T(8,128)(2,1)}), bf16[16,128,128]{2,1,0:T(8,128)(2,1)}, u32[]{:S(2)}, u32[]{:S(2)}) async-start(bf16[16,128,128]{2,1,0:T(8,128)(2,1)} %copy.72), calls=%async_computation | async-start | bytes 1048576 | tf_op jit(solution)/shard_map/all_to_all | solution.py:139
  84.5 4.1 %copy-start.15 = (s32[4,1]{0,1:T(1,128)S(1)}, s32[4,1]{0,1:T(1,128)}, u32[]{:S(2)}) copy-start(s32[4,1]{0,1:T(1,128)} %copy-done.14) | copy-start | bytes 52
  84.5 4.1 %copy-start.2 = (s32[512]{0:T(512)S(1)}, s32[512]{0:T(512)}, u32[]{:S(2)}) copy-start(s32[512]{0:T(512)} %param.22) | copy-start | bytes 6148
  84.5 25.7 %all-to-all-start.3 = ((bf16[16,128,384]{1,2,0:T(8,128)(2,1)}), bf16[16,128,384]{1,2,0:T(8,128)(2,1)S(1)}, u32[]{:S(2)}, u32[]{:S(2)}) async-start(bf16[16,128,384]{1,2,0:T(8,128)(2,1)} %bitcast.106), calls=%async_computation.3 | async-start | bytes 3145728 | tf_op jit(solution)/shard_map/all_to_all | solution.py:147
  88.5 106.6 %all-reduce.2.cloned.1.call-start = ((), (), s32[]{:S(2)}) async-start(), calls=%async_computation.4 | async-start | bytes 10485760 | tf_op jit(solution)/shard_map/psum | solution.py:162
  111.0 2.0 copy-start.12
  119.9 1.3 copy-start.6
  119.9 81.0 %all-gather.3.cloned.1.call-start = ((), (), s32[]{:S(2)}) async-start(), calls=%async_computation.5 | async-start | bytes 9748480 | tf_op jit(solution)/shard_map/all_gather | solution.py:168
  120.5 149.4 %all-gather.5.cloned.1.call-start = ((), (), s32[]{:S(2)}) async-start(), calls=%async_computation.6 | async-start | bytes 9748480 | tf_op jit(solution)/shard_map/all_gather | solution.py:172
  123.9 77.0 %copy-start.13 = (f32[5120]{0:T(1024)S(1)}, f32[5120]{0:T(1024)}, u32[]{:S(2)}) copy-start(f32[5120]{0:T(1024)} %param.27) | copy-start | bytes 61444
  269.9 12.8 %copy-start.1 = (bf16[512,384]{1,0:T(8,128)(2,1)S(1)}, bf16[512,384]{1,0:T(8,128)(2,1)}, u32[]{:S(2)}) copy-start(bf16[512,384]{1,0:T(8,128)(2,1)} %param.16) | copy-start | bytes 1179652
Sparse Core Ops, SparseCore 0:
  120.0 75.0 all-reduce.1
Sparse Core Ops, SparseCore 1:
  122.5 71.2 all-gather.2
  195.8 74.0 all-gather.4
where the time goes:
time: 291 us; the launch traced here: 290 us
  waiting for transfers between devices  183 us (63%)
  matrix products  39.9 us (14%)
  local copies, waits for them, and re-layouts  20.2 us (7%)
  starting transfers between devices  20.1 us (7%)
  between operations  16 us (5%)
  other arithmetic  11.3 us (4%)
    psum x1, waiting for transfers between devices, shards(): lax.psum(jnp.dot(attn_rows, w_out, preferred_element_type=jnp.float32).as...  71.2 us
    all_gather x1, waiting for transfers between devices, shards(): lax.all_gather(w_up, 'req', axis=0, tiled=True)  56.5 us
    all_to_all x1, waiting for transfers between devices, shards(): lax.all_to_all(attended.reshape(groups_all, PAGE, q_heads * HD), 'req', s...  20.9 us
    all_to_all x1, waiting for transfers between devices, shards(): lax.all_to_all(q_send, 'req', split_axis=0, concat_axis=0, tiled=True)  18.2 us
    dot_general x1, matrix products, shards(): jnp.dot(normed, lax.all_gather(w_up, 'req', axis=0, tiled=True), preferre...  12.8 us
    dot_general x1, matrix products, shards(): jnp.dot(normed, lax.all_gather(w_gate, 'req', axis=0, tiled=True), prefer...  12.5 us
    all_to_all x1, starting transfers between devices, shards(): lax.all_to_all(q_send, 'req', split_axis=0, concat_axis=0, tiled=True)  8.13 us
    all_to_all x1, waiting for transfers between devices, shards(): lax.all_to_all(k_send, 'req', split_axis=0, concat_axis=0, tiled=True)  7.9 us
  transfers between devices with their start and end apart: 7, of which 6 were waited for; matrix products, arithmetic and copies ran while one was open for 12% of the time, Pallas kernels for 0%

commit v1 on v0

v1 whole, which is shorter than its diff:
```python
import math

import jax
import jax.numpy as jnp
from jax import lax
from jax.sharding import PartitionSpec as P

HD = 128
PAGE = 128
REQS = 4


THETA = 1000000.0
EPS = 1e-06


def rotate(values, positions):
    half_dim = values.shape[-1] // 2
    frequencies = THETA ** (-jnp.arange(half_dim, dtype=jnp.float32) * (2.0 / values.shape[-1]))
    angles = positions[:, None] * frequencies[None, :]
    cosine = jnp.cos(angles)[:, None, :]
    sine_part = jnp.sin(angles)[:, None, :]
    first_half = values[..., :half_dim]
    second = values[..., half_dim:]
    return jnp.concatenate(
        [first_half * cosine - second * sine_part, second * cosine + first_half * sine_part],
        axis=-1,
    )


def normalize(resid_rows, summed, gain_row):
    state = resid_rows.astype(jnp.float32) + summed
    scale_row = lax.rsqrt(jnp.mean(state * state, axis=-1, keepdims=True) + EPS)
    return (state * scale_row * gain_row).astype(jnp.bfloat16)


def shards(
    q_pre,
    k_pre,
    v_pre,
    q_bias,
    k_bias,
    v_bias,
    segment_ids,
    lengths,
    page_table,
    w_out,
    residual,
    norm_gain,
    w_gate,
    w_up,
):
    me_req = lax.axis_index("req")
    groups_all = lax.axis_size("req")
    block_rows = q_pre.shape[0]
    kv_heads = k_pre.shape[1] // HD
    q_heads = q_pre.shape[1] // HD
    group_size = q_heads // kv_heads

    wg_full = lax.all_gather(w_gate, "req", axis=0, tiled=True)
    wu_full = lax.all_gather(w_up, "req", axis=0, tiled=True)

    own_lens = lax.dynamic_index_in_dim(lengths, me_req, 0, keepdims=False)
    own_pages = lax.dynamic_index_in_dim(page_table, me_req, 0, keepdims=False)
    own_owner = own_pages // REQS
    starts = jnp.cumsum(own_lens) - own_lens

    alive = segment_ids >= 0
    req_idx = jnp.clip(segment_ids - me_req * REQS, 0, REQS - 1)
    req_hit = req_idx[:, None] == jnp.arange(REQS)[None, :]
    row_start = jnp.sum(jnp.where(req_hit, starts[None, :], 0), axis=1)
    token = jnp.arange(block_rows, dtype=jnp.int32)
    positions = (token - row_start).astype(jnp.float32)
    keep = alive[:, None, None]

    queries = rotate(
        (q_pre.astype(jnp.float32) + q_bias).reshape(block_rows, q_heads, HD), positions
    )
    queries = jnp.where(keep, queries, 0.0).astype(jnp.bfloat16)
    keys = rotate((k_pre.astype(jnp.float32) + k_bias).reshape(block_rows, kv_heads, HD), positions)
    keys = jnp.where(keep, keys, 0.0).astype(jnp.bfloat16)
    values = (v_pre.astype(jnp.float32) + v_bias).reshape(block_rows, kv_heads, HD)
    values = jnp.where(keep, values, 0.0).astype(jnp.bfloat16)

    scale_factor = 1.0 / math.sqrt(HD)
    q_groups = queries.reshape(block_rows, kv_heads, group_size, HD)
    scores = (
        jnp.einsum("qhge,khe->hgqk", q_groups, keys, preferred_element_type=jnp.float32)
        * scale_factor
    )
    allowed = (
        (segment_ids[:, None] == segment_ids[None, :])
        & alive[None, :]
        & (token[None, :] <= token[:, None])
    )[None, None]
    row_max = jnp.max(jnp.where(allowed, scores, -1e30), axis=-1, keepdims=True)
    weights = jnp.where(allowed, jnp.exp(scores - row_max), 0.0)
    row_sum = jnp.sum(weights, axis=-1, keepdims=True)
    present = alive[None, None, :, None]
    probs = jnp.where(present, weights / jnp.where(present, row_sum, 1.0), 0.0).astype(
        jnp.bfloat16
    )
    attended = jnp.einsum("hgqk,khe->qhge", probs, values, preferred_element_type=jnp.float32)
    attended = attended.astype(jnp.bfloat16).reshape(block_rows, q_heads * HD)

    kv_rows = jnp.concatenate([keys, values], axis=-1)
    kv_rows = jnp.pad(kv_rows, ((0, PAGE), (0, 0), (0, 0)))
    slot = jnp.arange(PAGE, dtype=jnp.int32)
    pages = []
    for j in range(REQS):
        page = lax.dynamic_slice_in_dim(kv_rows, starts[j], PAGE, axis=0)
        page = jnp.where((slot < own_lens[j])[:, None, None], page, jnp.zeros((), jnp.bfloat16))
        pages.append(page)
    pages = jnp.stack(pages)
    to_owner = (own_owner[None, :] == jnp.arange(groups_all)[:, None]).astype(jnp.bfloat16)
    kv_send = jnp.einsum(
        "gj,jphc->gphc", to_owner, pages, preferred_element_type=jnp.float32
    ).astype(jnp.bfloat16)
    kv_in = lax.all_to_all(kv_send, "req", split_axis=0, concat_axis=0, tiled=True)
    hits = (
        page_table[None, :, :] == (me_req * REQS + jnp.arange(REQS, dtype=jnp.int32))[:, None, None]
    )
    page_select = jnp.sum(hits.astype(jnp.int32), axis=2).astype(jnp.bfloat16)
    cache_out = jnp.einsum(
        "ls,sphc->lhpc", page_select, kv_in, preferred_element_type=jnp.float32
    ).astype(jnp.bfloat16)

    summed = lax.psum(
        jnp.dot(attended, w_out, preferred_element_type=jnp.float32).astype(jnp.bfloat16), "mp"
    ).astype(jnp.float32)
    normed = normalize(residual, summed, norm_gain)
    gate_acc = jnp.dot(normed, wg_full, preferred_element_type=jnp.float32)
    up_acc = jnp.dot(normed, wu_full, preferred_element_type=jnp.float32)
    hidden = (jax.nn.silu(gate_acc) * up_acc).astype(jnp.bfloat16)
    return (hidden, cache_out)


def solution(mesh):
    in_specs = (
        P("req", "mp"),
        P("req", "mp"),
        P("req", "mp"),
        P("mp"),
        P("mp"),
        P("mp"),
        P("req"),
        P(),
        P(),
        P("mp", None),
        P("req", None),
        P(),
        P("req", "mp"),
        P("req", "mp"),
    )
    out_specs = (P("req", "mp"), P("req", "mp", None, None))
    return jax.shard_map(shards, mesh=mesh, in_specs=in_specs, out_specs=out_specs, check_vma=False)
```

time: 291 us -> 212 us (0.73)
  waiting for transfers between devices: 183 us -> 123 us
  local copies, waits for them, and re-layouts: 20.2 us -> 6.03 us
  starting transfers between devices: 20.1 us -> 8.26 us
  between operations: 16 us -> 23.5 us
  matrix products: 39.9 us -> 33.1 us
  other arithmetic: 11.3 us -> 16.9 us
    all_to_all x4 -> x1, waiting for transfers between devices: 54 us -> 18.8 us  [shards(): lax.all_to_all(kv_send, 'req', split_axis=0, concat_axis=0, tiled=True)]
    psum x1, waiting for transfers between devices: 71.2 us -> 36.1 us  [shards(): lax.psum(jnp.dot(attended, w_out, preferred_element_type=jnp.float32).ast...]
    all_to_all x4 -> x1, starting transfers between devices: 20 us -> 8.14 us  [shards(): lax.all_to_all(kv_send, 'req', split_axis=0, concat_axis=0, tiled=True)]
    gather x7 -> x0, local copies, waits for them, and re-layouts: 10.5 us -> none  [the longest x5 4.89 us: prepare(): picked = jnp.take(source, flat_index, axis=0).astype(jnp.float32) + bias_row]
    all_gather x2, waiting for transfers between devices: 56.5 us -> 66.7 us  [the longest x1 64 us: shards(): wu_full = lax.all_gather(w_up, 'req', axis=0, tiled=True)]
    dot_general x9 -> x7, matrix products: 39.9 us -> 33.1 us  [the longest x1 12.7 us: shards(): up_acc = jnp.dot(normed, wu_full, preferred_element_type=jnp.float32)]
    all_to_all x4 -> x0, local copies, waits for them, and re-layouts: 4.25 us -> none  [the longest x1 1.66 us: shards(): lax.all_to_all(q_send, 'req', split_axis=0, concat_axis=0, tiled=True)]
  transfers between devices with their start and end apart: 7 -> 4, of which waited for: 6 -> 4; matrix products, arithmetic and copies ran while one was open for 12% -> 13% of each run, Pallas kernels for 0% -> 0%
where the time goes in v1:
time: 212 us; the launch traced here: 211 us
  waiting for transfers between devices  123 us (58%)
  matrix products  33.1 us (16%)
  between operations  23.5 us (11%)
  other arithmetic  16.9 us (8%)
  starting transfers between devices  8.26 us (4%)
  local copies, waits for them, and re-layouts  6.03 us (3%)
    all_gather x1, waiting for transfers between devices, shards(): wu_full = lax.all_gather(w_up, 'req', axis=0, tiled=True)  64 us
    psum x1, waiting for transfers between devices, shards(): lax.psum(jnp.dot(attended, w_out, preferred_element_type=jnp.float32).ast...  36.1 us
    all_to_all x1, waiting for transfers between devices, shards(): lax.all_to_all(kv_send, 'req', split_axis=0, concat_axis=0, tiled=True)  18.8 us
    dot_general x1, matrix products, shards(): up_acc = jnp.dot(normed, wu_full, preferred_element_type=jnp.float32)  12.7 us
    dot_general x1, matrix products, shards(): gate_acc = jnp.dot(normed, wg_full, preferred_element_type=jnp.float32)  12.1 us
    all_to_all x1, starting transfers between devices, shards(): lax.all_to_all(kv_send, 'req', split_axis=0, concat_axis=0, tiled=True)  8.14 us
    reduce_sum x1, other arithmetic, normalize(): scale_row = lax.rsqrt(jnp.mean(state * state, axis=-1, keepdims=True) + EPS)  5.83 us
    dot_general x1, matrix products, shards(): jnp.dot(attended, w_out, preferred_element_type=jnp.float32)  4.72 us
  transfers between devices with their start and end apart: 4, of which 4 were waited for; matrix products, arithmetic and copies ran while one was open for 13% of the time, Pallas kernels for 0%

profile of v1, /device:TPU:0, one launch (start us, length us, event | category | flops | bytes accessed | tf_op | source)
XLA Modules:
  0.0 210.5 jit_solution(10629385373972112505)
XLA Ops:
  8.1 0.9 fusion.45
  9.2 0.7 broadcast_compare_fusion
  10.7 1.2 copy.81
  12.4 0.9 add_bitcast_fusion
  13.3 1.2 fusion.28
  14.6 1.0 fusion.15
  15.6 0.8 convert_add_fusion.1
  16.6 0.8 fusion
  17.4 0.7 fusion.3
  18.1 1.2 fusion.9
  19.3 0.9 copy-done
  20.2 4.7 %convolution_convert_fusion = bf16[512,5120]{1,0:T(8,128)(2,1)} fusion(bf16[512,384]{0,1:T(8,128)(2,1)S(1)} %bitcast.97, bf16[384,5120]{1,0:T(8,128)(2,1)S(1)} %copy-done), kind=kOutput, calls=%fused_computation.3 | convolution fusion | flops 2015887360 | bytes 9568256 | tf_op jit(solution)/shard_map/dot_general | solution.py:129
  35.9 0.7 iota_compare_fusion.5
  38.9 0.9 fusion.8
  39.8 1.4 copy.89
  41.2 8.1 %all-to-all-start = ((bf16[16,128,1,256]{3,1,2,0:T(8,128)(2,1)}), bf16[16,128,1,256]{3,1,2,0:T(8,128)(2,1)S(1)}, u32[]{:S(2)}, u32[]{:S(2)}) async-start(bf16[16,128,1,256]{3,1,2,0:T(8,128)(2,1)} %copy.89), calls=%async_computation | async-start | bytes 2097152 | tf_op jit(solution)/shard_map/all_to_all | solution.py:119
  49.4 18.8 %all-to-all-done = bf16[16,128,1,256]{3,1,2,0:T(8,128)(2,1)S(1)} async-done(((bf16[16,128,1,256]{3,1,2,0:T(8,128)(2,1)}), bf16[16,128,1,256]{3,1,2,0:T(8,128)(2,1)S(1)}, u32[]{:S(2)}, u32[]{:S(2)}) %all-to-all-start) | async-done | bytes 1048608 | tf_op jit(solution)/shard_map/all_to_all | solution.py:119
  68.9 0.7 copy.91
  69.7 36.1 %all-reduce.3.cloned.1.call-done = bf16[512,5120]{1,0:T(8,128)(2,1)} async-done(((bf16[512,5120]{1,0:T(8,128)(2,1)}), bf16[512,5120]{1,0:T(8,128)(2,1)}) %all-reduce.3.cloned.1.call-update) | async-done | bytes 5242896 | tf_op jit(solution)/shard_map/psum | solution.py:128
  105.8 5.8 %multiply_reduce_fusion = f32[512]{0:T(512)S(1)} fusion(bf16[512,5120]{1,0:T(8,128)(2,1)} %all-reduce.3.cloned.1.call-done, bf16[512,5120]{1,0:T(8,128)(2,1)} %param.24), kind=kLoop, calls=%fused_computation.1 | loop fusion | flops 13106688 | bytes 10487808 | tf_op jit(solution)/shard_map/reduce_sum | solution.py:33
  111.6 2.6 %all-gather.3.cloned.1.call-done = bf16[5120,864]{1,0:T(8,128)(2,1)} async-done(((bf16[320,864]{1,0:T(8,128)(2,1)}), bf16[5120,864]{1,0:T(8,128)(2,1)}) %all-gather.3.cloned.1.call-update) | async-done | bytes 8847376 | tf_op jit(solution)/shard_map/all_gather | solution.py:60
  114.3 12.1 %fusion.58 = f32[512,864]{0,1:T(8,128)S(1)} fusion(bf16[5120,864]{1,0:T(8,128)(2,1)} %all-gather.3.cloned.1.call-done, bf16[512,5120]{1,0:T(8,128)(2,1)} %all-reduce.3.cloned.1.call-done, bf16[512,5120]{1,0:T(8,128)(2,1)} %param.24, f32[5120]{0:T(1024)S(1)} %copy-done.4, f32[512]{0:T(512)S(1)} %add_rsqrt_fusion), kind=kOutput, calls=%fused_computation.105 | convolution fusion | flops 4545576960 | bytes 21125120 | tf_op jit(solution)/shard_map/dot_general | solution.py:132
  126.3 64.0 %all-gather.5.cloned.1.call-done = bf16[5120,864]{1,0:T(8,128)(2,1)} async-done(((bf16[320,864]{1,0:T(8,128)(2,1)}), bf16[5120,864]{1,0:T(8,128)(2,1)}) %all-gather.5.cloned.1.call-update) | async-done | bytes 8847376 | tf_op jit(solution)/shard_map/all_gather | solution.py:61
  190.4 12.7 %multiply_convert_fusion.1 = bf16[512,864]{0,1:T(8,128)(2,1)} fusion(f32[512,864]{0,1:T(8,128)S(1)} %fusion.58, bf16[5120,864]{1,0:T(8,128)(2,1)} %all-gather.5.cloned.1.call-done, bf16[512,5120]{1,0:T(8,128)(2,1)} %all-reduce.3.cloned.1.call-done, bf16[512,5120]{1,0:T(8,128)(2,1)} %param.24, f32[5120]{0:T(1024)S(1)} %copy-done.4, f32[512]{0:T(512)S(1)} %add_rsqrt_fusion), kind=kOutput, calls=%fused_computation.11 | convolution fusion | flops 4548231168 | bytes 22009856 | tf_op jit(solution)/shard_map/dot_general | solution.py:133
  (43 shorter events, 7.9 us)
Async XLA Ops:
  8.0 97.8 %all-reduce.3.cloned.1.call-start = ((), (), s32[]{:S(2)}) async-start(), calls=%async_computation.1 | async-start | bytes 10485760 | tf_op jit(solution)/shard_map/psum | solution.py:128
  15.6 2.5 %copy-start.1 = (bf16[512,128]{1,0:T(8,128)(2,1)S(1)}, bf16[512,128]{1,0:T(8,128)(2,1)}, u32[]{:S(2)}) copy-start(bf16[512,128]{1,0:T(8,128)(2,1)} %param.16) | copy-start | bytes 393220
  15.6 2.5 %copy-start.3 = (f32[128]{0:T(128)S(1)}, f32[128]{0:T(128)}, u32[]{:S(2)}) copy-start(f32[128]{0:T(128)} %param.19) | copy-start | bytes 1540
  18.1 2.1 %copy-start = (bf16[384,5120]{1,0:T(8,128)(2,1)S(1)}, bf16[384,5120]{1,0:T(8,128)(2,1)}, u32[]{:S(2)}) copy-start(bf16[384,5120]{1,0:T(8,128)(2,1)} %param.23) | copy-start | bytes 11796484
  25.0 24.4 %copy-start.2 = (s32[16,4]{0,1:T(4,128)S(1)}, s32[16,4]{0,1:T(4,128)}, u32[]{:S(2)}) copy-start(s32[16,4]{0,1:T(4,128)} %param.22) | copy-start | bytes 772
  25.0 89.3 %all-gather.3.cloned.1.call-start = ((), (), s32[]{:S(2)}) async-start(), calls=%async_computation.2 | async-start | bytes 9748480 | tf_op jit(solution)/shard_map/all_gather | solution.py:60
  25.6 164.8 %all-gather.5.cloned.1.call-start = ((), (), s32[]{:S(2)}) async-start(), calls=%async_computation.3 | async-start | bytes 9748480 | tf_op jit(solution)/shard_map/all_gather | solution.py:61
  41.2 27.1 %all-to-all-start = ((bf16[16,128,1,256]{3,1,2,0:T(8,128)(2,1)}), bf16[16,128,1,256]{3,1,2,0:T(8,128)(2,1)S(1)}, u32[]{:S(2)}, u32[]{:S(2)}) async-start(bf16[16,128,1,256]{3,1,2,0:T(8,128)(2,1)} %copy.89), calls=%async_computation | async-start | bytes 2097152 | tf_op jit(solution)/shard_map/all_to_all | solution.py:119
  69.7 44.6 %copy-start.4 = (f32[5120]{0:T(1024)S(1)}, f32[5120]{0:T(1024)}, u32[]{:S(2)}) copy-start(f32[5120]{0:T(1024)} %param.25) | copy-start | bytes 61444
Sparse Core Ops, SparseCore 0:
  25.1 80.6 all-reduce.2
Sparse Core Ops, SparseCore 1:
  27.6 86.6 all-gather.2
  116.3 74.0 all-gather.4

commit v2 on v1

--- a/solution.py
+++ b/solution.py
@@ -4,10 +4,13 @@
 import jax.numpy as jnp
 from jax import lax
 from jax.sharding import PartitionSpec as P
+from jax.experimental import pallas as pl
+from jax.experimental.pallas import tpu as pltpu
 
 HD = 128
 PAGE = 128
 REQS = 4
+RING = 4
 
 
 THETA = 1000000.0
@@ -26,6 +29,112 @@
         [first_half * cosine - second * sine_part, second * cosine + first_half * sine_part],
         axis=-1,
     )
+
+
+def gather_kernel(wg_ref, wu_ref, after_ref, out_ref, send_sems, recv_sems, local_sems):
+    me = lax.axis_index("req")
+    col = lax.axis_index("mp")
+    z = me // RING
+    y = me % RING
+    yp = (y + 1) % RING
+    ym = (y + RING - 1) % RING
+    zp = (z + 1) % RING
+    zm = (z + RING - 1) % RING
+    rows = wg_ref.shape[0]
+    half = rows // 2
+    mesh_id = pl.DeviceIdType.MESH
+
+    def to(zz, yy):
+        return (zz * RING + yy, col)
+
+    barrier = pltpu.get_barrier_semaphore()
+    for peer in (to(z, yp), to(z, ym), to(zp, y), to(zm, y)):
+        pl.semaphore_signal(barrier, inc=1, device_id=peer, device_id_type=mesh_id)
+    pl.semaphore_wait(barrier, 4)
+
+    def remote(k, src, dst, peer):
+        return pltpu.make_async_remote_copy(
+            src_ref=src,
+            dst_ref=dst,
+            send_sem=send_sems.at[k],
+            recv_sem=recv_sems.at[k],
+            device_id=peer,
+            device_id_type=mesh_id,
+        )
+
+    own_g = pltpu.make_async_copy(wg_ref, out_ref.at[0, z, y], local_sems.at[0])
+    own_u = pltpu.make_async_copy(wu_ref, out_ref.at[1, z, y], local_sems.at[1])
+    own_g.start()
+    own_u.start()
+
+    step1 = [
+        remote(0, wg_ref, out_ref.at[0, z, y], to(z, yp)),
+        remote(1, wg_ref, out_ref.at[0, z, y], to(z, ym)),
+        remote(2, wu_ref, out_ref.at[1, z, y], to(zp, y)),
+        remote(3, wu_ref, out_ref.at[1, z, y], to(zm, y)),
+    ]
+    for c in step1:
+        c.start()
+    for c in step1:
+        c.wait_recv()
+
+    low = pl.ds(0, half)
+    high = pl.ds(half, rows - half)
+    step2 = [
+        remote(4, out_ref.at[0, z, ym, low], out_ref.at[0, z, ym, low], to(z, yp)),
+        remote(5, out_ref.at[0, z, yp, high], out_ref.at[0, z, yp, high], to(z, ym)),
+        remote(6, out_ref.at[1, zm, y, low], out_ref.at[1, zm, y, low], to(zp, y)),
+        remote(7, out_ref.at[1, zp, y, high], out_ref.at[1, zp, y, high], to(zm, y)),
+    ]
+    for c in step2:
+        c.start()
+    own_g.wait()
+    own_u.wait()
+    for c in step2:
+        c.wait_recv()
+
+    step3 = [
+        remote(8, out_ref.at[0, z], out_ref.at[0, z], to(zp, y)),
+        remote(9, out_ref.at[0, z], out_ref.at[0, z], to(zm, y)),
+        remote(10, out_ref.at[1, :, y], out_ref.at[1, :, y], to(z, yp)),
+        remote(11, out_ref.at[1, :, y], out_ref.at[1, :, y], to(z, ym)),
+    ]
+    for c in step3:
+        c.start()
+    for c in step3:
+        c.wait_recv()
+
+    first = pl.ds(0, RING // 2)
+    second = pl.ds(RING // 2, RING - RING // 2)
+    step4 = [
+        remote(12, out_ref.at[0, zm, first], out_ref.at[0, zm, first], to(zp, y)),
+        remote(13, out_ref.at[0, zp, second], out_ref.at[0, zp, second], to(zm, y)),
+        remote(14, out_ref.at[1, first, ym], out_ref.at[1, first, ym], to(z, yp)),
+        remote(15, out_ref.at[1, second, yp], out_ref.at[1, second, yp], to(z, ym)),
+    ]
+    for c in step4:
+        c.start()
+    for c in step4:
+        c.wait_recv()
+    for c in step1 + step2 + step3 + step4:
+        c.wait_send()
+
+
+def gather_weights(w_gate, w_up, after):
+    rows, cols = w_gate.shape
+    any_spec = pl.BlockSpec(memory_space=pl.ANY)
+    return pl.pallas_call(
+        gather_kernel,
+        out_shape=jax.ShapeDtypeStruct((2, RING, RING, rows, cols), w_gate.dtype),
+        in_specs=[any_spec, any_spec, any_spec],
+        out_specs=any_spec,
+        scratch_shapes=[
+            pltpu.SemaphoreType.DMA((16,)),
+            pltpu.SemaphoreType.DMA((16,)),
+            pltpu.SemaphoreType.DMA((2,)),
+        ],
+        compiler_params=pltpu.CompilerParams(collective_id=0, has_side_effects=True),
+    )(w_gate, w_up, after)
 
 
 def normalize(resid_rows, summed, gain_row):
@@ -57,8 +166,6 @@
     q_heads = q_pre.shape[1] // HD
     group_size = q_heads // kv_heads
 
-    wg_full = lax.all_gather(w_gate, "req", axis=0, tiled=True)
-    wu_full = lax.all_gather(w_up, "req", axis=0, tiled=True)
 
     own_lens = lax.dynamic_index_in_dim(lengths, me_req, 0, keepdims=False)
     own_pages = lax.dynamic_index_in_dim(page_table, me_req, 0, keepdims=False)
@@ -125,10 +232,12 @@
         "ls,sphc->lhpc", page_select, kv_in, preferred_element_type=jnp.float32
     ).astype(jnp.bfloat16)
 
-    summed = lax.psum(
-        jnp.dot(attended, w_out, preferred_element_type=jnp.float32).astype(jnp.bfloat16), "mp"
-    ).astype(jnp.float32)
+    product = jnp.dot(attended, w_out, preferred_element_type=jnp.float32).astype(jnp.bfloat16)
+    summed = lax.psum(product, "mp").astype(jnp.float32)
     normed = normalize(residual, summed, norm_gain)
+    gathered = gather_weights(w_gate, w_up, product[:8, :128])
+    wg_full = gathered[0].reshape(-1, w_gate.shape[1])
+    wu_full = gathered[1].reshape(-1, w_up.shape[1])
     gate_acc = jnp.dot(normed, wg_full, preferred_element_type=jnp.float32)
     up_acc = jnp.dot(normed, wu_full, preferred_element_type=jnp.float32)
     hidden = (jax.nn.silu(gate_acc) * up_acc).astype(jnp.bfloat16)

time: 212 us -> 219 us (1.033)
  waiting for transfers between devices: 123 us -> 0.71 us
  Pallas kernels: 0 us -> 116 us
  local copies, waits for them, and re-layouts: 6.03 us -> 21.9 us
    pallas_call x0 -> x1, Pallas kernels: none -> 116 us  [gather_weights(): pl.pallas_call(gather_kernel, out_shape=jax.ShapeDtypeStruct((2, RING, RI...]
    all_gather x2 -> x0, waiting for transfers between devices: 66.7 us -> none  [the longest x1 64 us: shards(): wu_full = lax.all_gather(w_up, 'req', axis=0, tiled=True)]
    psum x1, waiting for transfers between devices: 36.1 us -> 0.01 us  [shards(): summed = lax.psum(product, 'mp').astype(jnp.float32)]
    all_to_all x1, waiting for transfers between devices: 18.8 us -> 0.01 us  [shards(): lax.all_to_all(kv_send, 'req', split_axis=0, concat_axis=0, tiled=True)]
    slice x0 -> x2, local copies, waits for them, and re-layouts: none -> 15.9 us  [the longest x1 14.6 us: shards(): wu_full = gathered[1].reshape(-1, w_up.shape[1])]
  transfers between devices with their start and end apart: 4 -> 2, of which waited for: 4 -> 0; matrix products, arithmetic and copies ran while one was open for 13% -> 11% of each run, Pallas kernels for 0% -> 53%
where the time goes in v2:
time: 219 us
  Pallas kernels  116 us (53%)
  matrix products  32.9 us (15%)
  local copies, waits for them, and re-layouts  21.9 us (10%)
  between operations  21.9 us (10%)
  other arithmetic  17 us (8%)
  starting transfers between devices  8.13 us (4%)
    pallas_call x1, Pallas kernels, gather_weights(): pl.pallas_call(gather_kernel, out_shape=jax.ShapeDtypeStruct((2, RING, RI...  116 us
    slice x1, local copies, waits for them, and re-layouts, shards(): wu_full = gathered[1].reshape(-1, w_up.shape[1])  14.6 us
    dot_general x1, matrix products, shards(): up_acc = jnp.dot(normed, wu_full, preferred_element_type=jnp.float32)  13.2 us
    dot_general x1, matrix products, shards(): gate_acc = jnp.dot(normed, wg_full, preferred_element_type=jnp.float32)  11.5 us
    all_to_all x1, starting transfers between devices, shards(): lax.all_to_all(kv_send, 'req', split_axis=0, concat_axis=0, tiled=True)  8.13 us
    reduce_sum x1, other arithmetic, normalize(): scale_row = lax.rsqrt(jnp.mean(state * state, axis=-1, keepdims=True) + EPS)  5.96 us
    dot_general x1, matrix products, shards(): jnp.dot(attended, w_out, preferred_element_type=jnp.float32)  4.64 us
  transfers between devices with their start and end apart: 2, of which 0 were waited for; matrix products, arithmetic and copies ran while one was open for 11% of the time, Pallas kernels for 53%

profile of v2, /device:TPU:0, one launch (start us, length us, event | category | flops | bytes accessed | tf_op | source)
XLA Modules:
  0.0 218.8 jit_solution(6179367688944255956)
XLA Ops:
  7.2 0.7 broadcast_compare_fusion
  8.6 0.9 fusion.45
  9.8 1.0 fusion.15
  10.8 0.9 add_bitcast_fusion
  12.3 1.2 fusion.28
  13.5 1.2 copy.81
  14.7 0.8 convert_add_fusion.1
  15.7 0.8 fusion
  16.5 0.7 fusion.3
  17.3 1.2 fusion.9
  18.5 0.9 copy-done.1
  19.4 4.6 %convolution_convert_fusion = bf16[512,5120]{1,0:T(8,128)(2,1)} fusion(bf16[512,384]{0,1:T(8,128)(2,1)S(1)} %bitcast.101, bf16[384,5120]{1,0:T(8,128)(2,1)S(1)} %copy-done.1), kind=kOutput, calls=%fused_computation.3 | convolution fusion | flops 2015887360 | bytes 9568256 | tf_op jit(solution)/shard_map/dot_general | solution.py:235
  24.0 1.3 slice.68.after_ref
  25.3 0.7 all-reduce.3.cloned.1.call-update
  36.7 0.7 iota_compare_fusion.6
  38.4 0.9 fusion.8
  39.4 1.4 copy.89
  40.7 8.1 %all-to-all-start = ((bf16[16,128,1,256]{3,1,2,0:T(8,128)(2,1)}), bf16[16,128,1,256]{3,1,2,0:T(8,128)(2,1)S(1)}, u32[]{:S(2)}, u32[]{:S(2)}) async-start(bf16[16,128,1,256]{3,1,2,0:T(8,128)(2,1)} %copy.89), calls=%async_computation | async-start | bytes 2097152 | tf_op jit(solution)/shard_map/all_to_all | solution.py:226
  48.9 116.3 %shard_map.149 = bf16[2,4,4,320,864]{4,3,2,1,0:T(8,128)(2,1)} custom-call(bf16[320,864]{1,0:T(8,128)(2,1)} %wg_ref.1, bf16[320,864]{1,0:T(8,128)(2,1)} %wu_ref.1, bf16[8,128]{1,0:T(8,128)(2,1)} %slice.68.after_ref), custom_call_target="tpu_custom_call" | custom-call | tf_op jit(solution)/shard_map/pallas_call | solution.py:126
  165.3 14.6 %fusion.59 = (bf16[1,4,4,320,864]{4,3,2,1,0:T(8,128)(2,1)}, bf16[1,4,4,320,864]{4,3,2,1,0:T(8,128)(2,1)}) fusion(bf16[2,4,4,320,864]{4,3,2,1,0:T(8,128)(2,1)} %shard_map.149), kind=kLoop, calls=%fused_computation.106 | loop fusion | bytes 35389440 | tf_op jit(solution)/shard_map/slice | solution.py:240
  180.6 0.7 copy.91
  181.4 6.0 %multiply_reduce_fusion = f32[512]{0:T(512)S(1)} fusion(bf16[512,5120]{1,0:T(8,128)(2,1)} %all-reduce.3.cloned.1.call-done, bf16[512,5120]{1,0:T(8,128)(2,1)} %param.24), kind=kLoop, calls=%fused_computation.1 | loop fusion | flops 13106688 | bytes 10487808 | tf_op jit(solution)/shard_map/reduce_sum | solution.py:142
  187.3 11.5 %fusion.58 = f32[512,864]{0,1:T(8,128)} fusion(bf16[5120,864]{1,0:T(8,128)(2,1)} %bitcast.97, bf16[512,5120]{1,0:T(8,128)(2,1)S(1)} %copy-done, bf16[512,5120]{1,0:T(8,128)(2,1)} %param.24, f32[5120]{0:T(1024)S(1)} %copy-done.5, f32[512]{0:T(512)S(1)} %add_rsqrt_fusion), kind=kOutput, calls=%fused_computation.105 | convolution fusion | flops 4545576960 | bytes 21125120 | tf_op jit(solution)/shard_map/dot_general | solution.py:241
  198.8 13.2 %multiply_convert_fusion.1 = bf16[512,864]{0,1:T(8,128)(2,1)} fusion(f32[512,864]{0,1:T(8,128)} %fusion.58, bf16[5120,864]{1,0:T(8,128)(2,1)} %bitcast.96, bf16[512,5120]{1,0:T(8,128)(2,1)} %all-reduce.3.cloned.1.call-done, bf16[512,5120]{1,0:T(8,128)(2,1)} %param.24, f32[5120]{0:T(1024)S(1)} %copy-done.5, f32[512]{0:T(512)S(1)} %add_rsqrt_fusion), kind=kOutput, calls=%fused_computation.11 | convolution fusion | flops 4548231168 | bytes 22009856 | tf_op jit(solution)/shard_map/dot_general | solution.py:242
  (42 shorter events, 6.6 us)
Async XLA Ops:
  14.7 2.5 %copy-start.2 = (bf16[512,128]{1,0:T(8,128)(2,1)S(1)}, bf16[512,128]{1,0:T(8,128)(2,1)}, u32[]{:S(2)}) copy-start(bf16[512,128]{1,0:T(8,128)(2,1)} %param.16) | copy-start | bytes 393220
  14.7 2.5 %copy-start.4 = (f32[128]{0:T(128)S(1)}, f32[128]{0:T(128)}, u32[]{:S(2)}) copy-start(f32[128]{0:T(128)} %param.19) | copy-start | bytes 1540
  17.2 2.1 copy-start.1
  25.3 156.1 %all-reduce.3.cloned.1.call-start = ((), (), s32[]{:S(2)}) async-start(), calls=%async_computation.1 | async-start | bytes 10485760 | tf_op jit(solution)/shard_map/psum | solution.py:236
  40.7 139.2 %all-to-all-start = ((bf16[16,128,1,256]{3,1,2,0:T(8,128)(2,1)}), bf16[16,128,1,256]{3,1,2,0:T(8,128)(2,1)S(1)}, u32[]{:S(2)}, u32[]{:S(2)}) async-start(bf16[16,128,1,256]{3,1,2,0:T(8,128)(2,1)} %copy.89), calls=%async_computation | async-start | bytes 2097152 | tf_op jit(solution)/shard_map/all_to_all | solution.py:226
  48.9 116.3 %copy-start.3 = (s32[16,4]{0,1:T(4,128)S(1)}, s32[16,4]{0,1:T(4,128)}, u32[]{:S(2)}) copy-start(s32[16,4]{0,1:T(4,128)} %param.22) | copy-start | bytes 772
  181.3 6.0 %copy-start.5 = (f32[5120]{0:T(1024)S(1)}, f32[5120]{0:T(1024)}, u32[]{:S(2)}) copy-start(f32[5120]{0:T(1024)} %param.25) | copy-start | bytes 61444
  181.3 6.0 %copy-start = (bf16[512,5120]{1,0:T(8,128)(2,1)S(1)}, bf16[512,5120]{1,0:T(8,128)(2,1)}, u32[]{:S(2)}) copy-start(bf16[512,5120]{1,0:T(8,128)(2,1)} %all-reduce.3.cloned.1.call-done) | copy-start | bytes 15728644
Sparse Core Ops, SparseCore 0:
  28.5 79.8 all-reduce.2

commit v3 on v1

--- a/solution.py
+++ b/solution.py
@@ -4,10 +4,13 @@
 import jax.numpy as jnp
 from jax import lax
 from jax.sharding import PartitionSpec as P
+from jax.experimental import pallas as pl
+from jax.experimental.pallas import tpu as pltpu
 
 HD = 128
 PAGE = 128
 REQS = 4
+RING = 4
 
 
 THETA = 1000000.0
@@ -27,6 +30,120 @@
         axis=-1,
     )
 
+
+def gather_kernel(wg_ref, wu_ref, after_ref, g_ref, u_ref, send_sems, recv_sems, local_sems):
+    me = lax.axis_index("req")
+    col = lax.axis_index("mp")
+    z = me // RING
+    y = me % RING
+    yp = (y + 1) % RING
+    ym = (y + RING - 1) % RING
+    y2 = (y + 2) % RING
+    zp = (z + 1) % RING
+    zm = (z + RING - 1) % RING
+    z2 = (z + 2) % RING
+    rows = wg_ref.shape[0]
+    low = pl.ds(0, rows // 2)
+    high = pl.ds(rows // 2, rows - rows // 2)
+    mesh_id = pl.DeviceIdType.MESH
+
+    def to(zz, yy):
+        return (zz * RING + yy, col)
+
+    barrier = pltpu.get_barrier_semaphore()
+    for peer in (to(z, yp), to(z, ym), to(zp, y), to(zm, y)):
+        pl.semaphore_signal(barrier, inc=1, device_id=peer, device_id_type=mesh_id)
+    pl.semaphore_wait(barrier, 4)
+
+    copies = []
+
+    def send(src, dst, peer):
+        k = len(copies)
+        c = pltpu.make_async_remote_copy(
+            src_ref=src,
+            dst_ref=dst,
+            send_sem=send_sems.at[k],
+            recv_sem=recv_sems.at[k],
+            device_id=peer,
+            device_id_type=mesh_id,
+        )
+        c.start()
+        copies.append(c)
+        return c
+
+    own_g = pltpu.make_async_copy(wg_ref, g_ref.at[z, y], local_sems.at[0])
+    own_u = pltpu.make_async_copy(wu_ref, u_ref.at[z, y], local_sems.at[1])
+    own_g.start()
+    own_u.start()
+
+    g_from_ym = send(wg_ref, g_ref.at[z, y], to(z, yp))
+    g_from_yp = send(wg_ref, g_ref.at[z, y], to(z, ym))
+    u_from_zm = send(wu_ref, u_ref.at[z, y], to(zp, y))
+    u_from_zp = send(wu_ref, u_ref.at[z, y], to(zm, y))
+    gz = {"y": (send(wg_ref, g_ref.at[z, y], to(zp, y)), send(wg_ref, g_ref.at[z, y], to(zm, y)))}
+    uy = {"z": (send(wu_ref, u_ref.at[z, y], to(z, yp)), send(wu_ref, u_ref.at[z, y], to(z, ym)))}
+
+    g_from_ym.wait_recv()
+    g_far_a = send(g_ref.at[z, ym, low], g_ref.at[z, ym, low], to(z, yp))
+    gz["ym"] = (send(g_ref.at[z, ym], g_ref.at[z, ym], to(zp, y)), send(g_ref.at[z, ym], g_ref.at[z, ym], to(zm, y)))
+    u_from_zm.wait_recv()
+    u_far_a = send(u_ref.at[zm, y, low], u_ref.at[zm, y, low], to(zp, y))
+    uy["zm"] = (send(u_ref.at[zm, y], u_ref.at[zm, y], to(z, yp)), send(u_ref.at[zm, y], u_ref.at[zm, y], to(z, ym)))
+    g_from_yp.wait_recv()
+    g_far_b = send(g_ref.at[z, yp, high], g_ref.at[z, yp, high], to(z, ym))
+    gz["yp"] = (send(g_ref.at[z, yp], g_ref.at[z, yp], to(zp, y)), send(g_ref.at[z, yp], g_ref.at[z, yp], to(zm, y)))
+    u_from_zp.wait_recv()
+    u_far_b = send(u_ref.at[zp, y, high], u_ref.at[zp, y, high], to(zm, y))
+    uy["zp"] = (send(u_ref.at[zp, y], u_ref.at[zp, y], to(z, yp)), send(u_ref.at[zp, y], u_ref.at[zp, y], to(z, ym)))
+
+    g_far_a.wait_recv()
+    g_far_b.wait_recv()
+    gz["y2"] = (send(g_ref.at[z, y2], g_ref.at[z, y2], to(zp, y)), send(g_ref.at[z, y2], g_ref.at[z, y2], to(zm, y)))
+    u_far_a.wait_recv()
+    u_far_b.wait_recv()
+    uy["z2"] = (send(u_ref.at[z2, y], u_ref.at[z2, y], to(z, yp)), send(u_ref.at[z2, y], u_ref.at[z2, y], to(z, ym)))
+
+    for key, yy in (("y", y), ("ym", ym), ("yp", yp), ("y2", y2)):
+        from_zm, from_zp = gz[key]
+        from_zm.wait_recv()
+        send(g_ref.at[zm, yy, low], g_ref.at[zm, yy, low], to(zp, y))
+        from_zp.wait_recv()
+        send(g_ref.at[zp, yy, high], g_ref.at[zp, yy, high], to(zm, y))
+    for key, zz in (("z", z), ("zm", zm), ("zp", zp), ("z2", z2)):
+        from_ym, from_yp = uy[key]
+        from_ym.wait_recv()
+        send(u_ref.at[zz, ym, low], u_ref.at[zz, ym, low], to(z, yp))
+        from_yp.wait_recv()
+        send(u_ref.at[zz, yp, high], u_ref.at[zz, yp, high], to(z, ym))
+
+    waited = [g_from_ym, g_from_yp, u_from_zm, u_from_zp, g_far_a, g_far_b, u_far_a, u_far_b]
+    waited += list(gz["y"]) + list(gz["ym"]) + list(gz["yp"]) + list(gz["y2"])
+    waited += list(uy["z"]) + list(uy["zm"]) + list(uy["zp"]) + list(uy["z2"])
+    for c in copies:
+        if not any(c is w for w in waited):
+            c.wait_recv()
+    for c in copies:
+        c.wait_send()
+    own_g.wait()
+    own_u.wait()
+
+
+def gather_weights(w_gate, w_up, after):
+    rows, cols = w_gate.shape
+    any_spec = pl.BlockSpec(memory_space=pl.ANY)
+    piece = jax.ShapeDtypeStruct((RING, RING, rows, cols), w_gate.dtype)
+    return pl.pallas_call(
+        gather_kernel,
+        out_shape=(piece, piece),
+        in_specs=[any_spec, any_spec, any_spec],
+        out_specs=(any_spec, any_spec),
+        scratch_shapes=[
+            pltpu.SemaphoreType.DMA((40,)),
+            pltpu.SemaphoreType.DMA((40,)),
+            pltpu.SemaphoreType.DMA((2,)),
+        ],
+        compiler_params=pltpu.CompilerParams(collective_id=0, has_side_effects=True),
+    )(w_gate, w_up, after)
 
 def normalize(resid_rows, summed, gain_row):
     state = resid_rows.astype(jnp.float32) + summed
@@ -57,8 +174,6 @@
     q_heads = q_pre.shape[1] // HD
     group_size = q_heads // kv_heads
 
-    wg_full = lax.all_gather(w_gate, "req", axis=0, tiled=True)
-    wu_full = lax.all_gather(w_up, "req", axis=0, tiled=True)
 
     own_lens = lax.dynamic_index_in_dim(lengths, me_req, 0, keepdims=False)
     own_pages = lax.dynamic_index_in_dim(page_table, me_req, 0, keepdims=False)
@@ -125,10 +240,12 @@
         "ls,sphc->lhpc", page_select, kv_in, preferred_element_type=jnp.float32
     ).astype(jnp.bfloat16)
 
-    summed = lax.psum(
-        jnp.dot(attended, w_out, preferred_element_type=jnp.float32).astype(jnp.bfloat16), "mp"
-    ).astype(jnp.float32)
+    product = jnp.dot(attended, w_out, preferred_element_type=jnp.float32).astype(jnp.bfloat16)
+    summed = lax.psum(product, "mp").astype(jnp.float32)
     normed = normalize(residual, summed, norm_gain)
+    g_full, u_full = gather_weights(w_gate, w_up, product[:8, :128])
+    wg_full = g_full.reshape(-1, w_gate.shape[1])
+    wu_full = u_full.reshape(-1, w_up.shape[1])
     gate_acc = jnp.dot(normed, wg_full, preferred_element_type=jnp.float32)
     up_acc = jnp.dot(normed, wu_full, preferred_element_type=jnp.float32)
     hidden = (jax.nn.silu(gate_acc) * up_acc).astype(jnp.bfloat16)

time: 212 us -> 199 us (0.939)
  waiting for transfers between devices: 123 us -> 0.71 us
  Pallas kernels: 0 us -> 111 us
    pallas_call x0 -> x1, Pallas kernels: none -> 111 us  [gather_weights(): pl.pallas_call(gather_kernel, out_shape=(piece, piece), in_specs=[any_spe...]
    all_gather x2 -> x0, waiting for transfers between devices: 66.7 us -> none  [the longest x1 64 us: shards(): wu_full = lax.all_gather(w_up, 'req', axis=0, tiled=True)]
    psum x1, waiting for transfers between devices: 36.1 us -> 0.01 us  [shards(): summed = lax.psum(product, 'mp').astype(jnp.float32)]
    all_to_all x1, waiting for transfers between devices: 18.8 us -> 0.01 us  [shards(): lax.all_to_all(kv_send, 'req', split_axis=0, concat_axis=0, tiled=True)]
  transfers between devices with their start and end apart: 4 -> 2, of which waited for: 4 -> 0; matrix products, arithmetic and copies ran while one was open for 13% -> 4% of each run, Pallas kernels for 0% -> 56%
where the time goes in v3:
time: 199 us; the launch traced here: 198 us
  Pallas kernels  111 us (56%)
  matrix products  32.7 us (16%)
  between operations  21.6 us (11%)
  other arithmetic  17 us (9%)
  starting transfers between devices  8.31 us (4%)
  local copies, waits for them, and re-layouts  7.21 us (4%)
    pallas_call x1, Pallas kernels, gather_weights(): pl.pallas_call(gather_kernel, out_shape=(piece, piece), in_specs=[any_spe...  111 us
    dot_general x1, matrix products, shards(): up_acc = jnp.dot(normed, wu_full, preferred_element_type=jnp.float32)  13.2 us
    dot_general x1, matrix products, shards(): gate_acc = jnp.dot(normed, wg_full, preferred_element_type=jnp.float32)  11.3 us
    all_to_all x1, starting transfers between devices, shards(): lax.all_to_all(kv_send, 'req', split_axis=0, concat_axis=0, tiled=True)  8.31 us
    reduce_sum x1, other arithmetic, normalize(): scale_row = lax.rsqrt(jnp.mean(state * state, axis=-1, keepdims=True) + EPS)  5.96 us
    dot_general x1, matrix products, shards(): jnp.dot(attended, w_out, preferred_element_type=jnp.float32)  4.65 us
  transfers between devices with their start and end apart: 2, of which 0 were waited for; matrix products, arithmetic and copies ran while one was open for 4% of the time, Pallas kernels for 56%

profile of v3, /device:TPU:0, one launch (start us, length us, event | category | flops | bytes accessed | tf_op | source)
XLA Modules:
  0.0 198.3 jit_solution(712361649398720540)
XLA Ops:
  7.2 0.7 broadcast_compare_fusion
  7.9 0.7 subtract_clamp_fusion
  8.6 0.9 fusion.45
  9.8 1.0 fusion.15
  10.8 0.9 add_bitcast_fusion
  12.3 1.2 fusion.28
  13.5 1.2 copy.81
  14.7 0.8 convert_add_fusion.1
  15.7 0.8 fusion
  16.5 0.7 fusion.3
  17.3 1.2 fusion.9
  18.4 0.9 copy-done.1
  19.4 4.6 %convolution_convert_fusion = bf16[512,5120]{1,0:T(8,128)(2,1)} fusion(bf16[512,384]{0,1:T(8,128)(2,1)S(1)} %bitcast.99, bf16[384,5120]{1,0:T(8,128)(2,1)S(1)} %copy-done.1), kind=kOutput, calls=%fused_computation.3 | convolution fusion | flops 2015887360 | bytes 9568256 | tf_op jit(solution)/shard_map/dot_general | solution.py:243
  24.0 1.3 slice.60.after_ref
  25.3 0.7 all-reduce.3.cloned.1.call-update
  34.6 0.7 iota_compare_fusion.7
  38.1 0.9 fusion.8
  39.0 1.3 copy.89
  40.4 8.3 %all-to-all-start = ((bf16[16,128,1,256]{3,1,2,0:T(8,128)(2,1)}), bf16[16,128,1,256]{3,1,2,0:T(8,128)(2,1)S(1)}, u32[]{:S(2)}, u32[]{:S(2)}) async-start(bf16[16,128,1,256]{3,1,2,0:T(8,128)(2,1)} %copy.89), calls=%async_computation | async-start | bytes 2097152 | tf_op jit(solution)/shard_map/all_to_all | solution.py:234
  48.7 110.7 %shard_map.149 = (bf16[4,4,320,864]{3,2,1,0:T(8,128)(2,1)}, bf16[4,4,320,864]{3,2,1,0:T(8,128)(2,1)}) custom-call(bf16[320,864]{1,0:T(8,128)(2,1)} %wg_ref.1, bf16[320,864]{1,0:T(8,128)(2,1)} %wu_ref.1, bf16[8,128]{1,0:T(8,128)(2,1)} %slice.60.after_ref), custom_call_target="tpu_custom_call" | custom-call | tf_op jit(solution)/shard_map/pallas_call | solution.py:135
  160.2 0.7 copy.91
  160.9 6.0 %multiply_reduce_fusion = f32[512]{0:T(512)S(1)} fusion(bf16[512,5120]{1,0:T(8,128)(2,1)} %all-reduce.3.cloned.1.call-done, bf16[512,5120]{1,0:T(8,128)(2,1)} %param.24), kind=kLoop, calls=%fused_computation.1 | loop fusion | flops 13106688 | bytes 10487808 | tf_op jit(solution)/shard_map/reduce_sum | solution.py:150
  166.9 11.3 %fusion.58 = f32[512,864]{0,1:T(8,128)} fusion(bf16[5120,864]{1,0:T(8,128)(2,1)} %bitcast.102, bf16[512,5120]{1,0:T(8,128)(2,1)S(1)} %copy-done, bf16[512,5120]{1,0:T(8,128)(2,1)} %param.24, f32[5120]{0:T(1024)S(1)} %copy-done.5, f32[512]{0:T(512)S(1)} %add_rsqrt_fusion), kind=kOutput, calls=%fused_computation.105 | convolution fusion | flops 4545576960 | bytes 21125120 | tf_op jit(solution)/shard_map/dot_general | solution.py:249
  178.2 13.2 %multiply_convert_fusion.1 = bf16[512,864]{0,1:T(8,128)(2,1)} fusion(f32[512,864]{0,1:T(8,128)} %fusion.58, bf16[5120,864]{1,0:T(8,128)(2,1)} %bitcast.101, bf16[512,5120]{1,0:T(8,128)(2,1)} %all-reduce.3.cloned.1.call-done, bf16[512,5120]{1,0:T(8,128)(2,1)} %param.24, f32[5120]{0:T(1024)S(1)} %copy-done.5, f32[512]{0:T(512)S(1)} %add_rsqrt_fusion), kind=kOutput, calls=%fused_computation.11 | convolution fusion | flops 4548231168 | bytes 22009856 | tf_op jit(solution)/shard_map/dot_general | solution.py:250
  (41 shorter events, 5.9 us)
Async XLA Ops:
  14.7 2.5 %copy-start.2 = (bf16[512,128]{1,0:T(8,128)(2,1)S(1)}, bf16[512,128]{1,0:T(8,128)(2,1)}, u32[]{:S(2)}) copy-start(bf16[512,128]{1,0:T(8,128)(2,1)} %param.16) | copy-start | bytes 393220
  14.7 2.5 %copy-start.4 = (f32[128]{0:T(128)S(1)}, f32[128]{0:T(128)}, u32[]{:S(2)}) copy-start(f32[128]{0:T(128)} %param.19) | copy-start | bytes 1540
  17.2 2.1 %copy-start.1 = (bf16[384,5120]{1,0:T(8,128)(2,1)S(1)}, bf16[384,5120]{1,0:T(8,128)(2,1)}, u32[]{:S(2)}) copy-start(bf16[384,5120]{1,0:T(8,128)(2,1)} %param.23) | copy-start | bytes 11796484
  25.3 135.7 %all-reduce.3.cloned.1.call-start = ((), (), s32[]{:S(2)}) async-start(), calls=%async_computation.1 | async-start | bytes 10485760 | tf_op jit(solution)/shard_map/psum | solution.py:244
  26.0 133.4 %copy-start.3 = (s32[16,4]{0,1:T(4,128)S(1)}, s32[16,4]{0,1:T(4,128)}, u32[]{:S(2)}) copy-start(s32[16,4]{0,1:T(4,128)} %param.22) | copy-start | bytes 772
  40.4 119.1 %all-to-all-start = ((bf16[16,128,1,256]{3,1,2,0:T(8,128)(2,1)}), bf16[16,128,1,256]{3,1,2,0:T(8,128)(2,1)S(1)}, u32[]{:S(2)}, u32[]{:S(2)}) async-start(bf16[16,128,1,256]{3,1,2,0:T(8,128)(2,1)} %copy.89), calls=%async_computation | async-start | bytes 2097152 | tf_op jit(solution)/shard_map/all_to_all | solution.py:234
  160.9 6.0 %copy-start.5 = (f32[5120]{0:T(1024)S(1)}, f32[5120]{0:T(1024)}, u32[]{:S(2)}) copy-start(f32[5120]{0:T(1024)} %param.25) | copy-start | bytes 61444
  160.9 6.0 %copy-start = (bf16[512,5120]{1,0:T(8,128)(2,1)S(1)}, bf16[512,5120]{1,0:T(8,128)(2,1)}, u32[]{:S(2)}) copy-start(bf16[512,5120]{1,0:T(8,128)(2,1)} %all-reduce.3.cloned.1.call-done) | copy-start | bytes 15728644
Sparse Core Ops, SparseCore 0:
  28.4 80.0 all-reduce.2

commit v4 on v3

--- a/solution.py
+++ b/solution.py
@@ -243,10 +243,20 @@
     product = jnp.dot(attended, w_out, preferred_element_type=jnp.float32).astype(jnp.bfloat16)
     summed = lax.psum(product, "mp").astype(jnp.float32)
     normed = normalize(residual, summed, norm_gain)
-    g_full, u_full = gather_weights(w_gate, w_up, product[:8, :128])
-    wg_full = g_full.reshape(-1, w_gate.shape[1])
-    wu_full = u_full.reshape(-1, w_up.shape[1])
-    gate_acc = jnp.dot(normed, wg_full, preferred_element_type=jnp.float32)
+    half = w_gate.shape[0] // 2
+    g_low, g_high = gather_weights(w_gate[:half], w_gate[half:], product[:8, :128])
+    wu_full = lax.all_gather(w_up, "req", axis=0, tiled=True)
+    cols = g_low.shape[-1]
+    split = normed.reshape(block_rows, -1, 2, half)
+    gate_acc = jnp.dot(
+        split[:, :, 0].reshape(block_rows, -1),
+        g_low.reshape(-1, cols),
+        preferred_element_type=jnp.float32,
+    ) + jnp.dot(
+        split[:, :, 1].reshape(block_rows, -1),
+        g_high.reshape(-1, cols),
+        preferred_element_type=jnp.float32,
+    )
     up_acc = jnp.dot(normed, wu_full, preferred_element_type=jnp.float32)
     hidden = (jax.nn.silu(gate_acc) * up_acc).astype(jnp.bfloat16)
     return (hidden, cache_out)

time: 199 us -> 204 us (1.025)
  local copies, waits for them, and re-layouts: 7.21 us -> 19.1 us
  Pallas kernels: 111 us -> 99.9 us
  other arithmetic: 17 us -> 24.5 us
  matrix products: 32.7 us -> 26.7 us
    pallas_call x1, Pallas kernels: 111 us -> 99.9 us  [gather_weights(): pl.pallas_call(gather_kernel, out_shape=(piece, piece), in_specs=[any_spe...]
    convert_element_type x0 -> x1, local copies, waits for them, and re-layouts: none -> 7.93 us  [normalize(): return (state * scale_row * gain_row).astype(jnp.bfloat16)]
    convert_element_type x0 -> x1, other arithmetic: none -> 7.5 us  [normalize(): return (state * scale_row * gain_row).astype(jnp.bfloat16)]
    dot_general x1 -> x2, matrix products: 11.3 us -> 7.35 us  [the longest x1 4.85 us: shards(): jnp.dot(split[:, :, 1].reshape(block_rows, -1), g_high.reshape(-1, cols),...]
    slice x1 -> x3, local copies, waits for them, and re-layouts: 1.25 us -> 5.16 us  [the longest x1 3.04 us: shards(): split[:, :, 1].reshape(block_rows, -1)]
    dot_general x1, matrix products: 13.2 us -> 11.1 us  [shards(): up_acc = jnp.dot(normed, wu_full, preferred_element_type=jnp.float32)]
  transfers between devices with their start and end apart: 2 -> 3, of which waited for: 0 -> 0; matrix products, arithmetic and copies ran while one was open for 4% -> 20% of each run, Pallas kernels for 56% -> 49%
where the time goes in v4:
time: 204 us; the launch traced here: 203 us
  Pallas kernels  99.9 us (49%)
  matrix products  26.7 us (13%)
  other arithmetic  24.5 us (12%)
  between operations  23.6 us (12%)
  local copies, waits for them, and re-layouts  19.1 us (9%)
  starting transfers between devices  8.19 us (4%)
    pallas_call x1, Pallas kernels, gather_weights(): pl.pallas_call(gather_kernel, out_shape=(piece, piece), in_specs=[any_spe...  99.9 us
    dot_general x1, matrix products, shards(): up_acc = jnp.dot(normed, wu_full, preferred_element_type=jnp.float32)  11.1 us
    all_to_all x1, starting transfers between devices, shards(): lax.all_to_all(kv_send, 'req', split_axis=0, concat_axis=0, tiled=True)  8.15 us
    convert_element_type x1, local copies, waits for them, and re-layouts, normalize(): return (state * scale_row * gain_row).astype(jnp.bfloat16)  7.93 us
    convert_element_type x1, other arithmetic, normalize(): return (state * scale_row * gain_row).astype(jnp.bfloat16)  7.5 us
    reduce_sum x1, other arithmetic, normalize(): scale_row = lax.rsqrt(jnp.mean(state * state, axis=-1, keepdims=True) + EPS)  5.96 us
    dot_general x1, matrix products, shards(): jnp.dot(split[:, :, 1].reshape(block_rows, -1), g_high.reshape(-1, cols),...  4.85 us
    dot_general x1, matrix products, shards(): jnp.dot(attended, w_out, preferred_element_type=jnp.float32)  4.65 us
  transfers between devices with their start and end apart: 3, of which 0 were waited for; matrix products, arithmetic and copies ran while one was open for 20% of the time, Pallas kernels for 49%

profile of v4, /device:TPU:0, one launch (start us, length us, event | category | flops | bytes accessed | tf_op | source)
XLA Modules:
  0.0 203.3 jit_solution(6679389569929403155)
XLA Ops:
  8.0 0.9 fusion.45
  10.7 1.2 copy.86
  12.4 0.9 add_bitcast_fusion
  13.3 1.2 fusion.28
  14.5 1.0 fusion.15
  15.5 0.8 convert_add_fusion.1
  16.5 0.8 fusion
  18.0 1.2 fusion.9
  19.2 0.9 copy-done.1
  20.1 4.6 %convolution_convert_fusion = bf16[512,5120]{1,0:T(8,128)(2,1)} fusion(bf16[512,384]{0,1:T(8,128)(2,1)S(1)} %bitcast.109, bf16[384,5120]{1,0:T(8,128)(2,1)S(1)} %copy-done.1), kind=kOutput, calls=%fused_computation.3 | convolution fusion | flops 2015887360 | bytes 9568256 | tf_op jit(solution)/shard_map/dot_general | solution.py:243
  24.8 1.3 slice.77.after_ref
  40.0 0.9 fusion.8
  41.0 1.4 copy.95
  42.4 8.1 %all-to-all-start = ((bf16[16,128,1,256]{3,1,2,0:T(8,128)(2,1)}), bf16[16,128,1,256]{3,1,2,0:T(8,128)(2,1)S(1)}, u32[]{:S(2)}, u32[]{:S(2)}) async-start(bf16[16,128,1,256]{3,1,2,0:T(8,128)(2,1)} %copy.95), calls=%async_computation | async-start | bytes 2097152 | tf_op jit(solution)/shard_map/all_to_all | solution.py:234
  50.5 0.9 fusion.59
  51.4 99.9 %shard_map.149 = (bf16[4,4,160,864]{3,2,1,0:T(8,128)(2,1)}, bf16[4,4,160,864]{3,2,1,0:T(8,128)(2,1)}) custom-call(bf16[160,864]{1,0:T(8,128)(2,1)} %get-tuple-element.25.wg_ref, bf16[160,864]{1,0:T(8,128)(2,1)} %get-tuple-element.24.wu_ref, bf16[8,128]{1,0:T(8,128)(2,1)} %slice.77.after_ref), custom_call_target="tpu_custom_call" | custom-call | tf_op jit(solution)/shard_map/pallas_call | solution.py:135
  152.1 0.7 copy.97
  152.9 6.0 %multiply_reduce_fusion = f32[512]{0:T(512)S(1)} fusion(bf16[512,5120]{1,0:T(8,128)(2,1)} %all-reduce.3.cloned.1.call-done, bf16[512,5120]{1,0:T(8,128)(2,1)} %param.24), kind=kLoop, calls=%fused_computation.1 | loop fusion | flops 13106688 | bytes 10487808 | tf_op jit(solution)/shard_map/reduce_sum | solution.py:150
  158.9 7.5 %multiply_convert_fusion = bf16[512,5120]{1,0:T(8,128)(2,1)} fusion(bf16[512,5120]{1,0:T(8,128)(2,1)S(1)} %copy-done, bf16[512,5120]{1,0:T(8,128)(2,1)} %param.24, f32[5120]{0:T(1024)S(1)} %copy-done.4, f32[512]{0:T(512)S(1)} %add_rsqrt_fusion), kind=kLoop, calls=%fused_computation | loop fusion | flops 15728640 | bytes 15751168 | tf_op jit(solution)/shard_map/convert_element_type | solution.py:151
  166.3 7.9 %copy.90 = bf16[512,5120]{0,1:T(8,128)(2,1)} copy(bf16[512,5120]{1,0:T(8,128)(2,1)} %multiply_convert_fusion) | data formatting | bytes 10485760 | tf_op jit(solution)/shard_map/convert_element_type | solution.py:151
  174.3 3.0 %fusion.58 = (bf16[512,16,1,160]{0,3,2,1:T(8,128)(2,1)S(1)}, bf16[512,16,1,160]{0,3,2,1:T(8,128)(2,1)S(1)}) fusion(bf16[512,16,2,160]{0,3,2,1:T(8,128)(2,1)} %bitcast.103), kind=kLoop, calls=%fused_computation.105 | loop fusion | bytes 10485760 | tf_op jit(solution)/shard_map/slice | solution.py:256
  177.3 4.9 %fusion.63 = f32[512,864]{0,1:T(8,128)S(1)} fusion(bf16[512,2560]{0,1:T(8,128)(2,1)S(1)} %bitcast.106, bf16[2560,864]{1,0:T(8,128)(2,1)} %bitcast.114), kind=kOutput, calls=%fused_computation.110 | convolution fusion | flops 2264924160 | bytes 8814592 | tf_op jit(solution)/shard_map/dot_general | solution.py:255
  182.2 2.5 %fusion.62 = f32[512,864]{0,1:T(8,128)S(1)} fusion(bf16[512,2560]{0,1:T(8,128)(2,1)S(1)} %bitcast.105, bf16[2560,864]{1,0:T(8,128)(2,1)S(1)} %bitcast.113), kind=kOutput, calls=%fused_computation.109 | convolution fusion | flops 2264924160 | bytes 8814592 | tf_op jit(solution)/shard_map/dot_general | solution.py:251
  184.8 11.1 %multiply_convert_fusion.1 = bf16[512,864]{0,1:T(8,128)(2,1)} fusion(f32[512,864]{0,1:T(8,128)S(1)} %fusion.62, f32[512,864]{0,1:T(8,128)S(1)} %fusion.63, bf16[512,5120]{1,0:T(8,128)(2,1)} %multiply_convert_fusion, bf16[5120,864]{1,0:T(8,128)(2,1)} %all-gather.2.cloned.1.call-done), kind=kOutput, calls=%fused_computation.11 | convolution fusion | flops 4532944896 | bytes 18513920 | tf_op jit(solution)/shard_map/dot_general | solution.py:260
  (56 shorter events, 10.1 us)
Async XLA Ops:
  16.5 1.5 copy-start.3
  16.5 1.5 copy-start.6
  18.0 2.1 %copy-start.1 = (bf16[384,5120]{1,0:T(8,128)(2,1)S(1)}, bf16[384,5120]{1,0:T(8,128)(2,1)}, u32[]{:S(2)}) copy-start(bf16[384,5120]{1,0:T(8,128)(2,1)} %param.23) | copy-start | bytes 11796484
  26.0 126.8 %all-reduce.3.cloned.1.call-start = ((), (), s32[]{:S(2)}) async-start(), calls=%async_computation.1 | async-start | bytes 10485760 | tf_op jit(solution)/shard_map/psum | solution.py:244
  26.8 158.0 %all-gather.2.cloned.1.call-start = ((), (), s32[]{:S(2)}) async-start(), calls=%async_computation.2 | async-start | bytes 9748480 | tf_op jit(solution)/shard_map/all_gather | solution.py:248
  39.8 10.7 %copy-start.2 = (bf16[320,864]{1,0:T(8,128)(2,1)S(1)}, bf16[320,864]{1,0:T(8,128)(2,1)}, u32[]{:S(2)}) copy-start(bf16[320,864]{1,0:T(8,128)(2,1)} %param.26) | copy-start | bytes 1658884
  41.0 110.4 %copy-start.5 = (s32[16,4]{0,1:T(4,128)S(1)}, s32[16,4]{0,1:T(4,128)}, u32[]{:S(2)}) copy-start(s32[16,4]{0,1:T(4,128)} %param.22) | copy-start | bytes 772
  42.4 109.1 %all-to-all-start = ((bf16[16,128,1,256]{3,1,2,0:T(8,128)(2,1)}), bf16[16,128,1,256]{3,1,2,0:T(8,128)(2,1)S(1)}, u32[]{:S(2)}, u32[]{:S(2)}) async-start(bf16[16,128,1,256]{3,1,2,0:T(8,128)(2,1)} %copy.95), calls=%async_computation | async-start | bytes 2097152 | tf_op jit(solution)/shard_map/all_to_all | solution.py:234
  152.9 6.0 %copy-start.4 = (f32[5120]{0:T(1024)S(1)}, f32[5120]{0:T(1024)}, u32[]{:S(2)}) copy-start(f32[5120]{0:T(1024)} %param.25) | copy-start | bytes 61444
  152.9 6.0 %copy-start = (bf16[512,5120]{1,0:T(8,128)(2,1)S(1)}, bf16[512,5120]{1,0:T(8,128)(2,1)}, u32[]{:S(2)}) copy-start(bf16[512,5120]{1,0:T(8,128)(2,1)} %all-reduce.3.cloned.1.call-done) | copy-start | bytes 15728644
  174.3 7.9 %slice-start = ((s8[4587520]{0:T(1024)(128)(4,1)}), s8[4194304]{0:T(1024)(128)(4,1)S(1)}, s32[]{:S(2)}) async-start(s8[4587520]{0:T(1024)(128)(4,1)} %bitcast.111), calls=%async_computation.3 | async-start | bytes 8388608
  177.3 4.9 %slice-start.1 = ((s8[4587520]{0:T(1024)(128)(4,1)}), s8[393216]{0:T(1024)(128)(4,1)S(1)}, s32[]{:S(2)}) async-start(s8[4587520]{0:T(1024)(128)(4,1)} %bitcast.111), calls=%async_computation.4 | async-start | bytes 786432
Sparse Core Ops, SparseCore 0:
  29.2 80.7 all-reduce.2
Sparse Core Ops, SparseCore 1:
  29.4 122.4 all-gather.1

commit v5 on v3

--- a/solution.py
+++ b/solution.py
@@ -218,19 +218,20 @@
     attended = jnp.einsum("hgqk,khe->qhge", probs, values, preferred_element_type=jnp.float32)
     attended = attended.astype(jnp.bfloat16).reshape(block_rows, q_heads * HD)
 
-    kv_rows = jnp.concatenate([keys, values], axis=-1)
-    kv_rows = jnp.pad(kv_rows, ((0, PAGE), (0, 0), (0, 0)))
+    kv_rows = jnp.concatenate([keys, values], axis=-1).reshape(block_rows, -1)
     slot = jnp.arange(PAGE, dtype=jnp.int32)
-    pages = []
-    for j in range(REQS):
-        page = lax.dynamic_slice_in_dim(kv_rows, starts[j], PAGE, axis=0)
-        page = jnp.where((slot < own_lens[j])[:, None, None], page, jnp.zeros((), jnp.bfloat16))
-        pages.append(page)
-    pages = jnp.stack(pages)
-    to_owner = (own_owner[None, :] == jnp.arange(groups_all)[:, None]).astype(jnp.bfloat16)
+    source = starts[:, None] + slot[None, :]
+    live_slot = slot[None, :] < own_lens[:, None]
+    owner_hit = own_owner[None, :] == jnp.arange(groups_all)[:, None]
+    picks = (
+        owner_hit[:, :, None, None]
+        & live_slot[None, :, :, None]
+        & (source[None, :, :, None] == token[None, None, None, :])
+    )
+    select = jnp.sum(picks.astype(jnp.int32), axis=1).astype(jnp.bfloat16)
     kv_send = jnp.einsum(
-        "gj,jphc->gphc", to_owner, pages, preferred_element_type=jnp.float32
-    ).astype(jnp.bfloat16)
+        "gst,tc->gsc", select, kv_rows, preferred_element_type=jnp.float32
+    ).astype(jnp.bfloat16).reshape(groups_all, PAGE, kv_heads, 2 * HD)
     kv_in = lax.all_to_all(kv_send, "req", split_axis=0, concat_axis=0, tiled=True)
     hits = (
         page_table[None, :, :] == (me_req * REQS + jnp.arange(REQS, dtype=jnp.int32))[:, None, None]

time: 199 us -> 189 us (0.950)
  between operations: 21.6 us -> 14.2 us
  local copies, waits for them, and re-layouts: 7.21 us -> 4.17 us
    lt x4 -> x1, other arithmetic: 2.53 us -> 0.07 us  [shards(): live_slot = slot[None, :] < own_lens[:, None]]
    reduce_sum x0 -> x1, other arithmetic: none -> 2.3 us  [shards(): select = jnp.sum(picks.astype(jnp.int32), axis=1).astype(jnp.bfloat16)]
  transfers between devices with their start and end apart: 2 -> 2, of which waited for: 0 -> 0; matrix products, arithmetic and copies ran while one was open for 4% -> 3% of each run, Pallas kernels for 56% -> 59%
where the time goes in v5:
time: 189 us
  Pallas kernels  111 us (59%)
  matrix products  33.7 us (18%)
  other arithmetic  17 us (9%)
  between operations  14.2 us (8%)
  starting transfers between devices  8.32 us (4%)
  local copies, waits for them, and re-layouts  4.17 us (2%)
    pallas_call x1, Pallas kernels, gather_weights(): pl.pallas_call(gather_kernel, out_shape=(piece, piece), in_specs=[any_spe...  111 us
    dot_general x1, matrix products, shards(): up_acc = jnp.dot(normed, wu_full, preferred_element_type=jnp.float32)  13.2 us
    dot_general x1, matrix products, shards(): gate_acc = jnp.dot(normed, wg_full, preferred_element_type=jnp.float32)  11.5 us
    all_to_all x1, starting transfers between devices, shards(): lax.all_to_all(kv_send, 'req', split_axis=0, concat_axis=0, tiled=True)  8.31 us
    reduce_sum x1, other arithmetic, normalize(): scale_row = lax.rsqrt(jnp.mean(state * state, axis=-1, keepdims=True) + EPS)  5.96 us
    dot_general x1, matrix products, shards(): jnp.dot(attended, w_out, preferred_element_type=jnp.float32)  4.65 us
  transfers between devices with their start and end apart: 2, of which 0 were waited for; matrix products, arithmetic and copies ran while one was open for 3% of the time, Pallas kernels for 59%

profile of v5, /device:TPU:0, one launch (start us, length us, event | category | flops | bytes accessed | tf_op | source)
XLA Modules:
  0.0 188.8 jit_solution(10892252656720831628)
XLA Ops:
  7.2 0.7 broadcast_compare_fusion
  7.9 0.7 subtract_clamp_fusion
  8.6 0.9 fusion.45
  9.8 1.0 fusion.22
  10.8 0.9 add_bitcast_fusion
  12.3 1.2 fusion.32
  13.5 1.2 copy.42
  14.7 0.8 convert_add_fusion.1
  15.7 0.8 fusion
  16.5 0.7 fusion.3
  17.2 1.2 fusion.16
  18.4 0.9 copy-done.1
  19.3 4.7 %convolution_convert_fusion = bf16[512,5120]{1,0:T(8,128)(2,1)} fusion(bf16[512,384]{0,1:T(8,128)(2,1)S(1)} %bitcast.83, bf16[384,5120]{1,0:T(8,128)(2,1)S(1)} %copy-done.1), kind=kOutput, calls=%fused_computation.4 | convolution fusion | flops 2015887360 | bytes 9568256 | tf_op jit(solution)/shard_map/dot_general | solution.py:244
  24.0 1.3 slice.24.after_ref
  25.2 0.7 all-reduce.2.cloned.1.call-update
  26.7 2.3 %convert_reduce_fusion = s32[16,128,512]{2,1,0:T(8,128)S(1)} fusion(pred[4,128,512]{2,1,0:T(8,128)(4,1)S(1)} %iota_compare_fusion, pred[16,4,128]{2,1,0:T(4,128)(4,1)S(1)} %broadcast_and_fusion), kind=kLoop, calls=%fused_computation | loop fusion | flops 11534336 | bytes 4464640 | tf_op jit(solution)/shard_map/reduce_sum | solution.py:231
  29.1 1.7 fusion.13
  30.8 8.3 %all-to-all-start = ((bf16[16,128,1,256]{3,1,2,0:T(8,128)(2,1)}), bf16[16,128,1,256]{3,1,2,0:T(8,128)(2,1)S(1)}, u32[]{:S(2)}, u32[]{:S(2)}) async-start(bf16[16,128,1,256]{3,1,2,0:T(8,128)(2,1)} %fusion.13), calls=%async_computation | async-start | bytes 2097152 | tf_op jit(solution)/shard_map/all_to_all | solution.py:235
  39.1 110.7 %shard_map.149 = (bf16[4,4,320,864]{3,2,1,0:T(8,128)(2,1)}, bf16[4,4,320,864]{3,2,1,0:T(8,128)(2,1)}) custom-call(bf16[320,864]{1,0:T(8,128)(2,1)} %wg_ref.1, bf16[320,864]{1,0:T(8,128)(2,1)} %wu_ref.1, bf16[8,128]{1,0:T(8,128)(2,1)} %slice.24.after_ref), custom_call_target="tpu_custom_call" | custom-call | tf_op jit(solution)/shard_map/pallas_call | solution.py:135
  149.9 0.7 fusion.19
  150.6 0.7 copy.48
  151.3 6.0 %multiply_reduce_fusion = f32[512]{0:T(512)S(1)} fusion(bf16[512,5120]{1,0:T(8,128)(2,1)} %all-reduce.2.cloned.1.call-done, bf16[512,5120]{1,0:T(8,128)(2,1)} %param.24), kind=kLoop, calls=%fused_computation.2 | loop fusion | flops 13106688 | bytes 10487808 | tf_op jit(solution)/shard_map/reduce_sum | solution.py:150
  157.3 11.5 %fusion.55 = f32[512,864]{0,1:T(8,128)} fusion(bf16[5120,864]{1,0:T(8,128)(2,1)} %bitcast.87, bf16[512,5120]{1,0:T(8,128)(2,1)S(1)} %copy-done, bf16[512,5120]{1,0:T(8,128)(2,1)} %param.24, f32[5120]{0:T(1024)S(1)} %copy-done.5, f32[512]{0:T(512)S(1)} %add_rsqrt_fusion), kind=kOutput, calls=%fused_computation.94 | convolution fusion | flops 4545576960 | bytes 21125120 | tf_op jit(solution)/shard_map/dot_general | solution.py:250
  168.8 13.2 %multiply_convert_fusion.1 = bf16[512,864]{0,1:T(8,128)(2,1)} fusion(f32[512,864]{0,1:T(8,128)} %fusion.55, bf16[5120,864]{1,0:T(8,128)(2,1)} %bitcast.86, bf16[512,5120]{1,0:T(8,128)(2,1)} %all-reduce.2.cloned.1.call-done, bf16[512,5120]{1,0:T(8,128)(2,1)} %param.24, f32[5120]{0:T(1024)S(1)} %copy-done.5, f32[512]{0:T(512)S(1)} %add_rsqrt_fusion), kind=kOutput, calls=%fused_computation.14 | convolution fusion | flops 4548231168 | bytes 22009856 | tf_op jit(solution)/shard_map/dot_general | solution.py:251
  (34 shorter events, 2.0 us)
Async XLA Ops:
  15.6 1.6 copy-start.2
  15.7 1.5 copy-start.4
  17.2 2.1 %copy-start.1 = (bf16[384,5120]{1,0:T(8,128)(2,1)S(1)}, bf16[384,5120]{1,0:T(8,128)(2,1)}, u32[]{:S(2)}) copy-start(bf16[384,5120]{1,0:T(8,128)(2,1)} %param.23) | copy-start | bytes 11796484
  25.2 126.1 %all-reduce.2.cloned.1.call-start = ((), (), s32[]{:S(2)}) async-start(), calls=%async_computation.1 | async-start | bytes 10485760 | tf_op jit(solution)/shard_map/psum | solution.py:245
  29.1 120.8 %copy-start.3 = (s32[16,4]{0,1:T(4,128)S(1)}, s32[16,4]{0,1:T(4,128)}, u32[]{:S(2)}) copy-start(s32[16,4]{0,1:T(4,128)} %param.22) | copy-start | bytes 772
  30.8 119.1 %all-to-all-start = ((bf16[16,128,1,256]{3,1,2,0:T(8,128)(2,1)}), bf16[16,128,1,256]{3,1,2,0:T(8,128)(2,1)S(1)}, u32[]{:S(2)}, u32[]{:S(2)}) async-start(bf16[16,128,1,256]{3,1,2,0:T(8,128)(2,1)} %fusion.13), calls=%async_computation | async-start | bytes 2097152 | tf_op jit(solution)/shard_map/all_to_all | solution.py:235
  151.3 6.0 %copy-start.5 = (f32[5120]{0:T(1024)S(1)}, f32[5120]{0:T(1024)}, u32[]{:S(2)}) copy-start(f32[5120]{0:T(1024)} %param.25) | copy-start | bytes 61444
  151.3 6.0 %copy-start = (bf16[512,5120]{1,0:T(8,128)(2,1)S(1)}, bf16[512,5120]{1,0:T(8,128)(2,1)}, u32[]{:S(2)}) copy-start(bf16[512,5120]{1,0:T(8,128)(2,1)} %all-reduce.2.cloned.1.call-done) | copy-start | bytes 15728644
Sparse Core Ops, SparseCore 0:
  28.4 80.3 all-reduce.1

commit v6 on v5

--- a/solution.py
+++ b/solution.py
@@ -11,6 +11,7 @@
 PAGE = 128
 REQS = 4
 RING = 4
+KV_SEMS = 40
 
 
 THETA = 1000000.0
@@ -31,7 +32,7 @@
     )
 
 
-def gather_kernel(wg_ref, wu_ref, after_ref, g_ref, u_ref, send_sems, recv_sems, local_sems):
+def gather_kernel(wg_ref, wu_ref, kv_ref, after_ref, g_ref, u_ref, kv_out, send_sems, recv_sems, local_sems):
     me = lax.axis_index("req")
     col = lax.axis_index("mp")
     z = me // RING
@@ -50,12 +51,30 @@
     def to(zz, yy):
         return (zz * RING + yy, col)
 
+    groups = kv_ref.shape[0]
     barrier = pltpu.get_barrier_semaphore()
-    for peer in (to(z, yp), to(z, ym), to(zp, y), to(zm, y)):
+    for d in range(1, groups):
+        peer = ((me + d) % groups, col)
         pl.semaphore_signal(barrier, inc=1, device_id=peer, device_id_type=mesh_id)
-    pl.semaphore_wait(barrier, 4)
+    pl.semaphore_wait(barrier, groups - 1)
 
     copies = []
+    own_kv = pltpu.make_async_copy(kv_ref.at[me], kv_out.at[me], local_sems.at[2])
+    own_kv.start()
+    for d in range(1, groups):
+        dest = (me + d) % groups
+        c = pltpu.make_async_remote_copy(
+            src_ref=kv_ref.at[dest],
+            dst_ref=kv_out.at[me],
+            send_sem=send_sems.at[KV_SEMS + d - 1],
+            recv_sem=recv_sems.at[KV_SEMS + d - 1],
+            device_id=(dest, col),
+            device_id_type=mesh_id,
+        )
+        c.start()
+        copies.append(c)
+    kv_copies = list(copies)
+    copies.clear()
 
     def send(src, dst, peer):
         k = len(copies)
@@ -124,26 +143,32 @@
             c.wait_recv()
     for c in copies:
         c.wait_send()
+    for c in kv_copies:
+        c.wait_recv()
+        c.wait_send()
     own_g.wait()
     own_u.wait()
-
-
-def gather_weights(w_gate, w_up, after):
+    own_kv.wait()
+
+
+def gather_weights(w_gate, w_up, kv_send, after):
     rows, cols = w_gate.shape
     any_spec = pl.BlockSpec(memory_space=pl.ANY)
     piece = jax.ShapeDtypeStruct((RING, RING, rows, cols), w_gate.dtype)
+    slots = jax.ShapeDtypeStruct(kv_send.shape, kv_send.dtype)
+    sems = KV_SEMS + kv_send.shape[0] - 1
     return pl.pallas_call(
         gather_kernel,
-        out_shape=(piece, piece),
-        in_specs=[any_spec, any_spec, any_spec],
-        out_specs=(any_spec, any_spec),
+        out_shape=(piece, piece, slots),
+        in_specs=[any_spec, any_spec, any_spec, any_spec],
+        out_specs=(any_spec, any_spec, any_spec),
         scratch_shapes=[
-            pltpu.SemaphoreType.DMA((40,)),
-            pltpu.SemaphoreType.DMA((40,)),
-            pltpu.SemaphoreType.DMA((2,)),
+            pltpu.SemaphoreType.DMA((sems,)),
+            pltpu.SemaphoreType.DMA((sems,)),
+            pltpu.SemaphoreType.DMA((3,)),
         ],
         compiler_params=pltpu.CompilerParams(collective_id=0, has_side_effects=True),
-    )(w_gate, w_up, after)
+    )(w_gate, w_up, kv_send, after)
 
 def normalize(resid_rows, summed, gain_row):
     state = resid_rows.astype(jnp.float32) + summed
@@ -231,20 +256,20 @@
     select = jnp.sum(picks.astype(jnp.int32), axis=1).astype(jnp.bfloat16)
     kv_send = jnp.einsum(
         "gst,tc->gsc", select, kv_rows, preferred_element_type=jnp.float32
-    ).astype(jnp.bfloat16).reshape(groups_all, PAGE, kv_heads, 2 * HD)
-    kv_in = lax.all_to_all(kv_send, "req", split_axis=0, concat_axis=0, tiled=True)
+    ).astype(jnp.bfloat16)
     hits = (
         page_table[None, :, :] == (me_req * REQS + jnp.arange(REQS, dtype=jnp.int32))[:, None, None]
     )
     page_select = jnp.sum(hits.astype(jnp.int32), axis=2).astype(jnp.bfloat16)
+
+    product = jnp.dot(attended, w_out, preferred_element_type=jnp.float32).astype(jnp.bfloat16)
+    summed = lax.psum(product, "mp").astype(jnp.float32)
+    normed = normalize(residual, summed, norm_gain)
+    g_full, u_full, kv_in = gather_weights(w_gate, w_up, kv_send, product[:8, :128])
+    kv_in = kv_in.reshape(groups_all, PAGE, kv_heads, 2 * HD)
     cache_out = jnp.einsum(
         "ls,sphc->lhpc", page_select, kv_in, preferred_element_type=jnp.float32
     ).astype(jnp.bfloat16)
-
-    product = jnp.dot(attended, w_out, preferred_element_type=jnp.float32).astype(jnp.bfloat16)
-    summed = lax.psum(product, "mp").astype(jnp.float32)
-    normed = normalize(residual, summed, norm_gain)
-    g_full, u_full = gather_weights(w_gate, w_up, product[:8, :128])
     wg_full = g_full.reshape(-1, w_gate.shape[1])
     wu_full = u_full.reshape(-1, w_up.shape[1])
     gate_acc = jnp.dot(normed, wg_full, preferred_element_type=jnp.float32)

time: 189 us -> 186 us (0.984)
  starting transfers between devices: 8.32 us -> 0.01 us
  Pallas kernels: 111 us -> 114 us
    all_to_all x1 -> x0, starting transfers between devices: 8.31 us -> none  [shards(): lax.all_to_all(kv_send, 'req', split_axis=0, concat_axis=0, tiled=True)]
    pallas_call x1, Pallas kernels: 111 us -> 114 us  [gather_weights(): pl.pallas_call(gather_kernel, out_shape=(piece, piece, slots), in_specs=[...]
  transfers between devices with their start and end apart: 2 -> 1, of which waited for: 0 -> 0; matrix products, arithmetic and copies ran while one was open for 3% -> 4% of each run, Pallas kernels for 59% -> 62%
where the time goes in v6:
time: 186 us
  Pallas kernels  114 us (61%)
  matrix products  35.2 us (19%)
  other arithmetic  17.2 us (9%)
  between operations  14.2 us (8%)
  local copies, waits for them, and re-layouts  4.17 us (2%)
    pallas_call x1, Pallas kernels, gather_weights(): pl.pallas_call(gather_kernel, out_shape=(piece, piece, slots), in_specs=[...  114 us
    dot_general x1, matrix products, shards(): up_acc = jnp.dot(normed, wu_full, preferred_element_type=jnp.float32)  13.4 us
    dot_general x1, matrix products, shards(): gate_acc = jnp.dot(normed, wg_full, preferred_element_type=jnp.float32)  11.5 us
    reduce_sum x1, other arithmetic, normalize(): scale_row = lax.rsqrt(jnp.mean(state * state, axis=-1, keepdims=True) + EPS)  5.96 us
    dot_general x1, matrix products, shards(): jnp.dot(attended, w_out, preferred_element_type=jnp.float32)  4.65 us
  transfers between devices with their start and end apart: 1, of which 0 were waited for; matrix products, arithmetic and copies ran while one was open for 4% of the time, Pallas kernels for 62%

profile of v6, /device:TPU:0, one launch (start us, length us, event | category | flops | bytes accessed | tf_op | source)
XLA Modules:
  0.0 185.9 jit_solution(2279850399405488522)
XLA Ops:
  7.2 0.7 broadcast_compare_fusion
  7.9 0.7 subtract_clamp_fusion
  8.6 0.9 fusion.41
  9.8 1.0 fusion.18
  10.8 0.9 add_bitcast_fusion
  11.7 0.5 multiply_cosine_fusion.1
  12.3 1.2 fusion.28
  13.5 1.2 copy.33
  14.7 0.8 convert_add_fusion.1
  15.7 0.8 fusion
  16.5 0.7 fusion.3
  17.2 1.2 fusion.13
  18.4 0.9 copy-done.1
  19.3 4.7 %convolution_convert_fusion = bf16[512,5120]{1,0:T(8,128)(2,1)} fusion(bf16[512,384]{0,1:T(8,128)(2,1)S(1)} %bitcast.76, bf16[384,5120]{1,0:T(8,128)(2,1)S(1)} %copy-done.1), kind=kOutput, calls=%fused_computation.4 | convolution fusion | flops 2015887360 | bytes 9568256 | tf_op jit(solution)/shard_map/dot_general | solution.py:265
  24.0 1.3 slice.24.after_ref
  25.2 0.7 all-reduce.2.cloned.1.call-update
  26.7 2.5 %convert_reduce_fusion = s32[16,128,512]{2,1,0:T(8,128)S(1)} fusion(pred[4,128,512]{2,1,0:T(8,128)(4,1)S(1)} %iota_compare_fusion, pred[16,4,128]{2,1,0:T(4,128)(4,1)S(1)} %broadcast_and_fusion), kind=kLoop, calls=%fused_computation | loop fusion | flops 11534336 | bytes 4464640 | tf_op jit(solution)/shard_map/reduce_sum | solution.py:256
  29.2 1.7 fusion.10.kv_ref
  31.0 114.4 %shard_map.149 = (bf16[4,4,320,864]{3,2,1,0:T(8,128)(2,1)}, bf16[4,4,320,864]{3,2,1,0:T(8,128)(2,1)}, bf16[16,128,256]{2,1,0:T(8,128)(2,1)}) custom-call(bf16[320,864]{1,0:T(8,128)(2,1)} %wg_ref.1, bf16[320,864]{1,0:T(8,128)(2,1)} %wu_ref.1, bf16[16,128,256]{2,1,0:T(8,128)(2,1)} %fusion.10.kv_ref, bf16[8,128]{1,0:T(8,128)(2,1)} %slice.24.after_ref), custom_call_target="tpu_custom_call" | custom-call | tf_op jit(solution)/shard_map/pallas_call | solution.py:160
  145.5 1.9 %fusion.16 = bf16[4,1,128,256]{3,0,2,1:T(4,128)(2,1)S(1)} fusion(bf16[16,128,256]{2,1,0:T(8,128)(2,1)} %get-tuple-element.7, s32[4,16]{1,0:T(4,128)S(1)} %convert_reduce_fusion.1), kind=kOutput, calls=%fused_computation.22 | convolution fusion | flops 4325440 | bytes 1310976 | tf_op jit(solution)/shard_map/ls,sphc->lhpc/dot_general | solution.py:270
  147.4 0.7 copy.38
  148.1 6.0 %multiply_reduce_fusion = f32[512]{0:T(512)S(1)} fusion(bf16[512,5120]{1,0:T(8,128)(2,1)} %all-reduce.2.cloned.1.call-done, bf16[512,5120]{1,0:T(8,128)(2,1)} %param.24), kind=kLoop, calls=%fused_computation.2 | loop fusion | flops 13106688 | bytes 10487808 | tf_op jit(solution)/shard_map/reduce_sum | solution.py:175
  154.1 11.5 %fusion.51 = f32[512,864]{0,1:T(8,128)} fusion(bf16[5120,864]{1,0:T(8,128)(2,1)} %bitcast.80, bf16[512,5120]{1,0:T(8,128)(2,1)S(1)} %copy-done, bf16[512,5120]{1,0:T(8,128)(2,1)} %param.24, f32[5120]{0:T(1024)S(1)} %copy-done.5, f32[512]{0:T(512)S(1)} %add_rsqrt_fusion), kind=kOutput, calls=%fused_computation.92 | convolution fusion | flops 4545576960 | bytes 21125120 | tf_op jit(solution)/shard_map/dot_general | solution.py:275
  165.6 13.4 %multiply_convert_fusion.1 = bf16[512,864]{0,1:T(8,128)(2,1)} fusion(f32[512,864]{0,1:T(8,128)} %fusion.51, bf16[5120,864]{1,0:T(8,128)(2,1)} %bitcast.79, bf16[512,5120]{1,0:T(8,128)(2,1)} %all-reduce.2.cloned.1.call-done, bf16[512,5120]{1,0:T(8,128)(2,1)} %param.24, f32[5120]{0:T(1024)S(1)} %copy-done.5, f32[512]{0:T(512)S(1)} %add_rsqrt_fusion), kind=kOutput, calls=%fused_computation.14 | convolution fusion | flops 4548231168 | bytes 22009856 | tf_op jit(solution)/shard_map/dot_general | solution.py:276
  (32 shorter events, 1.4 us)
Async XLA Ops:
  15.6 1.6 copy-start.2
  15.7 1.5 copy-start.4
  17.2 2.1 %copy-start.1 = (bf16[384,5120]{1,0:T(8,128)(2,1)S(1)}, bf16[384,5120]{1,0:T(8,128)(2,1)}, u32[]{:S(2)}) copy-start(bf16[384,5120]{1,0:T(8,128)(2,1)} %param.23) | copy-start | bytes 11796484
  25.2 122.9 %all-reduce.2.cloned.1.call-start = ((), (), s32[]{:S(2)}) async-start(), calls=%async_computation | async-start | bytes 10485760 | tf_op jit(solution)/shard_map/psum | solution.py:266
  29.2 116.2 %copy-start.3 = (s32[16,4]{0,1:T(4,128)S(1)}, s32[16,4]{0,1:T(4,128)}, u32[]{:S(2)}) copy-start(s32[16,4]{0,1:T(4,128)} %param.22) | copy-start | bytes 772
  148.1 6.0 %copy-start.5 = (f32[5120]{0:T(1024)S(1)}, f32[5120]{0:T(1024)}, u32[]{:S(2)}) copy-start(f32[5120]{0:T(1024)} %param.25) | copy-start | bytes 61444
  148.1 6.0 %copy-start = (bf16[512,5120]{1,0:T(8,128)(2,1)S(1)}, bf16[512,5120]{1,0:T(8,128)(2,1)}, u32[]{:S(2)}) copy-start(bf16[512,5120]{1,0:T(8,128)(2,1)} %all-reduce.2.cloned.1.call-done) | copy-start | bytes 15728644
Sparse Core Ops, SparseCore 0:
  28.4 80.3 all-reduce.1

commit v7 on v6

--- a/solution.py
+++ b/solution.py
@@ -11,7 +11,7 @@
 PAGE = 128
 REQS = 4
 RING = 4
-KV_SEMS = 40
+KV_SEMS = 36
 
 
 THETA = 1000000.0
@@ -32,7 +32,10 @@
     )
 
 
-def gather_kernel(wg_ref, wu_ref, kv_ref, after_ref, g_ref, u_ref, kv_out, send_sems, recv_sems, local_sems):
+def gather_kernel(
+    wg_ref, wu_ref, gm_ref, gp_ref, um_ref, up_ref, kv_ref, after_ref,
+    g_ref, u_ref, kv_out, send_sems, recv_sems, local_sems,
+):
     me = lax.axis_index("req")
     col = lax.axis_index("mp")
     z = me // RING
@@ -59,7 +62,7 @@
     pl.semaphore_wait(barrier, groups - 1)
 
     copies = []
-    own_kv = pltpu.make_async_copy(kv_ref.at[me], kv_out.at[me], local_sems.at[2])
+    own_kv = pltpu.make_async_copy(kv_ref.at[me], kv_out.at[me], local_sems.at[6])
     own_kv.start()
     for d in range(1, groups):
         dest = (me + d) % groups
@@ -90,30 +93,29 @@
         copies.append(c)
         return c
 
-    own_g = pltpu.make_async_copy(wg_ref, g_ref.at[z, y], local_sems.at[0])
-    own_u = pltpu.make_async_copy(wu_ref, u_ref.at[z, y], local_sems.at[1])
-    own_g.start()
-    own_u.start()
-
-    g_from_ym = send(wg_ref, g_ref.at[z, y], to(z, yp))
-    g_from_yp = send(wg_ref, g_ref.at[z, y], to(z, ym))
-    u_from_zm = send(wu_ref, u_ref.at[z, y], to(zp, y))
-    u_from_zp = send(wu_ref, u_ref.at[z, y], to(zm, y))
+    placed = []
+    for k, (src_ref, dst_ref) in enumerate((
+        (wg_ref, g_ref.at[z, y]),
+        (wu_ref, u_ref.at[z, y]),
+        (gm_ref, g_ref.at[z, ym]),
+        (gp_ref, g_ref.at[z, yp]),
+        (um_ref, u_ref.at[zm, y]),
+        (up_ref, u_ref.at[zp, y]),
+    )):
+        c = pltpu.make_async_copy(src_ref, dst_ref, local_sems.at[k])
+        c.start()
+        placed.append(c)
+
+    g_far_a = send(gm_ref.at[low], g_ref.at[z, ym, low], to(z, yp))
+    g_far_b = send(gp_ref.at[high], g_ref.at[z, yp, high], to(z, ym))
+    u_far_a = send(um_ref.at[low], u_ref.at[zm, y, low], to(zp, y))
+    u_far_b = send(up_ref.at[high], u_ref.at[zp, y, high], to(zm, y))
     gz = {"y": (send(wg_ref, g_ref.at[z, y], to(zp, y)), send(wg_ref, g_ref.at[z, y], to(zm, y)))}
     uy = {"z": (send(wu_ref, u_ref.at[z, y], to(z, yp)), send(wu_ref, u_ref.at[z, y], to(z, ym)))}
-
-    g_from_ym.wait_recv()
-    g_far_a = send(g_ref.at[z, ym, low], g_ref.at[z, ym, low], to(z, yp))
-    gz["ym"] = (send(g_ref.at[z, ym], g_ref.at[z, ym], to(zp, y)), send(g_ref.at[z, ym], g_ref.at[z, ym], to(zm, y)))
-    u_from_zm.wait_recv()
-    u_far_a = send(u_ref.at[zm, y, low], u_ref.at[zm, y, low], to(zp, y))
-    uy["zm"] = (send(u_ref.at[zm, y], u_ref.at[zm, y], to(z, yp)), send(u_ref.at[zm, y], u_ref.at[zm, y], to(z, ym)))
-    g_from_yp.wait_recv()
-    g_far_b = send(g_ref.at[z, yp, high], g_ref.at[z, yp, high], to(z, ym))
-    gz["yp"] = (send(g_ref.at[z, yp], g_ref.at[z, yp], to(zp, y)), send(g_ref.at[z, yp], g_ref.at[z, yp], to(zm, y)))
-    u_from_zp.wait_recv()
-    u_far_b = send(u_ref.at[zp, y, high], u_ref.at[zp, y, high], to(zm, y))
-    uy["zp"] = (send(u_ref.at[zp, y], u_ref.at[zp, y], to(z, yp)), send(u_ref.at[zp, y], u_ref.at[zp, y], to(z, ym)))
+    gz["ym"] = (send(gm_ref, g_ref.at[z, ym], to(zp, y)), send(gm_ref, g_ref.at[z, ym], to(zm, y)))
+    uy["zm"] = (send(um_ref, u_ref.at[zm, y], to(z, yp)), send(um_ref, u_ref.at[zm, y], to(z, ym)))
+    gz["yp"] = (send(gp_ref, g_ref.at[z, yp], to(zp, y)), send(gp_ref, g_ref.at[z, yp], to(zm, y)))
+    uy["zp"] = (send(up_ref, u_ref.at[zp, y], to(z, yp)), send(up_ref, u_ref.at[zp, y], to(z, ym)))
 
     g_far_a.wait_recv()
     g_far_b.wait_recv()
@@ -135,7 +137,8 @@
         from_yp.wait_recv()
         send(u_ref.at[zz, yp, high], u_ref.at[zz, yp, high], to(z, ym))
 
-    waited = [g_from_ym, g_from_yp, u_from_zm, u_from_zp, g_far_a, g_far_b, u_far_a, u_far_b]
+    assert len(copies) <= KV_SEMS
+    waited = [g_far_a, g_far_b, u_far_a, u_far_b]
     waited += list(gz["y"]) + list(gz["ym"]) + list(gz["yp"]) + list(gz["y2"])
     waited += list(uy["z"]) + list(uy["zm"]) + list(uy["zp"]) + list(uy["z2"])
     for c in copies:
@@ -146,12 +149,29 @@
     for c in kv_copies:
         c.wait_recv()
         c.wait_send()
-    own_g.wait()
-    own_u.wait()
+    for c in placed:
+        c.wait()
     own_kv.wait()
 
 
-def gather_weights(w_gate, w_up, kv_send, after):
+def y_shift(d, n):
+    return [(i, (i // RING) * RING + (i % RING + d) % RING) for i in range(n)]
+
+
+def z_shift(d, n):
+    return [(i, ((i // RING + d) % RING) * RING + i % RING) for i in range(n)]
+
+
+def first_hops(w_gate, w_up, n):
+    return (
+        lax.ppermute(w_gate, "req", y_shift(1, n)),
+        lax.ppermute(w_gate, "req", y_shift(-1, n)),
+        lax.ppermute(w_up, "req", z_shift(1, n)),
+        lax.ppermute(w_up, "req", z_shift(-1, n)),
+    )
+
+
+def gather_weights(w_gate, w_up, hops, kv_send, after):
     rows, cols = w_gate.shape
     any_spec = pl.BlockSpec(memory_space=pl.ANY)
     piece = jax.ShapeDtypeStruct((RING, RING, rows, cols), w_gate.dtype)
@@ -160,15 +180,15 @@
     return pl.pallas_call(
         gather_kernel,
         out_shape=(piece, piece, slots),
-        in_specs=[any_spec, any_spec, any_spec, any_spec],
+        in_specs=[any_spec] * 8,
         out_specs=(any_spec, any_spec, any_spec),
         scratch_shapes=[
             pltpu.SemaphoreType.DMA((sems,)),
             pltpu.SemaphoreType.DMA((sems,)),
-            pltpu.SemaphoreType.DMA((3,)),
+            pltpu.SemaphoreType.DMA((7,)),
         ],
         compiler_params=pltpu.CompilerParams(collective_id=0, has_side_effects=True),
-    )(w_gate, w_up, kv_send, after)
+    )(w_gate, w_up, *hops, kv_send, after)
 
 def normalize(resid_rows, summed, gain_row):
     state = resid_rows.astype(jnp.float32) + summed
@@ -200,6 +220,8 @@
     group_size = q_heads // kv_heads
 
 
+    hops = first_hops(w_gate, w_up, groups_all)
+
     own_lens = lax.dynamic_index_in_dim(lengths, me_req, 0, keepdims=False)
     own_pages = lax.dynamic_index_in_dim(page_table, me_req, 0, keepdims=False)
     own_owner = own_pages // REQS
@@ -265,7 +287,7 @@
     product = jnp.dot(attended, w_out, preferred_element_type=jnp.float32).astype(jnp.bfloat16)
     summed = lax.psum(product, "mp").astype(jnp.float32)
     normed = normalize(residual, summed, norm_gain)
-    g_full, u_full, kv_in = gather_weights(w_gate, w_up, kv_send, product[:8, :128])
+    g_full, u_full, kv_in = gather_weights(w_gate, w_up, hops, kv_send, product[:8, :128])
     kv_in = kv_in.reshape(groups_all, PAGE, kv_heads, 2 * HD)
     cache_out = jnp.einsum(
         "ls,sphc->lhpc", page_select, kv_in, preferred_element_type=jnp.float32

time: 186 us -> 193 us (1.038)
  starting transfers between devices: 0.01 us -> 7.43 us
  Pallas kernels: 114 us -> 112 us
  local copies, waits for them, and re-layouts: 4.17 us -> 6.17 us
    ppermute x0 -> x4, starting transfers between devices: none -> 7.43 us  [the longest x1 2.12 us: first_hops(): lax.ppermute(w_up, 'req', z_shift(-1, n))]
    pallas_call x1, Pallas kernels: 114 us -> 112 us  [gather_weights(): pl.pallas_call(gather_kernel, out_shape=(piece, piece, slots), in_specs=[...]
    unnamed x15 -> x23, local copies, waits for them, and re-layouts: 2.92 us -> 4.91 us
  transfers between devices with their start and end apart: 1 -> 5, of which waited for: 0 -> 0; matrix products, arithmetic and copies ran while one was open for 4% -> 13% of each run, Pallas kernels for 62% -> 58%
where the time goes in v7:
time: 193 us
  Pallas kernels  112 us (58%)
  matrix products  35.2 us (18%)
  other arithmetic  17.2 us (9%)
  between operations  14.3 us (7%)
  starting transfers between devices  7.43 us (4%)
  local copies, waits for them, and re-layouts  6.17 us (3%)
    pallas_call x1, Pallas kernels, gather_weights(): pl.pallas_call(gather_kernel, out_shape=(piece, piece, slots), in_specs=[...  112 us
    dot_general x1, matrix products, shards(): up_acc = jnp.dot(normed, wu_full, preferred_element_type=jnp.float32)  13.4 us
    dot_general x1, matrix products, shards(): gate_acc = jnp.dot(normed, wg_full, preferred_element_type=jnp.float32)  11.5 us
    reduce_sum x1, other arithmetic, normalize(): scale_row = lax.rsqrt(jnp.mean(state * state, axis=-1, keepdims=True) + EPS)  5.96 us
    unnamed x23, local copies, waits for them, and re-layouts  4.91 us
    dot_general x1, matrix products, shards(): jnp.dot(attended, w_out, preferred_element_type=jnp.float32)  4.65 us
  transfers between devices with their start and end apart: 5, of which 0 were waited for; matrix products, arithmetic and copies ran while one was open for 13% of the time, Pallas kernels for 58%

profile of v7, /device:TPU:0, one launch (start us, length us, event | category | flops | bytes accessed | tf_op | source)
XLA Modules:
  0.0 192.6 jit_solution(4234721864885691419)
XLA Ops:
  7.2 1.7 collective-permute-start
  8.9 1.6 collective-permute-start.1
  10.5 2.0 %collective-permute-start.2 = (bf16[320,864]{1,0:T(8,128)(2,1)}, bf16[320,864]{1,0:T(8,128)(2,1)S(1)}, u32[]{:S(2)}, u32[]{:S(2)}) collective-permute-start(bf16[320,864]{1,0:T(8,128)(2,1)} %wu_ref.1), channel_id=1, source_target_pairs={{0,32},{8,40},{16,48},{24,56},{32,64},{40,72},{48,80},{56,88},{64,... | collective-permute-start | bytes 1658888 | tf_op jit(solution)/shard_map/ppermute | solution.py:169
  12.5 2.1 %collective-permute-start.3 = (bf16[320,864]{1,0:T(8,128)(2,1)}, bf16[320,864]{1,0:T(8,128)(2,1)S(1)}, u32[]{:S(2)}, u32[]{:S(2)}) collective-permute-start(bf16[320,864]{1,0:T(8,128)(2,1)} %wu_ref.1), channel_id=1, source_target_pairs={{0,96},{8,104},{16,112},{24,120},{32,0},{40,8},{48,16},{56,24},{64... | collective-permute-start | bytes 1658888 | tf_op jit(solution)/shard_map/ppermute | solution.py:170
  16.0 0.9 fusion.41
  17.2 1.0 fusion.18
  18.2 0.9 add_bitcast_fusion
  19.7 1.2 fusion.28
  20.9 1.2 copy.33
  22.1 0.8 convert_add_fusion.1
  23.1 0.8 fusion
  24.6 1.2 fusion.13
  25.9 0.9 copy-done.1
  26.7 4.7 %convolution_convert_fusion = bf16[512,5120]{1,0:T(8,128)(2,1)} fusion(bf16[512,384]{0,1:T(8,128)(2,1)S(1)} %bitcast.76, bf16[384,5120]{1,0:T(8,128)(2,1)S(1)} %copy-done.1), kind=kOutput, calls=%fused_computation.4 | convolution fusion | flops 2015887360 | bytes 9568256 | tf_op jit(solution)/shard_map/dot_general | solution.py:287
  31.4 1.3 slice.24.after_ref
  34.1 2.5 %convert_reduce_fusion = s32[16,128,512]{2,1,0:T(8,128)S(1)} fusion(pred[4,128,512]{2,1,0:T(8,128)(4,1)S(1)} %iota_compare_fusion, pred[16,4,128]{2,1,0:T(4,128)(4,1)S(1)} %broadcast_and_fusion), kind=kLoop, calls=%fused_computation | loop fusion | flops 11534336 | bytes 4464640 | tf_op jit(solution)/shard_map/reduce_sum | solution.py:278
  36.8 1.7 fusion.10.kv_ref
  38.5 0.8 copy-done.2
  39.7 0.8 copy-done.5
  40.5 111.7 %shard_map.149 = (bf16[4,4,320,864]{3,2,1,0:T(8,128)(2,1)}, bf16[4,4,320,864]{3,2,1,0:T(8,128)(2,1)}, bf16[16,128,256]{2,1,0:T(8,128)(2,1)}) custom-call(bf16[320,864]{1,0:T(8,128)(2,1)} %wg_ref.1, bf16[320,864]{1,0:T(8,128)(2,1)} %wu_ref.1, bf16[320,864]{1,0:T(8,128)(2,1)} %copy-done.2, bf16[320,864]{1,0:T(8,128)(2,1)} %copy-done.3, ...), custom_call_target="tpu_custom_call" | custom-call | tf_op jit(solution)/shard_map/pallas_call | solution.py:180
  152.3 1.9 fusion.16
  154.9 6.0 %multiply_reduce_fusion = f32[512]{0:T(512)S(1)} fusion(bf16[512,5120]{1,0:T(8,128)(2,1)} %all-reduce.2.cloned.1.call-done, bf16[512,5120]{1,0:T(8,128)(2,1)} %param.24), kind=kLoop, calls=%fused_computation.2 | loop fusion | flops 13106688 | bytes 10487808 | tf_op jit(solution)/shard_map/reduce_sum | solution.py:195
  160.9 11.5 %fusion.52 = f32[512,864]{0,1:T(8,128)} fusion(bf16[5120,864]{1,0:T(8,128)(2,1)} %bitcast.80, bf16[512,5120]{1,0:T(8,128)(2,1)S(1)} %copy-done, bf16[512,5120]{1,0:T(8,128)(2,1)} %param.24, f32[5120]{0:T(1024)S(1)} %copy-done.9, f32[512]{0:T(512)S(1)} %add_rsqrt_fusion), kind=kOutput, calls=%fused_computation.93 | convolution fusion | flops 4545576960 | bytes 21125120 | tf_op jit(solution)/shard_map/dot_general | solution.py:297
  172.4 13.4 %multiply_convert_fusion.1 = bf16[512,864]{0,1:T(8,128)(2,1)} fusion(f32[512,864]{0,1:T(8,128)} %fusion.52, bf16[5120,864]{1,0:T(8,128)(2,1)} %bitcast.79, bf16[512,5120]{1,0:T(8,128)(2,1)} %all-reduce.2.cloned.1.call-done, bf16[512,5120]{1,0:T(8,128)(2,1)} %param.24, f32[5120]{0:T(1024)S(1)} %copy-done.9, f32[512]{0:T(512)S(1)} %add_rsqrt_fusion), kind=kOutput, calls=%fused_computation.14 | convolution fusion | flops 4548231168 | bytes 22009856 | tf_op jit(solution)/shard_map/dot_general | solution.py:298
  (48 shorter events, 5.9 us)
Async XLA Ops:
  7.2 31.3 %collective-permute-start = (bf16[320,864]{1,0:T(8,128)(2,1)}, bf16[320,864]{1,0:T(8,128)(2,1)S(1)}, u32[]{:S(2)}, u32[]{:S(2)}) collective-permute-start(bf16[320,864]{1,0:T(8,128)(2,1)} %wg_ref.1), channel_id=1, source_target_pairs={{0,8},{8,16},{16,24},{24,0},{32,40},{40,48},{48,56},{56,32},{64,72... | collective-permute-start | bytes 1658888 | tf_op jit(solution)/shard_map/ppermute | solution.py:167
  8.9 29.6 %collective-permute-start.1 = (bf16[320,864]{1,0:T(8,128)(2,1)}, bf16[320,864]{1,0:T(8,128)(2,1)S(1)}, u32[]{:S(2)}, u32[]{:S(2)}) collective-permute-start(bf16[320,864]{1,0:T(8,128)(2,1)} %wg_ref.1), channel_id=1, source_target_pairs={{0,24},{8,0},{16,8},{24,16},{32,56},{40,32},{48,40},{56,48},{64,88... | collective-permute-start | bytes 1658888 | tf_op jit(solution)/shard_map/ppermute | solution.py:168
  10.5 28.0 %collective-permute-start.2 = (bf16[320,864]{1,0:T(8,128)(2,1)}, bf16[320,864]{1,0:T(8,128)(2,1)S(1)}, u32[]{:S(2)}, u32[]{:S(2)}) collective-permute-start(bf16[320,864]{1,0:T(8,128)(2,1)} %wu_ref.1), channel_id=1, source_target_pairs={{0,32},{8,40},{16,48},{24,56},{32,64},{40,72},{48,80},{56,88},{64,... | collective-permute-start | bytes 1658888 | tf_op jit(solution)/shard_map/ppermute | solution.py:169
  12.5 26.1 %collective-permute-start.3 = (bf16[320,864]{1,0:T(8,128)(2,1)}, bf16[320,864]{1,0:T(8,128)(2,1)S(1)}, u32[]{:S(2)}, u32[]{:S(2)}) collective-permute-start(bf16[320,864]{1,0:T(8,128)(2,1)} %wu_ref.1), channel_id=1, source_target_pairs={{0,96},{8,104},{16,112},{24,120},{32,0},{40,8},{48,16},{56,24},{64... | collective-permute-start | bytes 1658888 | tf_op jit(solution)/shard_map/ppermute | solution.py:170
  23.1 1.6 copy-start.6
  23.1 1.6 copy-start.8
  24.6 2.1 %copy-start.1 = (bf16[384,5120]{1,0:T(8,128)(2,1)S(1)}, bf16[384,5120]{1,0:T(8,128)(2,1)}, u32[]{:S(2)}) copy-start(bf16[384,5120]{1,0:T(8,128)(2,1)} %param.23) | copy-start | bytes 11796484
  31.4 2.0 %copy-start.7 = (s32[16,4]{0,1:T(4,128)S(1)}, s32[16,4]{0,1:T(4,128)}, u32[]{:S(2)}) copy-start(s32[16,4]{0,1:T(4,128)} %param.22) | copy-start | bytes 772
  32.7 122.2 %all-reduce.2.cloned.1.call-start = ((), (), s32[]{:S(2)}) async-start(), calls=%async_computation | async-start | bytes 10485760 | tf_op jit(solution)/shard_map/psum | solution.py:288
  38.5 0.8 copy-start.2
  38.5 1.0 copy-start.3
  38.5 1.2 copy-start.4
  39.7 0.8 copy-start.5
  154.9 6.0 %copy-start.9 = (f32[5120]{0:T(1024)S(1)}, f32[5120]{0:T(1024)}, u32[]{:S(2)}) copy-start(f32[5120]{0:T(1024)} %param.25) | copy-start | bytes 61444
  154.9 6.0 %copy-start = (bf16[512,5120]{1,0:T(8,128)(2,1)S(1)}, bf16[512,5120]{1,0:T(8,128)(2,1)}, u32[]{:S(2)}) copy-start(bf16[512,5120]{1,0:T(8,128)(2,1)} %all-reduce.2.cloned.1.call-done) | copy-start | bytes 15728644
Sparse Core Ops, SparseCore 0:
  35.9 77.0 all-reduce.1

commit v8 on v6

--- a/solution.py
+++ b/solution.py
@@ -12,6 +12,7 @@
 REQS = 4
 RING = 4
 KV_SEMS = 40
+AR_TILE = 512
 
 
 THETA = 1000000.0
@@ -32,7 +33,10 @@
     )
 
 
-def gather_kernel(wg_ref, wu_ref, kv_ref, after_ref, g_ref, u_ref, kv_out, send_sems, recv_sems, local_sems):
+def gather_kernel(
+    wg_ref, wu_ref, kv_ref, prod_ref, g_ref, u_ref, kv_out, sum_ref,
+    send_sems, recv_sems, local_sems, ar_send, ar_recv, a_buf, p_buf, b_src, b_buf, m_buf,
+):
     me = lax.axis_index("req")
     col = lax.axis_index("mp")
     z = me // RING
@@ -52,11 +56,37 @@
         return (zz * RING + yy, col)
 
     groups = kv_ref.shape[0]
+    xs = prod_ref.shape[0]
+    cx = col // 2
+    cc = col % 2
+    core_peer = (me, cx * 2 + 1 - cc)
+    x_peers = [(me, ((cx + d) % xs) * 2 + cc) for d in range(1, xs)]
+
     barrier = pltpu.get_barrier_semaphore()
     for d in range(1, groups):
         peer = ((me + d) % groups, col)
         pl.semaphore_signal(barrier, inc=1, device_id=peer, device_id_type=mesh_id)
-    pl.semaphore_wait(barrier, groups - 1)
+    for peer in [core_peer] + x_peers:
+        pl.semaphore_signal(barrier, inc=1, device_id=peer, device_id_type=mesh_id)
+    pl.semaphore_wait(barrier, groups - 1 + xs)
+
+    def ar_copy(k, src, dst, peer):
+        c = pltpu.make_async_remote_copy(
+            src_ref=src,
+            dst_ref=dst,
+            send_sem=ar_send.at[k],
+            recv_sem=ar_recv.at[k],
+            device_id=peer,
+            device_id_type=mesh_id,
+        )
+        c.start()
+        return c
+
+    ar_a = ar_copy(0, prod_ref.at[:, 1 - cc], a_buf, core_peer)
+    p_load = pltpu.make_async_copy(prod_ref.at[:, cc], p_buf, local_sems.at[3])
+    p_load.start()
+    width = AR_TILE
+    tiles = a_buf.shape[-1] // width
 
     copies = []
     own_kv = pltpu.make_async_copy(kv_ref.at[me], kv_out.at[me], local_sems.at[2])
@@ -102,6 +132,22 @@
     gz = {"y": (send(wg_ref, g_ref.at[z, y], to(zp, y)), send(wg_ref, g_ref.at[z, y], to(zm, y)))}
     uy = {"z": (send(wu_ref, u_ref.at[z, y], to(z, yp)), send(wu_ref, u_ref.at[z, y], to(z, ym)))}
 
+    ar_a.wait_recv()
+    p_load.wait()
+
+    def add_pair(i, carry):
+        xi = i // tiles
+        cols = pl.ds(pl.multiple_of((i % tiles) * width, width), width)
+        b_src[xi, :, cols] = p_buf[xi, :, cols].astype(jnp.float32) + a_buf[xi, :, cols].astype(
+            jnp.float32
+        )
+        return carry
+
+    lax.fori_loop(0, xs * tiles, add_pair, 0)
+    ar_b = [
+        ar_copy(d, b_src.at[(cx + d) % xs], b_buf.at[cx], x_peers[d - 1]) for d in range(1, xs)
+    ]
+
     g_from_ym.wait_recv()
     g_far_a = send(g_ref.at[z, ym, low], g_ref.at[z, ym, low], to(z, yp))
     gz["ym"] = (send(g_ref.at[z, ym], g_ref.at[z, ym], to(zp, y)), send(g_ref.at[z, ym], g_ref.at[z, ym], to(zm, y)))
@@ -122,6 +168,26 @@
     u_far_b.wait_recv()
     uy["z2"] = (send(u_ref.at[z2, y], u_ref.at[z2, y], to(z, yp)), send(u_ref.at[z2, y], u_ref.at[z2, y], to(z, ym)))
 
+    for c in ar_b:
+        c.wait_recv()
+
+    def add_chips(t, carry):
+        cols = pl.ds(pl.multiple_of(t * width, width), width)
+        acc = b_src[cx, :, cols]
+        for d in range(1, xs):
+            acc = acc + b_buf[(cx + d) % xs, :, cols]
+        m_buf[:, cols] = acc.astype(m_buf.dtype)
+        return carry
+
+    lax.fori_loop(0, tiles, add_chips, 0)
+    own_sum = pltpu.make_async_copy(m_buf, sum_ref.at[cx, cc], local_sems.at[4])
+    own_sum.start()
+    own_sum.wait()
+    ar_c = [
+        ar_copy(xs - 1 + d, sum_ref.at[cx, cc], sum_ref.at[cx, cc], x_peers[d - 1])
+        for d in range(1, xs)
+    ]
+
     for key, yy in (("y", y), ("ym", ym), ("yp", yp), ("y2", y2)):
         from_zm, from_zp = gz[key]
         from_zm.wait_recv()
@@ -134,6 +200,13 @@
         send(u_ref.at[zz, ym, low], u_ref.at[zz, ym, low], to(z, yp))
         from_yp.wait_recv()
         send(u_ref.at[zz, yp, high], u_ref.at[zz, yp, high], to(z, ym))
+
+    for c in ar_c:
+        c.wait_recv()
+    ar_d = ar_copy(2 * xs - 1, sum_ref.at[:, cc], sum_ref.at[:, cc], core_peer)
+    ar_d.wait_recv()
+    for c in [ar_a] + ar_b + ar_c + [ar_d]:
+        c.wait_send()
 
     waited = [g_from_ym, g_from_yp, u_from_zm, u_from_zp, g_far_a, g_far_b, u_far_a, u_far_b]
     waited += list(gz["y"]) + list(gz["ym"]) + list(gz["yp"]) + list(gz["y2"])
@@ -151,24 +224,35 @@
     own_kv.wait()
 
 
-def gather_weights(w_gate, w_up, kv_send, after):
+def gather_weights(w_gate, w_up, kv_send, product):
     rows, cols = w_gate.shape
+    xs, _, chunk, width = product.shape
     any_spec = pl.BlockSpec(memory_space=pl.ANY)
     piece = jax.ShapeDtypeStruct((RING, RING, rows, cols), w_gate.dtype)
     slots = jax.ShapeDtypeStruct(kv_send.shape, kv_send.dtype)
+    sums = jax.ShapeDtypeStruct(product.shape, product.dtype)
     sems = KV_SEMS + kv_send.shape[0] - 1
     return pl.pallas_call(
         gather_kernel,
-        out_shape=(piece, piece, slots),
+        out_shape=(piece, piece, slots, sums),
         in_specs=[any_spec, any_spec, any_spec, any_spec],
-        out_specs=(any_spec, any_spec, any_spec),
+        out_specs=(any_spec, any_spec, any_spec, any_spec),
         scratch_shapes=[
             pltpu.SemaphoreType.DMA((sems,)),
             pltpu.SemaphoreType.DMA((sems,)),
-            pltpu.SemaphoreType.DMA((3,)),
+            pltpu.SemaphoreType.DMA((5,)),
+            pltpu.SemaphoreType.DMA((2 * xs,)),
+            pltpu.SemaphoreType.DMA((2 * xs,)),
+            pltpu.VMEM((xs, chunk, width), product.dtype),
+            pltpu.VMEM((xs, chunk, width), product.dtype),
+            pltpu.VMEM((xs, chunk, width), jnp.float32),
+            pltpu.VMEM((xs, chunk, width), jnp.float32),
+            pltpu.VMEM((chunk, width), product.dtype),
         ],
-        compiler_params=pltpu.CompilerParams(collective_id=0, has_side_effects=True),
-    )(w_gate, w_up, kv_send, after)
+        compiler_params=pltpu.CompilerParams(
+            collective_id=0, has_side_effects=True, vmem_limit_bytes=48 * 1024 * 1024
+        ),
+    )(w_gate, w_up, kv_send, product)
 
 def normalize(resid_rows, summed, gain_row):
     state = resid_rows.astype(jnp.float32) + summed
@@ -263,9 +347,11 @@
     page_select = jnp.sum(hits.astype(jnp.int32), axis=2).astype(jnp.bfloat16)
 
     product = jnp.dot(attended, w_out, preferred_element_type=jnp.float32).astype(jnp.bfloat16)
-    summed = lax.psum(product, "mp").astype(jnp.float32)
+    n_mp = lax.axis_size("mp")
+    product = product.reshape(n_mp // 2, 2, block_rows // n_mp, product.shape[-1])
+    g_full, u_full, kv_in, summed = gather_weights(w_gate, w_up, kv_send, product)
+    summed = summed.reshape(block_rows, -1).astype(jnp.float32)
     normed = normalize(residual, summed, norm_gain)
-    g_full, u_full, kv_in = gather_weights(w_gate, w_up, kv_send, product[:8, :128])
     kv_in = kv_in.reshape(groups_all, PAGE, kv_heads, 2 * HD)
     cache_out = jnp.einsum(
         "ls,sphc->lhpc", page_select, kv_in, preferred_element_type=jnp.float32

time: 186 us -> 169 us (0.909)
  between operations: 14.2 us -> 0.94 us
  matrix products: 35.2 us -> 28.9 us
  other arithmetic: 17.2 us -> 19.6 us
  Pallas kernels: 114 us -> 116 us
    convert_element_type x0 -> x1, other arithmetic: none -> 5.58 us  [normalize(): return (state * scale_row * gain_row).astype(jnp.bfloat16)]
    dot_general x1, matrix products: 13.4 us -> 9.55 us  [shards(): up_acc = jnp.dot(normed, wu_full, preferred_element_type=jnp.float32)]
  transfers between devices with their start and end apart: 1 -> 0, of which waited for: 0 -> 0; matrix products, arithmetic and copies ran while one was open for 4% -> 0% of each run, Pallas kernels for 62% -> 0%
where the time goes in v8:
time: 169 us
  Pallas kernels  116 us (69%)
  matrix products  28.9 us (17%)
  other arithmetic  19.6 us (12%)
  local copies, waits for them, and re-layouts  3.3 us (2%)
    pallas_call x1, Pallas kernels, gather_weights(): pl.pallas_call(gather_kernel, out_shape=(piece, piece, slots, sums), in_s...  116 us
    dot_general x1, matrix products, shards(): gate_acc = jnp.dot(normed, wg_full, preferred_element_type=jnp.float32)  11.3 us
    dot_general x1, matrix products, shards(): up_acc = jnp.dot(normed, wu_full, preferred_element_type=jnp.float32)  9.55 us
    convert_element_type x1, other arithmetic, normalize(): return (state * scale_row * gain_row).astype(jnp.bfloat16)  5.58 us
    dot_general x1, matrix products, shards(): jnp.dot(attended, w_out, preferred_element_type=jnp.float32)  4.71 us
    reduce_sum x1, other arithmetic, normalize(): scale_row = lax.rsqrt(jnp.mean(state * state, axis=-1, keepdims=True) + EPS)  4.46 us

profile of v8, /device:TPU:0, one launch (start us, length us, event | category | flops | bytes accessed | tf_op | source)
XLA Modules:
  0.0 168.9 jit_solution(15682441302845210934)
XLA Ops:
  0.6 0.9 fusion.41
  1.6 0.2 reduce-window.4
  1.8 0.7 subtract_clamp_fusion
  2.6 0.5 multiply_cosine_fusion.1
  3.2 1.2 copy.33
  4.3 0.8 convert_add_fusion.1
  5.3 0.9 add_bitcast_fusion
  6.2 1.2 fusion.28
  7.5 0.2 fusion.18
  7.7 0.8 fusion
  8.5 0.7 fusion.3
  9.3 1.2 fusion.13
  10.5 0.9 copy-done.4
  11.4 4.7 %convolution_convert_fusion = bf16[512,5120]{1,0:T(8,128)(2,1)} fusion(bf16[512,384]{0,1:T(8,128)(2,1)S(1)} %bitcast.86, bf16[384,5120]{1,0:T(8,128)(2,1)S(1)} %copy-done.4), kind=kOutput, calls=%fused_computation.4 | convolution fusion | flops 2015887360 | bytes 9568256 | tf_op jit(solution)/shard_map/dot_general | solution.py:349
  16.3 0.2 iota_compare_fusion.1
  16.8 2.3 %convert_reduce_fusion = s32[16,128,512]{2,1,0:T(8,128)S(1)} fusion(pred[4,128,512]{2,1,0:T(8,128)(4,1)S(1)} %iota_compare_fusion.1, pred[16,4,128]{2,1,0:T(4,128)(4,1)S(1)} %broadcast_and_fusion), kind=kLoop, calls=%fused_computation | loop fusion | flops 11534336 | bytes 4464640 | tf_op jit(solution)/shard_map/reduce_sum | solution.py:340
  19.3 0.7 fusion.10.kv_ref
  20.3 116.1 %shard_map.149 = (bf16[4,4,320,864]{3,2,1,0:T(8,128)(2,1)}, bf16[4,4,320,864]{3,2,1,0:T(8,128)(2,1)}, bf16[16,128,256]{2,1,0:T(8,128)(2,1)S(1)}, bf16[4,2,64,5120]{3,2,1,0:T(8,128)(2,1)}) custom-call(bf16[320,864]{1,0:T(8,128)(2,1)S(1)} %copy-done, bf16[320,864]{1,0:T(8,128)(2,1)S(1)} %copy-done.1, bf16[16,128,256]{2,1,0:T(8,128)(2,1)S(1)} %fusion.10.kv_ref, ...), custom_call_target="tpu_custom_call" | custom-call | tf_op jit(solution)/shard_map/pallas_call | solution.py:235
  136.4 4.5 %multiply_reduce_fusion = f32[512]{0:T(512)S(1)} fusion(bf16[512,5120]{1,0:T(8,128)(2,1)S(1)} %bitcast.81, bf16[4,2,64,5120]{3,2,1,0:T(8,128)(2,1)} %get-tuple-element.6), kind=kLoop, calls=%fused_computation.3 | loop fusion | flops 13106688 | bytes 10487808 | tf_op jit(solution)/shard_map/reduce_sum | solution.py:259
  140.9 5.6 %multiply_convert_fusion = bf16[512,5120]{1,0:T(8,128)(2,1)} fusion(bf16[512,5120]{1,0:T(8,128)(2,1)S(1)} %bitcast.81, bf16[4,2,64,5120]{3,2,1,0:T(8,128)(2,1)S(1)} %copy-done.2, f32[5120]{0:T(1024)S(1)} %copy-done.7, f32[512]{0:T(512)S(1)} %add_rsqrt_fusion), kind=kLoop, calls=%fused_computation.2 | loop fusion | flops 15728640 | bytes 15751168 | tf_op jit(solution)/shard_map/convert_element_type | solution.py:260
  146.5 11.3 %fusion.51 = f32[512,864]{0,1:T(8,128)S(1)} fusion(bf16[512,5120]{1,0:T(8,128)(2,1)} %multiply_convert_fusion, bf16[5120,864]{1,0:T(8,128)(2,1)} %bitcast.90), kind=kOutput, calls=%fused_computation.92 | convolution fusion | flops 4529848320 | bytes 15859712 | tf_op jit(solution)/shard_map/dot_general | solution.py:361
  157.9 9.5 %multiply_convert_fusion.1 = bf16[512,864]{0,1:T(8,128)(2,1)} fusion(f32[512,864]{0,1:T(8,128)S(1)} %fusion.51, bf16[512,5120]{1,0:T(8,128)(2,1)S(1)} %copy-done.3, bf16[5120,864]{1,0:T(8,128)(2,1)} %bitcast.89), kind=kOutput, calls=%fused_computation.14 | convolution fusion | flops 4532502528 | bytes 16744448 | tf_op jit(solution)/shard_map/dot_general | solution.py:362
  167.5 0.7 fusion.16
  168.2 0.7 copy.38
  (42 shorter events, 1.4 us)
Async XLA Ops:
  0.6 6.8 %copy-start.6 = (s32[512]{0:T(512)S(1)}, s32[512]{0:T(512)}, u32[]{:S(2)}) copy-start(s32[512]{0:T(512)} %param.20) | copy-start | bytes 6148
  7.7 1.5 copy-start.5
  7.7 1.5 copy-start.9
  9.3 2.1 %copy-start.4 = (bf16[384,5120]{1,0:T(8,128)(2,1)S(1)}, bf16[384,5120]{1,0:T(8,128)(2,1)}, u32[]{:S(2)}) copy-start(bf16[384,5120]{1,0:T(8,128)(2,1)} %param.23) | copy-start | bytes 11796484
  16.7 119.7 %slice-start = ((s8[5242880]{0:T(1024)(128)(4,1)}), s8[4194304]{0:T(1024)(128)(4,1)S(1)}, s32[]{:S(2)}) async-start(s8[5242880]{0:T(1024)(128)(4,1)} %bitcast.80), calls=%async_computation | async-start | bytes 8388608
  19.1 1.1 copy-start
  19.1 1.2 copy-start.1
  19.2 117.2 %slice-start.1 = ((s8[5242880]{0:T(1024)(128)(4,1)}), s8[1048576]{0:T(1024)(128)(4,1)S(1)}, s32[]{:S(2)}) async-start(s8[5242880]{0:T(1024)(128)(4,1)} %bitcast.80), calls=%async_computation.1 | async-start | bytes 2097152
  136.4 4.5 %copy-start.2 = (bf16[4,2,64,5120]{3,2,1,0:T(8,128)(2,1)S(1)}, bf16[4,2,64,5120]{3,2,1,0:T(8,128)(2,1)}, u32[]{:S(2)}) copy-start(bf16[4,2,64,5120]{3,2,1,0:T(8,128)(2,1)} %get-tuple-element.6) | copy-start | bytes 15728644
  136.4 4.5 %copy-start.7 = (f32[5120]{0:T(1024)S(1)}, f32[5120]{0:T(1024)}, u32[]{:S(2)}) copy-start(f32[5120]{0:T(1024)} %param.25) | copy-start | bytes 61444
  146.5 11.3 %copy-start.3 = (bf16[512,5120]{1,0:T(8,128)(2,1)S(1)}, bf16[512,5120]{1,0:T(8,128)(2,1)}, u32[]{:S(2)}) copy-start(bf16[512,5120]{1,0:T(8,128)(2,1)} %multiply_convert_fusion) | copy-start | bytes 15728644
  157.8 9.6 %copy-start.8 = (s32[16,4]{0,1:T(4,128)S(1)}, s32[16,4]{0,1:T(4,128)}, u32[]{:S(2)}) copy-start(s32[16,4]{0,1:T(4,128)} %param.22) | copy-start | bytes 772

commit v9 on v8

--- a/solution.py
+++ b/solution.py
@@ -34,8 +34,9 @@
 
 
 def gather_kernel(
-    wg_ref, wu_ref, kv_ref, prod_ref, g_ref, u_ref, kv_out, sum_ref,
+    wg_ref, wu_ref, kv_ref, prod_ref, res_ref, gain_ref, g_ref, u_ref, kv_out, sum_ref,
     send_sems, recv_sems, local_sems, ar_send, ar_recv, a_buf, p_buf, b_src, b_buf, m_buf,
+    r_buf, gain_buf,
 ):
     me = lax.axis_index("req")
     col = lax.axis_index("mp")
@@ -85,6 +86,10 @@
     ar_a = ar_copy(0, prod_ref.at[:, 1 - cc], a_buf, core_peer)
     p_load = pltpu.make_async_copy(prod_ref.at[:, cc], p_buf, local_sems.at[3])
     p_load.start()
+    r_load = pltpu.make_async_copy(res_ref.at[cx, cc], r_buf, local_sems.at[5])
+    r_load.start()
+    g_load = pltpu.make_async_copy(gain_ref, gain_buf, local_sems.at[6])
+    g_load.start()
     width = AR_TILE
     tiles = a_buf.shape[-1] // width
 
@@ -171,15 +176,28 @@
     for c in ar_b:
         c.wait_recv()
 
-    def add_chips(t, carry):
+    r_load.wait()
+    g_load.wait()
+
+    def add_chips(t, squares):
         cols = pl.ds(pl.multiple_of(t * width, width), width)
         acc = b_src[cx, :, cols]
         for d in range(1, xs):
             acc = acc + b_buf[(cx + d) % xs, :, cols]
-        m_buf[:, cols] = acc.astype(m_buf.dtype)
+        state = acc + r_buf[:, cols].astype(jnp.float32)
+        b_src[cx, :, cols] = state
+        return squares + jnp.sum(state * state, axis=1, keepdims=True)
+
+    squares = lax.fori_loop(0, tiles, add_chips, jnp.zeros((m_buf.shape[0], 1), jnp.float32))
+    scale = lax.rsqrt(squares / m_buf.shape[1] + EPS)
+
+    def scale_rows(t, carry):
+        cols = pl.ds(pl.multiple_of(t * width, width), width)
+        normed = b_src[cx, :, cols] * scale * gain_buf[:, cols]
+        m_buf[:, cols] = normed.astype(m_buf.dtype)
         return carry
 
-    lax.fori_loop(0, tiles, add_chips, 0)
+    lax.fori_loop(0, tiles, scale_rows, 0)
     own_sum = pltpu.make_async_copy(m_buf, sum_ref.at[cx, cc], local_sems.at[4])
     own_sum.start()
     own_sum.wait()
@@ -224,7 +242,7 @@
     own_kv.wait()
 
 
-def gather_weights(w_gate, w_up, kv_send, product):
+def gather_weights(w_gate, w_up, kv_send, product, residual, gain):
     rows, cols = w_gate.shape
     xs, _, chunk, width = product.shape
     any_spec = pl.BlockSpec(memory_space=pl.ANY)
@@ -235,12 +253,12 @@
     return pl.pallas_call(
         gather_kernel,
         out_shape=(piece, piece, slots, sums),
-        in_specs=[any_spec, any_spec, any_spec, any_spec],
+        in_specs=[any_spec] * 6,
         out_specs=(any_spec, any_spec, any_spec, any_spec),
         scratch_shapes=[
             pltpu.SemaphoreType.DMA((sems,)),
             pltpu.SemaphoreType.DMA((sems,)),
-            pltpu.SemaphoreType.DMA((5,)),
+            pltpu.SemaphoreType.DMA((7,)),
             pltpu.SemaphoreType.DMA((2 * xs,)),
             pltpu.SemaphoreType.DMA((2 * xs,)),
             pltpu.VMEM((xs, chunk, width), product.dtype),
@@ -248,11 +266,13 @@
             pltpu.VMEM((xs, chunk, width), jnp.float32),
             pltpu.VMEM((xs, chunk, width), jnp.float32),
             pltpu.VMEM((chunk, width), product.dtype),
+            pltpu.VMEM((chunk, width), residual.dtype),
+            pltpu.VMEM((1, width), jnp.float32),
         ],
         compiler_params=pltpu.CompilerParams(
             collective_id=0, has_side_effects=True, vmem_limit_bytes=48 * 1024 * 1024
         ),
-    )(w_gate, w_up, kv_send, product)
+    )(w_gate, w_up, kv_send, product, residual, gain)
 
 def normalize(resid_rows, summed, gain_row):
     state = resid_rows.astype(jnp.float32) + summed
@@ -349,9 +369,15 @@
     product = jnp.dot(attended, w_out, preferred_element_type=jnp.float32).astype(jnp.bfloat16)
     n_mp = lax.axis_size("mp")
     product = product.reshape(n_mp // 2, 2, block_rows // n_mp, product.shape[-1])
-    g_full, u_full, kv_in, summed = gather_weights(w_gate, w_up, kv_send, product)
-    summed = summed.reshape(block_rows, -1).astype(jnp.float32)
-    normed = normalize(residual, summed, norm_gain)
+    g_full, u_full, kv_in, normed = gather_weights(
+        w_gate,
+        w_up,
+        kv_send,
+        product,
+        residual.reshape(product.shape),
+        norm_gain.reshape(1, -1).astype(jnp.float32),
+    )
+    normed = normed.reshape(block_rows, -1)
     kv_in = kv_in.reshape(groups_all, PAGE, kv_heads, 2 * HD)
     cache_out = jnp.einsum(
         "ls,sphc->lhpc", page_select, kv_in, preferred_element_type=jnp.float32

time: 169 us -> 158 us (0.935)
  other arithmetic: 19.6 us -> 8.75 us
    convert_element_type x1 -> x0, other arithmetic: 5.58 us -> none  [normalize(): return (state * scale_row * gain_row).astype(jnp.bfloat16)]
    reduce_sum x1 -> x0, other arithmetic: 4.46 us -> none  [normalize(): scale_row = lax.rsqrt(jnp.mean(state * state, axis=-1, keepdims=True) + EPS)]
where the time goes in v9:
time: 158 us
  Pallas kernels  116 us (73%)
  matrix products  28.9 us (18%)
  other arithmetic  8.75 us (6%)
  local copies, waits for them, and re-layouts  3.33 us (2%)
    pallas_call x1, Pallas kernels, gather_weights(): pl.pallas_call(gather_kernel, out_shape=(piece, piece, slots, sums), in_s...  116 us
    dot_general x1, matrix products, shards(): gate_acc = jnp.dot(normed, wg_full, preferred_element_type=jnp.float32)  11.3 us
    dot_general x1, matrix products, shards(): up_acc = jnp.dot(normed, wu_full, preferred_element_type=jnp.float32)  9.55 us
    dot_general x1, matrix products, shards(): jnp.dot(attended, w_out, preferred_element_type=jnp.float32)  4.7 us
    unnamed x25, local copies, waits for them, and re-layouts  3.33 us

profile of v9, /device:TPU:0, one launch (start us, length us, event | category | flops | bytes accessed | tf_op | source)
XLA Modules:
  0.0 158.1 jit_solution(3964786987756095001)
XLA Ops:
  0.7 0.9 fusion.41
  1.7 0.2 reduce-window.4
  1.9 0.7 subtract_clamp_fusion
  2.7 0.5 multiply_cosine_fusion.1
  3.2 1.2 copy.33
  4.4 0.8 convert_add_fusion
  5.4 1.2 fusion.28
  6.7 0.2 fusion.18
  6.9 0.8 fusion
  7.7 0.7 fusion.3
  8.5 1.2 fusion.13
  9.7 0.9 copy-done.3
  10.6 4.7 %convolution_convert_fusion = bf16[512,5120]{1,0:T(8,128)(2,1)} fusion(bf16[512,384]{0,1:T(8,128)(2,1)S(1)} %bitcast.85, bf16[384,5120]{1,0:T(8,128)(2,1)S(1)} %copy-done.3), kind=kOutput, calls=%fused_computation.1 | convolution fusion | flops 2015887360 | bytes 9568256 | tf_op jit(solution)/shard_map/dot_general | solution.py:369
  15.3 0.2 fusion.30
  15.5 0.2 iota_compare_fusion.1
  15.9 2.3 %convert_reduce_fusion = s32[16,128,512]{2,1,0:T(8,128)S(1)} fusion(pred[4,128,512]{2,1,0:T(8,128)(4,1)S(1)} %iota_compare_fusion.1, pred[16,4,128]{2,1,0:T(4,128)(4,1)S(1)} %broadcast_and_fusion), kind=kLoop, calls=%fused_computation | loop fusion | flops 11534336 | bytes 4464640 | tf_op jit(solution)/shard_map/reduce_sum | solution.py:360
  18.4 0.7 fusion.10.kv_ref
  19.1 0.2 copy-done
  19.3 0.2 copy-done.1
  19.5 116.2 %shard_map.149 = (bf16[4,4,320,864]{3,2,1,0:T(8,128)(2,1)}, bf16[4,4,320,864]{3,2,1,0:T(8,128)(2,1)}, bf16[16,128,256]{2,1,0:T(8,128)(2,1)S(1)}, bf16[4,2,64,5120]{3,2,1,0:T(8,128)(2,1)}) custom-call(bf16[320,864]{1,0:T(8,128)(2,1)S(1)} %copy-done, bf16[320,864]{1,0:T(8,128)(2,1)S(1)} %copy-done.1, bf16[16,128,256]{2,1,0:T(8,128)(2,1)S(1)} %fusion.10.kv_ref, ...), custom_call_target="tpu_custom_call" | custom-call | tf_op jit(solution)/shard_map/pallas_call | solution.py:253
  135.7 11.3 %fusion.51 = f32[512,864]{0,1:T(8,128)S(1)} fusion(bf16[512,5120]{1,0:T(8,128)(2,1)} %bitcast.90, bf16[5120,864]{1,0:T(8,128)(2,1)} %bitcast.89), kind=kOutput, calls=%fused_computation.88 | convolution fusion | flops 4529848320 | bytes 15859712 | tf_op jit(solution)/shard_map/dot_general | solution.py:387
  147.0 9.5 %multiply_convert_fusion = bf16[512,864]{0,1:T(8,128)(2,1)} fusion(f32[512,864]{0,1:T(8,128)S(1)} %fusion.51, bf16[512,5120]{1,0:T(8,128)(2,1)S(1)} %bitcast.91, bf16[5120,864]{1,0:T(8,128)(2,1)} %bitcast.88), kind=kOutput, calls=%fused_computation.11 | convolution fusion | flops 4532502528 | bytes 16744448 | tf_op jit(solution)/shard_map/dot_general | solution.py:388
  156.7 0.7 fusion.16
  157.4 0.7 copy.38
  (36 shorter events, 0.9 us)
Async XLA Ops:
  0.6 6.0 %copy-start.6 = (s32[512]{0:T(512)S(1)}, s32[512]{0:T(512)}, u32[]{:S(2)}) copy-start(s32[512]{0:T(512)} %param.20) | copy-start | bytes 6148
  0.6 4.7 %copy-start.4 = (bf16[512,128]{1,0:T(8,128)(2,1)S(1)}, bf16[512,128]{1,0:T(8,128)(2,1)}, u32[]{:S(2)}) copy-start(bf16[512,128]{1,0:T(8,128)(2,1)} %param.15) | copy-start | bytes 393220
  0.7 4.7 %copy-start.8 = (f32[128]{0:T(128)S(1)}, f32[128]{0:T(128)}, u32[]{:S(2)}) copy-start(f32[128]{0:T(128)} %param.18) | copy-start | bytes 1540
  6.9 1.5 copy-start.5
  6.9 1.5 copy-start.9
  8.5 2.1 %copy-start.3 = (bf16[384,5120]{1,0:T(8,128)(2,1)S(1)}, bf16[384,5120]{1,0:T(8,128)(2,1)}, u32[]{:S(2)}) copy-start(bf16[384,5120]{1,0:T(8,128)(2,1)} %param.23) | copy-start | bytes 11796484
  18.3 1.1 copy-start
  18.3 1.3 copy-start.1
  18.3 1.2 copy-start.2
  135.7 11.3 %copy-start.10 = (bf16[4,2,64,5120]{3,2,1,0:T(8,128)(2,1)S(1)}, bf16[4,2,64,5120]{3,2,1,0:T(8,128)(2,1)}, u32[]{:S(2)}) copy-start(bf16[4,2,64,5120]{3,2,1,0:T(8,128)(2,1)} %get-tuple-element.6) | copy-start | bytes 15728644
  147.0 9.6 %copy-start.7 = (s32[16,4]{0,1:T(4,128)S(1)}, s32[16,4]{0,1:T(4,128)}, u32[]{:S(2)}) copy-start(s32[16,4]{0,1:T(4,128)} %param.22) | copy-start | bytes 772

commit v10 on v9

--- a/solution.py
+++ b/solution.py
@@ -94,6 +94,33 @@
     tiles = a_buf.shape[-1] // width
 
     copies = []
+
+    def send(src, dst, peer):
+        k = len(copies)
+        c = pltpu.make_async_remote_copy(
+            src_ref=src,
+            dst_ref=dst,
+            send_sem=send_sems.at[k],
+            recv_sem=recv_sems.at[k],
+            device_id=peer,
+            device_id_type=mesh_id,
+        )
+        c.start()
+        copies.append(c)
+        return c
+
+    own_g = pltpu.make_async_copy(wg_ref, g_ref.at[z, y], local_sems.at[0])
+    own_u = pltpu.make_async_copy(wu_ref, u_ref.at[z, y], local_sems.at[1])
+    own_g.start()
+    own_u.start()
+
+    g_from_ym = send(wg_ref, g_ref.at[z, y], to(z, yp))
+    g_from_yp = send(wg_ref, g_ref.at[z, y], to(z, ym))
+    u_from_zm = send(wu_ref, u_ref.at[z, y], to(zp, y))
+    u_from_zp = send(wu_ref, u_ref.at[z, y], to(zm, y))
+    gz = {"y": (send(wg_ref, g_ref.at[z, y], to(zp, y)), send(wg_ref, g_ref.at[z, y], to(zm, y)))}
+    uy = {"z": (send(wu_ref, u_ref.at[z, y], to(z, yp)), send(wu_ref, u_ref.at[z, y], to(z, ym)))}
+    kv_copies = []
     own_kv = pltpu.make_async_copy(kv_ref.at[me], kv_out.at[me], local_sems.at[2])
     own_kv.start()
     for d in range(1, groups):
@@ -107,35 +134,7 @@
             device_id_type=mesh_id,
         )
         c.start()
-        copies.append(c)
-    kv_copies = list(copies)
-    copies.clear()
-
-    def send(src, dst, peer):
-        k = len(copies)
-        c = pltpu.make_async_remote_copy(
-            src_ref=src,
-            dst_ref=dst,
-            send_sem=send_sems.at[k],
-            recv_sem=recv_sems.at[k],
-            device_id=peer,
-            device_id_type=mesh_id,
-        )
-        c.start()
-        copies.append(c)
-        return c
-
-    own_g = pltpu.make_async_copy(wg_ref, g_ref.at[z, y], local_sems.at[0])
-    own_u = pltpu.make_async_copy(wu_ref, u_ref.at[z, y], local_sems.at[1])
-    own_g.start()
-    own_u.start()
-
-    g_from_ym = send(wg_ref, g_ref.at[z, y], to(z, yp))
-    g_from_yp = send(wg_ref, g_ref.at[z, y], to(z, ym))
-    u_from_zm = send(wu_ref, u_ref.at[z, y], to(zp, y))
-    u_from_zp = send(wu_ref, u_ref.at[z, y], to(zm, y))
-    gz = {"y": (send(wg_ref, g_ref.at[z, y], to(zp, y)), send(wg_ref, g_ref.at[z, y], to(zm, y)))}
-    uy = {"z": (send(wu_ref, u_ref.at[z, y], to(z, yp)), send(wu_ref, u_ref.at[z, y], to(z, ym)))}
+        kv_copies.append(c)
 
     ar_a.wait_recv()
     p_load.wait()
@@ -351,15 +350,13 @@
     slot = jnp.arange(PAGE, dtype=jnp.int32)
     source = starts[:, None] + slot[None, :]
     live_slot = slot[None, :] < own_lens[:, None]
-    owner_hit = own_owner[None, :] == jnp.arange(groups_all)[:, None]
-    picks = (
-        owner_hit[:, :, None, None]
-        & live_slot[None, :, :, None]
-        & (source[None, :, :, None] == token[None, None, None, :])
-    )
-    select = jnp.sum(picks.astype(jnp.int32), axis=1).astype(jnp.bfloat16)
+    select = (live_slot[:, :, None] & (source[:, :, None] == token[None, None, :])).astype(
+        jnp.bfloat16
+    )
+    pages = jnp.einsum("jst,tc->jsc", select, kv_rows, preferred_element_type=jnp.float32)
+    to_owner = (own_owner[None, :] == jnp.arange(groups_all)[:, None]).astype(jnp.bfloat16)
     kv_send = jnp.einsum(
-        "gst,tc->gsc", select, kv_rows, preferred_element_type=jnp.float32
+        "gj,jsc->gsc", to_owner, pages.astype(jnp.bfloat16), preferred_element_type=jnp.float32
     ).astype(jnp.bfloat16)
     hits = (
         page_table[None, :, :] == (me_req * REQS + jnp.arange(REQS, dtype=jnp.int32))[:, None, None]

time: 158 us -> 155 us (0.981)
  other arithmetic: 8.75 us -> 6.12 us
    reduce_sum x1 -> x0, other arithmetic: 2.31 us -> none  [shards(): select = jnp.sum(picks.astype(jnp.int32), axis=1).astype(jnp.bfloat16)]
where the time goes in v10:
time: 155 us
  Pallas kernels  116 us (75%)
  matrix products  29.2 us (19%)
  other arithmetic  6.12 us (4%)
  local copies, waits for them, and re-layouts  3.3 us (2%)
    pallas_call x1, Pallas kernels, gather_weights(): pl.pallas_call(gather_kernel, out_shape=(piece, piece, slots, sums), in_s...  116 us
    dot_general x1, matrix products, shards(): gate_acc = jnp.dot(normed, wg_full, preferred_element_type=jnp.float32)  11.3 us
    dot_general x1, matrix products, shards(): up_acc = jnp.dot(normed, wu_full, preferred_element_type=jnp.float32)  9.54 us
    dot_general x1, matrix products, shards(): jnp.dot(attended, w_out, preferred_element_type=jnp.float32)  4.71 us

profile of v10, /device:TPU:0, one launch (start us, length us, event | category | flops | bytes accessed | tf_op | source)
XLA Modules:
  0.0 155.2 jit_solution(12588206874310217778)
XLA Ops:
  0.7 0.9 fusion.42
  1.7 0.2 reduce-window.4
  1.9 0.7 subtract_clamp_fusion
  2.7 0.5 multiply_cosine_fusion.1
  3.2 1.2 copy.37
  4.4 0.8 convert_add_fusion
  5.2 0.1 multiply_subtract_fusion
  5.4 1.2 fusion.27
  6.7 0.2 fusion.15
  6.9 0.8 fusion
  7.7 0.7 fusion.3
  8.5 1.2 fusion.8
  9.7 0.9 copy-done.3
  10.6 4.7 %convolution_convert_fusion = bf16[512,5120]{1,0:T(8,128)(2,1)} fusion(bf16[512,384]{0,1:T(8,128)(2,1)S(1)} %bitcast.88, bf16[384,5120]{1,0:T(8,128)(2,1)S(1)} %copy-done.3), kind=kOutput, calls=%fused_computation | convolution fusion | flops 2015887360 | bytes 9568256 | tf_op jit(solution)/shard_map/dot_general | solution.py:366
  15.3 0.2 fusion.29
  15.6 0.1 fusion.40
  15.8 0.4 convolution_convert_fusion.2
  16.1 0.6 fusion.33
  16.7 0.4 copy.53.kv_ref
  17.1 115.7 %shard_map.149 = (bf16[4,4,320,864]{3,2,1,0:T(8,128)(2,1)}, bf16[4,4,320,864]{3,2,1,0:T(8,128)(2,1)}, bf16[16,128,256]{2,1,0:T(8,128)(2,1)S(1)}, bf16[4,2,64,5120]{3,2,1,0:T(8,128)(2,1)}) custom-call(bf16[320,864]{1,0:T(8,128)(2,1)S(1)} %copy-done, bf16[320,864]{1,0:T(8,128)(2,1)S(1)} %copy-done.1, bf16[16,128,256]{2,1,0:T(8,128)(2,1)S(1)} %copy.53.kv_ref, ...), custom_call_target="tpu_custom_call" | custom-call | tf_op jit(solution)/shard_map/pallas_call | solution.py:252
  132.9 11.3 %fusion.55 = f32[512,864]{0,1:T(8,128)S(1)} fusion(bf16[512,5120]{1,0:T(8,128)(2,1)} %bitcast.93, bf16[5120,864]{1,0:T(8,128)(2,1)} %bitcast.92), kind=kOutput, calls=%fused_computation.92 | convolution fusion | flops 4529848320 | bytes 15859712 | tf_op jit(solution)/shard_map/dot_general | solution.py:384
  144.2 9.5 %multiply_convert_fusion = bf16[512,864]{0,1:T(8,128)(2,1)} fusion(f32[512,864]{0,1:T(8,128)S(1)} %fusion.55, bf16[512,5120]{1,0:T(8,128)(2,1)S(1)} %bitcast.94, bf16[5120,864]{1,0:T(8,128)(2,1)} %bitcast.91), kind=kOutput, calls=%fused_computation.9 | convolution fusion | flops 4532502528 | bytes 16744448 | tf_op jit(solution)/shard_map/dot_general | solution.py:385
  153.8 0.7 fusion.11
  154.5 0.7 copy.42
  (34 shorter events, 0.5 us)
Async XLA Ops:
  0.6 6.0 %copy-start.6 = (s32[512]{0:T(512)S(1)}, s32[512]{0:T(512)}, u32[]{:S(2)}) copy-start(s32[512]{0:T(512)} %param.20) | copy-start | bytes 6148
  0.6 4.7 %copy-start.4 = (bf16[512,128]{1,0:T(8,128)(2,1)S(1)}, bf16[512,128]{1,0:T(8,128)(2,1)}, u32[]{:S(2)}) copy-start(bf16[512,128]{1,0:T(8,128)(2,1)} %param.15) | copy-start | bytes 393220
  0.7 4.7 %copy-start.8 = (f32[128]{0:T(128)S(1)}, f32[128]{0:T(128)}, u32[]{:S(2)}) copy-start(f32[128]{0:T(128)} %param.18) | copy-start | bytes 1540
  6.9 1.5 copy-start.5
  6.9 1.5 copy-start.9
  8.4 2.1 %copy-start.3 = (bf16[384,5120]{1,0:T(8,128)(2,1)S(1)}, bf16[384,5120]{1,0:T(8,128)(2,1)}, u32[]{:S(2)}) copy-start(bf16[384,5120]{1,0:T(8,128)(2,1)} %param.23) | copy-start | bytes 11796484
  15.3 1.8 %copy-start = (bf16[320,864]{1,0:T(8,128)(2,1)S(1)}, bf16[320,864]{1,0:T(8,128)(2,1)}, u32[]{:S(2)}) copy-start(bf16[320,864]{1,0:T(8,128)(2,1)} %wg_ref.1) | copy-start | bytes 1658884
  15.3 1.8 %copy-start.1 = (bf16[320,864]{1,0:T(8,128)(2,1)S(1)}, bf16[320,864]{1,0:T(8,128)(2,1)}, u32[]{:S(2)}) copy-start(bf16[320,864]{1,0:T(8,128)(2,1)} %wu_ref.1) | copy-start | bytes 1658884
  15.3 1.8 %copy-start.2 = (f32[5120]{0:T(1024)S(1)}, f32[5120]{0:T(1024)}, u32[]{:S(2)}) copy-start(f32[5120]{0:T(1024)} %param.25) | copy-start | bytes 61444
  132.9 11.3 %copy-start.10 = (bf16[4,2,64,5120]{3,2,1,0:T(8,128)(2,1)S(1)}, bf16[4,2,64,5120]{3,2,1,0:T(8,128)(2,1)}, u32[]{:S(2)}) copy-start(bf16[4,2,64,5120]{3,2,1,0:T(8,128)(2,1)} %get-tuple-element.6) | copy-start | bytes 15728644
  144.2 9.6 %copy-start.7 = (s32[16,4]{0,1:T(4,128)S(1)}, s32[16,4]{0,1:T(4,128)}, u32[]{:S(2)}) copy-start(s32[16,4]{0,1:T(4,128)} %param.22) | copy-start | bytes 772

commit v11 on v10

--- a/solution.py
+++ b/solution.py
@@ -205,16 +205,18 @@
         for d in range(1, xs)
     ]
 
-    for key, yy in (("y", y), ("ym", ym), ("yp", yp), ("y2", y2)):
-        from_zm, from_zp = gz[key]
+    for (gkey, yy), (ukey, zz) in zip(
+        (("y", y), ("ym", ym), ("yp", yp), ("y2", y2)),
+        (("z", z), ("zm", zm), ("zp", zp), ("z2", z2)),
+    ):
+        from_zm, from_zp = gz[gkey]
+        from_ym, from_yp = uy[ukey]
         from_zm.wait_recv()
         send(g_ref.at[zm, yy, low], g_ref.at[zm, yy, low], to(zp, y))
+        from_ym.wait_recv()
+        send(u_ref.at[zz, ym, low], u_ref.at[zz, ym, low], to(z, yp))
         from_zp.wait_recv()
         send(g_ref.at[zp, yy, high], g_ref.at[zp, yy, high], to(zm, y))
-    for key, zz in (("z", z), ("zm", zm), ("zp", zp), ("z2", z2)):
-        from_ym, from_yp = uy[key]
-        from_ym.wait_recv()
-        send(u_ref.at[zz, ym, low], u_ref.at[zz, ym, low], to(z, yp))
         from_yp.wait_recv()
         send(u_ref.at[zz, yp, high], u_ref.at[zz, yp, high], to(z, ym))
 

time: 155 us -> 155 us (level)
  Pallas kernels: 116 us -> 114 us
where the time goes in v11:
time: 155 us; the launch traced here: 154 us
  Pallas kernels  114 us (74%)
  matrix products  29.1 us (19%)
  other arithmetic  6.12 us (4%)
  local copies, waits for them, and re-layouts  3.3 us (2%)
    pallas_call x1, Pallas kernels, gather_weights(): pl.pallas_call(gather_kernel, out_shape=(piece, piece, slots, sums), in_s...  114 us
    dot_general x1, matrix products, shards(): gate_acc = jnp.dot(normed, wg_full, preferred_element_type=jnp.float32)  11.3 us
    dot_general x1, matrix products, shards(): up_acc = jnp.dot(normed, wu_full, preferred_element_type=jnp.float32)  9.54 us
    dot_general x1, matrix products, shards(): jnp.dot(attended, w_out, preferred_element_type=jnp.float32)  4.71 us

profile of v11, /device:TPU:0, one launch (start us, length us, event | category | flops | bytes accessed | tf_op | source)
XLA Modules:
  0.0 153.9 jit_solution(16310310187381576308)
XLA Ops:
  0.7 0.9 fusion.42
  1.7 0.2 reduce-window.4
  1.9 0.7 subtract_clamp_fusion
  2.7 0.5 multiply_cosine_fusion.1
  3.2 1.2 copy.37
  4.4 0.8 convert_add_fusion
  5.2 0.1 multiply_subtract_fusion
  5.4 1.2 fusion.27
  6.7 0.2 fusion.15
  6.9 0.8 fusion
  7.7 0.7 fusion.3
  8.5 1.2 fusion.8
  9.7 0.9 copy-done.3
  10.6 4.7 %convolution_convert_fusion = bf16[512,5120]{1,0:T(8,128)(2,1)} fusion(bf16[512,384]{0,1:T(8,128)(2,1)S(1)} %bitcast.88, bf16[384,5120]{1,0:T(8,128)(2,1)S(1)} %copy-done.3), kind=kOutput, calls=%fused_computation | convolution fusion | flops 2015887360 | bytes 9568256 | tf_op jit(solution)/shard_map/dot_general | solution.py:368
  15.3 0.2 fusion.29
  15.6 0.1 fusion.40
  15.8 0.4 convolution_convert_fusion.2
  16.1 0.6 fusion.33
  16.7 0.4 copy.53.kv_ref
  17.1 114.4 %shard_map.149 = (bf16[4,4,320,864]{3,2,1,0:T(8,128)(2,1)}, bf16[4,4,320,864]{3,2,1,0:T(8,128)(2,1)}, bf16[16,128,256]{2,1,0:T(8,128)(2,1)S(1)}, bf16[4,2,64,5120]{3,2,1,0:T(8,128)(2,1)}) custom-call(bf16[320,864]{1,0:T(8,128)(2,1)S(1)} %copy-done, bf16[320,864]{1,0:T(8,128)(2,1)S(1)} %copy-done.1, bf16[16,128,256]{2,1,0:T(8,128)(2,1)S(1)} %copy.53.kv_ref, ...), custom_call_target="tpu_custom_call" | custom-call | tf_op jit(solution)/shard_map/pallas_call | solution.py:254
  131.5 11.3 %fusion.55 = f32[512,864]{0,1:T(8,128)S(1)} fusion(bf16[512,5120]{1,0:T(8,128)(2,1)} %bitcast.93, bf16[5120,864]{1,0:T(8,128)(2,1)} %bitcast.92), kind=kOutput, calls=%fused_computation.92 | convolution fusion | flops 4529848320 | bytes 15859712 | tf_op jit(solution)/shard_map/dot_general | solution.py:386
  142.8 9.5 %multiply_convert_fusion = bf16[512,864]{0,1:T(8,128)(2,1)} fusion(f32[512,864]{0,1:T(8,128)S(1)} %fusion.55, bf16[512,5120]{1,0:T(8,128)(2,1)S(1)} %bitcast.94, bf16[5120,864]{1,0:T(8,128)(2,1)} %bitcast.91), kind=kOutput, calls=%fused_computation.9 | convolution fusion | flops 4532502528 | bytes 16744448 | tf_op jit(solution)/shard_map/dot_general | solution.py:387
  152.5 0.7 fusion.11
  153.2 0.7 copy.42
  (34 shorter events, 0.5 us)
Async XLA Ops:
  0.6 6.0 %copy-start.6 = (s32[512]{0:T(512)S(1)}, s32[512]{0:T(512)}, u32[]{:S(2)}) copy-start(s32[512]{0:T(512)} %param.20) | copy-start | bytes 6148
  0.6 4.7 %copy-start.4 = (bf16[512,128]{1,0:T(8,128)(2,1)S(1)}, bf16[512,128]{1,0:T(8,128)(2,1)}, u32[]{:S(2)}) copy-start(bf16[512,128]{1,0:T(8,128)(2,1)} %param.15) | copy-start | bytes 393220
  0.7 4.7 %copy-start.8 = (f32[128]{0:T(128)S(1)}, f32[128]{0:T(128)}, u32[]{:S(2)}) copy-start(f32[128]{0:T(128)} %param.18) | copy-start | bytes 1540
  6.9 1.5 %copy-start.5 = (bf16[512,128]{1,0:T(8,128)(2,1)S(1)}, bf16[512,128]{1,0:T(8,128)(2,1)}, u32[]{:S(2)}) copy-start(bf16[512,128]{1,0:T(8,128)(2,1)} %param.16) | copy-start | bytes 393220
  6.9 1.5 copy-start.9
  8.4 2.1 %copy-start.3 = (bf16[384,5120]{1,0:T(8,128)(2,1)S(1)}, bf16[384,5120]{1,0:T(8,128)(2,1)}, u32[]{:S(2)}) copy-start(bf16[384,5120]{1,0:T(8,128)(2,1)} %param.23) | copy-start | bytes 11796484
  15.3 1.8 %copy-start = (bf16[320,864]{1,0:T(8,128)(2,1)S(1)}, bf16[320,864]{1,0:T(8,128)(2,1)}, u32[]{:S(2)}) copy-start(bf16[320,864]{1,0:T(8,128)(2,1)} %wg_ref.1) | copy-start | bytes 1658884
  15.3 1.8 %copy-start.1 = (bf16[320,864]{1,0:T(8,128)(2,1)S(1)}, bf16[320,864]{1,0:T(8,128)(2,1)}, u32[]{:S(2)}) copy-start(bf16[320,864]{1,0:T(8,128)(2,1)} %wu_ref.1) | copy-start | bytes 1658884
  15.3 1.8 %copy-start.2 = (f32[5120]{0:T(1024)S(1)}, f32[5120]{0:T(1024)}, u32[]{:S(2)}) copy-start(f32[5120]{0:T(1024)} %param.25) | copy-start | bytes 61444
  131.5 11.3 %copy-start.10 = (bf16[4,2,64,5120]{3,2,1,0:T(8,128)(2,1)S(1)}, bf16[4,2,64,5120]{3,2,1,0:T(8,128)(2,1)}, u32[]{:S(2)}) copy-start(bf16[4,2,64,5120]{3,2,1,0:T(8,128)(2,1)} %get-tuple-element.6) | copy-start | bytes 15728644
  142.8 9.6 %copy-start.7 = (s32[16,4]{0,1:T(4,128)S(1)}, s32[16,4]{0,1:T(4,128)}, u32[]{:S(2)}) copy-start(s32[16,4]{0,1:T(4,128)} %param.22) | copy-start | bytes 772

commit v12 on v11

--- a/solution.py
+++ b/solution.py
@@ -34,8 +34,8 @@
 
 
 def gather_kernel(
-    wg_ref, wu_ref, kv_ref, prod_ref, res_ref, gain_ref, g_ref, u_ref, kv_out, sum_ref,
-    send_sems, recv_sems, local_sems, ar_send, ar_recv, a_buf, p_buf, b_src, b_buf, m_buf,
+    wg_ref, wu_ref, kv_ref, att_ref, wout_ref, res_ref, gain_ref, g_ref, u_ref, kv_out, sum_ref,
+    send_sems, recv_sems, local_sems, ar_send, ar_recv, a_buf, prod_v, b_src, b_buf, m_buf,
     r_buf, gain_buf,
 ):
     me = lax.axis_index("req")
@@ -57,7 +57,7 @@
         return (zz * RING + yy, col)
 
     groups = kv_ref.shape[0]
-    xs = prod_ref.shape[0]
+    xs = prod_v.shape[0]
     cx = col // 2
     cc = col % 2
     core_peer = (me, cx * 2 + 1 - cc)
@@ -83,9 +83,6 @@
         c.start()
         return c
 
-    ar_a = ar_copy(0, prod_ref.at[:, 1 - cc], a_buf, core_peer)
-    p_load = pltpu.make_async_copy(prod_ref.at[:, cc], p_buf, local_sems.at[3])
-    p_load.start()
     r_load = pltpu.make_async_copy(res_ref.at[cx, cc], r_buf, local_sems.at[5])
     r_load.start()
     g_load = pltpu.make_async_copy(gain_ref, gain_buf, local_sems.at[6])
@@ -136,13 +133,23 @@
         c.start()
         kv_copies.append(c)
 
+    chunk = prod_v.shape[2]
+
+    def project(k, carry):
+        rows = att_ref[pl.ds(pl.multiple_of(k * chunk, chunk), chunk), :]
+        part = jnp.dot(rows, wout_ref[...], preferred_element_type=jnp.float32)
+        prod_v[k // 2, k % 2] = part.astype(prod_v.dtype)
+        return carry
+
+    lax.fori_loop(0, 2 * xs, project, 0)
+    ar_a = ar_copy(0, prod_v.at[:, 1 - cc], a_buf, core_peer)
+
     ar_a.wait_recv()
-    p_load.wait()
 
     def add_pair(i, carry):
         xi = i // tiles
         cols = pl.ds(pl.multiple_of((i % tiles) * width, width), width)
-        b_src[xi, :, cols] = p_buf[xi, :, cols].astype(jnp.float32) + a_buf[xi, :, cols].astype(
+        b_src[xi, :, cols] = prod_v[xi, cc, :, cols].astype(jnp.float32) + a_buf[xi, :, cols].astype(
             jnp.float32
         )
         return carry
@@ -243,10 +250,12 @@
     own_kv.wait()
 
 
-def gather_weights(w_gate, w_up, kv_send, product, residual, gain):
+def gather_weights(w_gate, w_up, kv_send, attended, w_out, residual, gain):
     rows, cols = w_gate.shape
-    xs, _, chunk, width = product.shape
+    xs, _, chunk, width = residual.shape
+    product = jax.ShapeDtypeStruct(residual.shape, jnp.bfloat16)
     any_spec = pl.BlockSpec(memory_space=pl.ANY)
+    vmem_spec = pl.BlockSpec(memory_space=pltpu.VMEM)
     piece = jax.ShapeDtypeStruct((RING, RING, rows, cols), w_gate.dtype)
     slots = jax.ShapeDtypeStruct(kv_send.shape, kv_send.dtype)
     sums = jax.ShapeDtypeStruct(product.shape, product.dtype)
@@ -254,7 +263,7 @@
     return pl.pallas_call(
         gather_kernel,
         out_shape=(piece, piece, slots, sums),
-        in_specs=[any_spec] * 6,
+        in_specs=[any_spec] * 3 + [vmem_spec] * 2 + [any_spec] * 2,
         out_specs=(any_spec, any_spec, any_spec, any_spec),
         scratch_shapes=[
             pltpu.SemaphoreType.DMA((sems,)),
@@ -263,7 +272,7 @@
             pltpu.SemaphoreType.DMA((2 * xs,)),
             pltpu.SemaphoreType.DMA((2 * xs,)),
             pltpu.VMEM((xs, chunk, width), product.dtype),
-            pltpu.VMEM((xs, chunk, width), product.dtype),
+            pltpu.VMEM(product.shape, product.dtype),
             pltpu.VMEM((xs, chunk, width), jnp.float32),
             pltpu.VMEM((xs, chunk, width), jnp.float32),
             pltpu.VMEM((chunk, width), product.dtype),
@@ -273,7 +282,7 @@
         compiler_params=pltpu.CompilerParams(
             collective_id=0, has_side_effects=True, vmem_limit_bytes=48 * 1024 * 1024
         ),
-    )(w_gate, w_up, kv_send, product, residual, gain)
+    )(w_gate, w_up, kv_send, attended, w_out, residual, gain)
 
 def normalize(resid_rows, summed, gain_row):
     state = resid_rows.astype(jnp.float32) + summed
@@ -365,15 +374,15 @@
     )
     page_select = jnp.sum(hits.astype(jnp.int32), axis=2).astype(jnp.bfloat16)
 
-    product = jnp.dot(attended, w_out, preferred_element_type=jnp.float32).astype(jnp.bfloat16)
     n_mp = lax.axis_size("mp")
-    product = product.reshape(n_mp // 2, 2, block_rows // n_mp, product.shape[-1])
+    split_rows = (n_mp // 2, 2, block_rows // n_mp, residual.shape[-1])
     g_full, u_full, kv_in, normed = gather_weights(
         w_gate,
         w_up,
         kv_send,
-        product,
-        residual.reshape(product.shape),
+        attended,
+        w_out,
+        residual.reshape(split_rows),
         norm_gain.reshape(1, -1).astype(jnp.float32),
     )
     normed = normed.reshape(block_rows, -1)

time: 155 us -> 156 us (level)
  Pallas kernels: 114 us -> 121 us
  matrix products: 29.1 us -> 24.5 us
    pallas_call x1, Pallas kernels: 114 us -> 121 us  [gather_weights(): pl.pallas_call(gather_kernel, out_shape=(piece, piece, slots, sums), in_s...]
    dot_general x1 -> x0, matrix products: 4.71 us -> none  [shards(): jnp.dot(attended, w_out, preferred_element_type=jnp.float32)]
where the time goes in v12:
time: 156 us; the launch traced here: 155 us
  Pallas kernels  121 us (78%)
  matrix products  24.5 us (16%)
  other arithmetic  6.14 us (4%)
  local copies, waits for them, and re-layouts  2.59 us (2%)
    pallas_call x1, Pallas kernels, gather_weights(): pl.pallas_call(gather_kernel, out_shape=(piece, piece, slots, sums), in_s...  121 us
    dot_general x1, matrix products, shards(): gate_acc = jnp.dot(normed, wg_full, preferred_element_type=jnp.float32)  11.3 us
    dot_general x1, matrix products, shards(): up_acc = jnp.dot(normed, wu_full, preferred_element_type=jnp.float32)  9.54 us

profile of v12, /device:TPU:0, one launch (start us, length us, event | category | flops | bytes accessed | tf_op | source)
XLA Modules:
  0.0 154.8 jit_solution(12947711848632998341)
XLA Ops:
  0.7 0.9 fusion.42
  1.6 0.1 copy.50
  1.7 0.2 reduce-window.4
  1.9 0.7 subtract_clamp_fusion
  2.7 0.5 multiply_cosine_fusion.1
  3.2 1.2 copy.39
  4.4 0.8 convert_add_fusion
  5.2 0.1 multiply_subtract_fusion
  5.4 1.2 fusion.27
  6.7 0.2 fusion.15
  6.9 0.8 fusion
  7.7 0.7 fusion.3
  8.5 1.2 fusion.8
  9.7 0.2 copy.43.att_ref
  9.9 0.2 fusion.29
  10.3 0.1 fusion.40
  10.4 0.4 convolution_convert_fusion.1
  10.8 0.6 fusion.33
  11.4 0.3 copy.56.kv_ref
  11.8 120.6 %shard_map.149 = (bf16[4,4,320,864]{3,2,1,0:T(8,128)(2,1)}, bf16[4,4,320,864]{3,2,1,0:T(8,128)(2,1)}, bf16[16,128,256]{2,1,0:T(8,128)(2,1)S(1)}, bf16[4,2,64,5120]{3,2,1,0:T(8,128)(2,1)}) custom-call(bf16[320,864]{1,0:T(8,128)(2,1)S(1)} %copy-done, bf16[320,864]{1,0:T(8,128)(2,1)S(1)} %copy-done.1, bf16[16,128,256]{2,1,0:T(8,128)(2,1)S(1)} %copy.56.kv_ref, ...), custom_call_target="tpu_custom_call" | custom-call | tf_op jit(solution)/shard_map/pallas_call | solution.py:263
  132.4 11.3 %fusion.55 = f32[512,864]{0,1:T(8,128)S(1)} fusion(bf16[512,5120]{1,0:T(8,128)(2,1)} %bitcast.89, bf16[5120,864]{1,0:T(8,128)(2,1)} %bitcast.88), kind=kOutput, calls=%fused_computation.91 | convolution fusion | flops 4529848320 | bytes 15859712 | tf_op jit(solution)/shard_map/dot_general | solution.py:395
  143.7 9.5 %multiply_convert_fusion = bf16[512,864]{0,1:T(8,128)(2,1)} fusion(f32[512,864]{0,1:T(8,128)S(1)} %fusion.55, bf16[512,5120]{1,0:T(8,128)(2,1)S(1)} %bitcast.90, bf16[5120,864]{1,0:T(8,128)(2,1)} %bitcast.87), kind=kOutput, calls=%fused_computation.8 | convolution fusion | flops 4532502528 | bytes 16744448 | tf_op jit(solution)/shard_map/dot_general | solution.py:396
  153.4 0.7 fusion.11
  154.0 0.7 copy.45
  (32 shorter events, 0.4 us)
Async XLA Ops:
  0.6 6.0 %copy-start.5 = (s32[512]{0:T(512)S(1)}, s32[512]{0:T(512)}, u32[]{:S(2)}) copy-start(s32[512]{0:T(512)} %param.20) | copy-start | bytes 6148
  0.6 4.7 %copy-start.3 = (bf16[512,128]{1,0:T(8,128)(2,1)S(1)}, bf16[512,128]{1,0:T(8,128)(2,1)}, u32[]{:S(2)}) copy-start(bf16[512,128]{1,0:T(8,128)(2,1)} %param.15) | copy-start | bytes 393220
  0.7 4.7 %copy-start.7 = (f32[128]{0:T(128)S(1)}, f32[128]{0:T(128)}, u32[]{:S(2)}) copy-start(f32[128]{0:T(128)} %param.18) | copy-start | bytes 1540
  6.9 1.6 %copy-start.4 = (bf16[512,128]{1,0:T(8,128)(2,1)S(1)}, bf16[512,128]{1,0:T(8,128)(2,1)}, u32[]{:S(2)}) copy-start(bf16[512,128]{1,0:T(8,128)(2,1)} %param.16) | copy-start | bytes 393220
  6.9 1.6 %copy-start.8 = (f32[128]{0:T(128)S(1)}, f32[128]{0:T(128)}, u32[]{:S(2)}) copy-start(f32[128]{0:T(128)} %param.19) | copy-start | bytes 1540
  9.7 2.1 %copy-start = (bf16[320,864]{1,0:T(8,128)(2,1)S(1)}, bf16[320,864]{1,0:T(8,128)(2,1)}, u32[]{:S(2)}) copy-start(bf16[320,864]{1,0:T(8,128)(2,1)} %wg_ref.1) | copy-start | bytes 1658884
  9.7 2.1 %copy-start.1 = (bf16[320,864]{1,0:T(8,128)(2,1)S(1)}, bf16[320,864]{1,0:T(8,128)(2,1)}, u32[]{:S(2)}) copy-start(bf16[320,864]{1,0:T(8,128)(2,1)} %wu_ref.1) | copy-start | bytes 1658884
  9.7 2.1 %copy-start.2 = (f32[5120]{0:T(1024)S(1)}, f32[5120]{0:T(1024)}, u32[]{:S(2)}) copy-start(f32[5120]{0:T(1024)} %param.25) | copy-start | bytes 61444
  132.4 11.3 %copy-start.9 = (bf16[4,2,64,5120]{3,2,1,0:T(8,128)(2,1)S(1)}, bf16[4,2,64,5120]{3,2,1,0:T(8,128)(2,1)}, u32[]{:S(2)}) copy-start(bf16[4,2,64,5120]{3,2,1,0:T(8,128)(2,1)} %get-tuple-element.6) | copy-start | bytes 15728644
  143.7 9.6 %copy-start.6 = (s32[16,4]{0,1:T(4,128)S(1)}, s32[16,4]{0,1:T(4,128)}, u32[]{:S(2)}) copy-start(s32[16,4]{0,1:T(4,128)} %param.22) | copy-start | bytes 772

commit v13 on v12

--- a/solution.py
+++ b/solution.py
@@ -36,7 +36,7 @@
 def gather_kernel(
     wg_ref, wu_ref, kv_ref, att_ref, wout_ref, res_ref, gain_ref, g_ref, u_ref, kv_out, sum_ref,
     send_sems, recv_sems, local_sems, ar_send, ar_recv, a_buf, prod_v, b_src, b_buf, m_buf,
-    r_buf, gain_buf,
+    r_buf, gain_buf, s_buf,
 ):
     me = lax.axis_index("req")
     col = lax.axis_index("mp")
@@ -149,9 +149,8 @@
     def add_pair(i, carry):
         xi = i // tiles
         cols = pl.ds(pl.multiple_of((i % tiles) * width, width), width)
-        b_src[xi, :, cols] = prod_v[xi, cc, :, cols].astype(jnp.float32) + a_buf[xi, :, cols].astype(
-            jnp.float32
-        )
+        pair = prod_v[xi, cc, :, cols].astype(jnp.float32) + a_buf[xi, :, cols].astype(jnp.float32)
+        b_src[xi, :, cols] = pair.astype(b_src.dtype)
         return carry
 
     lax.fori_loop(0, xs * tiles, add_pair, 0)
@@ -187,11 +186,11 @@
 
     def add_chips(t, squares):
         cols = pl.ds(pl.multiple_of(t * width, width), width)
-        acc = b_src[cx, :, cols]
+        acc = b_src[cx, :, cols].astype(jnp.float32)
         for d in range(1, xs):
-            acc = acc + b_buf[(cx + d) % xs, :, cols]
+            acc = acc + b_buf[(cx + d) % xs, :, cols].astype(jnp.float32)
         state = acc + r_buf[:, cols].astype(jnp.float32)
-        b_src[cx, :, cols] = state
+        s_buf[:, cols] = state
         return squares + jnp.sum(state * state, axis=1, keepdims=True)
 
     squares = lax.fori_loop(0, tiles, add_chips, jnp.zeros((m_buf.shape[0], 1), jnp.float32))
@@ -199,7 +198,7 @@
 
     def scale_rows(t, carry):
         cols = pl.ds(pl.multiple_of(t * width, width), width)
-        normed = b_src[cx, :, cols] * scale * gain_buf[:, cols]
+        normed = s_buf[:, cols] * scale * gain_buf[:, cols]
         m_buf[:, cols] = normed.astype(m_buf.dtype)
         return carry
 
@@ -273,11 +272,12 @@
             pltpu.SemaphoreType.DMA((2 * xs,)),
             pltpu.VMEM((xs, chunk, width), product.dtype),
             pltpu.VMEM(product.shape, product.dtype),
-            pltpu.VMEM((xs, chunk, width), jnp.float32),
-            pltpu.VMEM((xs, chunk, width), jnp.float32),
+            pltpu.VMEM((xs, chunk, width), product.dtype),
+            pltpu.VMEM((xs, chunk, width), product.dtype),
             pltpu.VMEM((chunk, width), product.dtype),
             pltpu.VMEM((chunk, width), residual.dtype),
             pltpu.VMEM((1, width), jnp.float32),
+            pltpu.VMEM((chunk, width), jnp.float32),
         ],
         compiler_params=pltpu.CompilerParams(
             collective_id=0, has_side_effects=True, vmem_limit_bytes=48 * 1024 * 1024

time: 156 us -> 152 us (0.974)
  Pallas kernels: 121 us -> 117 us
    pallas_call x1, Pallas kernels: 121 us -> 117 us  [gather_weights(): pl.pallas_call(gather_kernel, out_shape=(piece, piece, slots, sums), in_s...]
where the time goes in v13:
time: 152 us; the launch traced here: 151 us
  Pallas kernels  117 us (77%)
  matrix products  24.5 us (16%)
  other arithmetic  6.14 us (4%)
  local copies, waits for them, and re-layouts  2.59 us (2%)
    pallas_call x1, Pallas kernels, gather_weights(): pl.pallas_call(gather_kernel, out_shape=(piece, piece, slots, sums), in_s...  117 us
    dot_general x1, matrix products, shards(): gate_acc = jnp.dot(normed, wg_full, preferred_element_type=jnp.float32)  11.3 us
    dot_general x1, matrix products, shards(): up_acc = jnp.dot(normed, wu_full, preferred_element_type=jnp.float32)  9.54 us

profile of v13, /device:TPU:0, one launch (start us, length us, event | category | flops | bytes accessed | tf_op | source)
XLA Modules:
  0.0 150.6 jit_solution(15061024587263847571)
XLA Ops:
  0.7 0.9 fusion.42
  1.6 0.1 copy.50
  1.7 0.2 reduce-window.4
  1.9 0.7 subtract_clamp_fusion
  2.7 0.5 multiply_cosine_fusion.1
  3.2 1.2 copy.39
  4.4 0.8 convert_add_fusion
  5.2 0.1 multiply_subtract_fusion
  5.4 1.2 fusion.27
  6.7 0.2 fusion.15
  6.9 0.8 fusion
  7.7 0.7 fusion.3
  8.5 1.2 fusion.8
  9.7 0.2 copy.43.att_ref
  9.9 0.2 fusion.29
  10.3 0.1 fusion.40
  10.4 0.4 convolution_convert_fusion.1
  10.8 0.6 fusion.33
  11.4 0.3 copy.56.kv_ref
  11.8 116.5 %shard_map.149 = (bf16[4,4,320,864]{3,2,1,0:T(8,128)(2,1)}, bf16[4,4,320,864]{3,2,1,0:T(8,128)(2,1)}, bf16[16,128,256]{2,1,0:T(8,128)(2,1)S(1)}, bf16[4,2,64,5120]{3,2,1,0:T(8,128)(2,1)}) custom-call(bf16[320,864]{1,0:T(8,128)(2,1)S(1)} %copy-done, bf16[320,864]{1,0:T(8,128)(2,1)S(1)} %copy-done.1, bf16[16,128,256]{2,1,0:T(8,128)(2,1)S(1)} %copy.56.kv_ref, ...), custom_call_target="tpu_custom_call" | custom-call | tf_op jit(solution)/shard_map/pallas_call | solution.py:262
  128.3 11.3 %fusion.55 = f32[512,864]{0,1:T(8,128)S(1)} fusion(bf16[512,5120]{1,0:T(8,128)(2,1)} %bitcast.89, bf16[5120,864]{1,0:T(8,128)(2,1)} %bitcast.88), kind=kOutput, calls=%fused_computation.91 | convolution fusion | flops 4529848320 | bytes 15859712 | tf_op jit(solution)/shard_map/dot_general | solution.py:395
  139.6 9.5 %multiply_convert_fusion = bf16[512,864]{0,1:T(8,128)(2,1)} fusion(f32[512,864]{0,1:T(8,128)S(1)} %fusion.55, bf16[512,5120]{1,0:T(8,128)(2,1)S(1)} %bitcast.90, bf16[5120,864]{1,0:T(8,128)(2,1)} %bitcast.87), kind=kOutput, calls=%fused_computation.8 | convolution fusion | flops 4532502528 | bytes 16744448 | tf_op jit(solution)/shard_map/dot_general | solution.py:396
  149.2 0.7 fusion.11
  149.9 0.7 copy.45
  (32 shorter events, 0.4 us)
Async XLA Ops:
  0.6 6.0 %copy-start.5 = (s32[512]{0:T(512)S(1)}, s32[512]{0:T(512)}, u32[]{:S(2)}) copy-start(s32[512]{0:T(512)} %param.20) | copy-start | bytes 6148
  0.6 4.7 %copy-start.3 = (bf16[512,128]{1,0:T(8,128)(2,1)S(1)}, bf16[512,128]{1,0:T(8,128)(2,1)}, u32[]{:S(2)}) copy-start(bf16[512,128]{1,0:T(8,128)(2,1)} %param.15) | copy-start | bytes 393220
  0.7 4.7 %copy-start.7 = (f32[128]{0:T(128)S(1)}, f32[128]{0:T(128)}, u32[]{:S(2)}) copy-start(f32[128]{0:T(128)} %param.18) | copy-start | bytes 1540
  6.9 1.6 %copy-start.4 = (bf16[512,128]{1,0:T(8,128)(2,1)S(1)}, bf16[512,128]{1,0:T(8,128)(2,1)}, u32[]{:S(2)}) copy-start(bf16[512,128]{1,0:T(8,128)(2,1)} %param.16) | copy-start | bytes 393220
  6.9 1.6 %copy-start.8 = (f32[128]{0:T(128)S(1)}, f32[128]{0:T(128)}, u32[]{:S(2)}) copy-start(f32[128]{0:T(128)} %param.19) | copy-start | bytes 1540
  9.7 2.1 %copy-start = (bf16[320,864]{1,0:T(8,128)(2,1)S(1)}, bf16[320,864]{1,0:T(8,128)(2,1)}, u32[]{:S(2)}) copy-start(bf16[320,864]{1,0:T(8,128)(2,1)} %wg_ref.1) | copy-start | bytes 1658884
  9.7 2.1 %copy-start.1 = (bf16[320,864]{1,0:T(8,128)(2,1)S(1)}, bf16[320,864]{1,0:T(8,128)(2,1)}, u32[]{:S(2)}) copy-start(bf16[320,864]{1,0:T(8,128)(2,1)} %wu_ref.1) | copy-start | bytes 1658884
  9.7 2.1 %copy-start.2 = (f32[5120]{0:T(1024)S(1)}, f32[5120]{0:T(1024)}, u32[]{:S(2)}) copy-start(f32[5120]{0:T(1024)} %param.25) | copy-start | bytes 61444
  128.3 11.3 %copy-start.9 = (bf16[4,2,64,5120]{3,2,1,0:T(8,128)(2,1)S(1)}, bf16[4,2,64,5120]{3,2,1,0:T(8,128)(2,1)}, u32[]{:S(2)}) copy-start(bf16[4,2,64,5120]{3,2,1,0:T(8,128)(2,1)} %get-tuple-element.6) | copy-start | bytes 15728644
  139.6 9.6 %copy-start.6 = (s32[16,4]{0,1:T(4,128)S(1)}, s32[16,4]{0,1:T(4,128)}, u32[]{:S(2)}) copy-start(s32[16,4]{0,1:T(4,128)} %param.22) | copy-start | bytes 772

commit v14 on v13

--- a/solution.py
+++ b/solution.py
@@ -34,9 +34,9 @@
 
 
 def gather_kernel(
-    wg_ref, wu_ref, kv_ref, att_ref, wout_ref, res_ref, gain_ref, g_ref, u_ref, kv_out, sum_ref,
-    send_sems, recv_sems, local_sems, ar_send, ar_recv, a_buf, prod_v, b_src, b_buf, m_buf,
-    r_buf, gain_buf, s_buf,
+    wg_ref, wu_ref, kv_ref, att_ref, wout_ref, res_ref, gain_ref, src_ref, g_ref, u_ref, kv_out,
+    sum_ref, send_sems, recv_sems, local_sems, ar_send, ar_recv, a_buf, prod_v, b_src, b_buf,
+    m_buf, r_buf, gain_buf, s_buf, kv_land,
 ):
     me = lax.axis_index("req")
     col = lax.axis_index("mp")
@@ -118,13 +118,13 @@
     gz = {"y": (send(wg_ref, g_ref.at[z, y], to(zp, y)), send(wg_ref, g_ref.at[z, y], to(zm, y)))}
     uy = {"z": (send(wu_ref, u_ref.at[z, y], to(z, yp)), send(wu_ref, u_ref.at[z, y], to(z, ym)))}
     kv_copies = []
-    own_kv = pltpu.make_async_copy(kv_ref.at[me], kv_out.at[me], local_sems.at[2])
+    own_kv = pltpu.make_async_copy(kv_ref.at[me], kv_land.at[me], local_sems.at[2])
     own_kv.start()
     for d in range(1, groups):
         dest = (me + d) % groups
         c = pltpu.make_async_remote_copy(
             src_ref=kv_ref.at[dest],
-            dst_ref=kv_out.at[me],
+            dst_ref=kv_land.at[me],
             send_sem=send_sems.at[KV_SEMS + d - 1],
             recv_sem=recv_sems.at[KV_SEMS + d - 1],
             device_id=(dest, col),
@@ -247,23 +247,26 @@
     own_g.wait()
     own_u.wait()
     own_kv.wait()
-
-
-def gather_weights(w_gate, w_up, kv_send, attended, w_out, residual, gain):
+    for page in range(kv_out.shape[0]):
+        kv_out[page] = kv_land[src_ref[page]]
+
+
+def gather_weights(w_gate, w_up, kv_send, attended, w_out, residual, gain, page_src):
     rows, cols = w_gate.shape
     xs, _, chunk, width = residual.shape
     product = jax.ShapeDtypeStruct(residual.shape, jnp.bfloat16)
     any_spec = pl.BlockSpec(memory_space=pl.ANY)
     vmem_spec = pl.BlockSpec(memory_space=pltpu.VMEM)
     piece = jax.ShapeDtypeStruct((RING, RING, rows, cols), w_gate.dtype)
-    slots = jax.ShapeDtypeStruct(kv_send.shape, kv_send.dtype)
+    slots = jax.ShapeDtypeStruct((page_src.shape[0],) + kv_send.shape[1:], kv_send.dtype)
+    smem_spec = pl.BlockSpec(memory_space=pltpu.SMEM)
     sums = jax.ShapeDtypeStruct(product.shape, product.dtype)
     sems = KV_SEMS + kv_send.shape[0] - 1
     return pl.pallas_call(
         gather_kernel,
         out_shape=(piece, piece, slots, sums),
-        in_specs=[any_spec] * 3 + [vmem_spec] * 2 + [any_spec] * 2,
-        out_specs=(any_spec, any_spec, any_spec, any_spec),
+        in_specs=[any_spec] * 3 + [vmem_spec] * 2 + [any_spec] * 2 + [smem_spec],
+        out_specs=(any_spec, any_spec, vmem_spec, any_spec),
         scratch_shapes=[
             pltpu.SemaphoreType.DMA((sems,)),
             pltpu.SemaphoreType.DMA((sems,)),
@@ -278,11 +281,12 @@
             pltpu.VMEM((chunk, width), residual.dtype),
             pltpu.VMEM((1, width), jnp.float32),
             pltpu.VMEM((chunk, width), jnp.float32),
+            pltpu.VMEM(kv_send.shape, kv_send.dtype),
         ],
         compiler_params=pltpu.CompilerParams(
             collective_id=0, has_side_effects=True, vmem_limit_bytes=48 * 1024 * 1024
         ),
-    )(w_gate, w_up, kv_send, attended, w_out, residual, gain)
+    )(w_gate, w_up, kv_send, attended, w_out, residual, gain, page_src)
 
 def normalize(resid_rows, summed, gain_row):
     state = resid_rows.astype(jnp.float32) + summed
@@ -372,7 +376,7 @@
     hits = (
         page_table[None, :, :] == (me_req * REQS + jnp.arange(REQS, dtype=jnp.int32))[:, None, None]
     )
-    page_select = jnp.sum(hits.astype(jnp.int32), axis=2).astype(jnp.bfloat16)
+    page_src = jnp.argmax(jnp.any(hits, axis=2), axis=1).astype(jnp.int32)
 
     n_mp = lax.axis_size("mp")
     split_rows = (n_mp // 2, 2, block_rows // n_mp, residual.shape[-1])
@@ -384,12 +388,11 @@
         w_out,
         residual.reshape(split_rows),
         norm_gain.reshape(1, -1).astype(jnp.float32),
+        page_src,
     )
     normed = normed.reshape(block_rows, -1)
-    kv_in = kv_in.reshape(groups_all, PAGE, kv_heads, 2 * HD)
-    cache_out = jnp.einsum(
-        "ls,sphc->lhpc", page_select, kv_in, preferred_element_type=jnp.float32
-    ).astype(jnp.bfloat16)
+    assert kv_heads == 1
+    cache_out = kv_in.reshape(REQS, kv_heads, PAGE, 2 * HD)
     wg_full = g_full.reshape(-1, w_gate.shape[1])
     wu_full = u_full.reshape(-1, w_up.shape[1])
     gate_acc = jnp.dot(normed, wg_full, preferred_element_type=jnp.float32)

time: 152 us -> 155 us (1.020)
  other arithmetic: 6.14 us -> 10 us
where the time goes in v14:
time: 155 us; the launch traced here: 153 us
  Pallas kernels  117 us (75%)
  matrix products  23.8 us (15%)
  other arithmetic  10 us (6%)
  local copies, waits for them, and re-layouts  1.6 us (1%)
    pallas_call x1, Pallas kernels, gather_weights(): pl.pallas_call(gather_kernel, out_shape=(piece, piece, slots, sums), in_s...  117 us
    dot_general x1, matrix products, shards(): gate_acc = jnp.dot(normed, wg_full, preferred_element_type=jnp.float32)  11.3 us
    dot_general x1, matrix products, shards(): up_acc = jnp.dot(normed, wu_full, preferred_element_type=jnp.float32)  9.55 us

profile of v14, /device:TPU:0, one launch (start us, length us, event | category | flops | bytes accessed | tf_op | source)
XLA Modules:
  0.0 152.9 jit_solution(13985624128499277086)
XLA Ops:
  0.7 0.7 broadcast_compare_fusion
  1.4 0.8 compare_reduce_fusion
  2.2 0.6 iota_reduce_fusion
  2.8 0.7 subtract_clamp_fusion
  3.5 0.9 fusion.40
  4.5 0.2 reduce-window.4
  4.9 1.1 fusion.38
  6.0 1.0 fusion.13
  7.0 0.9 add_bitcast_fusion
  7.9 1.2 fusion.25
  9.1 0.2 fusion.27
  9.3 0.4 convolution_convert_fusion
  9.7 0.5 multiply_cosine_fusion.1
  10.2 0.2 copy.37
  10.7 0.6 fusion.31
  11.3 0.4 copy.51.kv_ref
  11.7 0.8 fusion
  12.5 0.7 fusion.3
  13.3 1.2 fusion.8
  14.5 0.2 copy.41.att_ref
  14.7 116.6 %shard_map.149 = (bf16[4,4,320,864]{3,2,1,0:T(8,128)(2,1)}, bf16[4,4,320,864]{3,2,1,0:T(8,128)(2,1)}, bf16[4,128,256]{2,1,0:T(8,128)(2,1)S(1)}, bf16[4,2,64,5120]{3,2,1,0:T(8,128)(2,1)}) custom-call(bf16[320,864]{1,0:T(8,128)(2,1)S(1)} %copy-done, bf16[320,864]{1,0:T(8,128)(2,1)S(1)} %copy-done.1, bf16[16,128,256]{2,1,0:T(8,128)(2,1)S(1)} %copy.51.kv_ref, ...), custom_call_target="tpu_custom_call" | custom-call | tf_op jit(solution)/shard_map/pallas_call | solution.py:265
  131.4 11.3 %fusion.51 = f32[512,864]{0,1:T(8,128)S(1)} fusion(bf16[512,5120]{1,0:T(8,128)(2,1)} %bitcast.86, bf16[5120,864]{1,0:T(8,128)(2,1)} %bitcast.85), kind=kOutput, calls=%fused_computation.87 | convolution fusion | flops 4529848320 | bytes 15859712 | tf_op jit(solution)/shard_map/dot_general | solution.py:398
  142.6 9.5 %multiply_convert_fusion = bf16[512,864]{0,1:T(8,128)(2,1)} fusion(f32[512,864]{0,1:T(8,128)S(1)} %fusion.51, bf16[512,5120]{1,0:T(8,128)(2,1)S(1)} %bitcast.87, bf16[5120,864]{1,0:T(8,128)(2,1)} %bitcast.84), kind=kOutput, calls=%fused_computation.8 | convolution fusion | flops 4532502528 | bytes 16744448 | tf_op jit(solution)/shard_map/dot_general | solution.py:399
  152.2 0.7 copy.53
  (28 shorter events, 0.7 us)
Async XLA Ops:
  0.6 9.8 %copy-start.5 = (f32[384]{0:T(512)S(1)}, f32[384]{0:T(512)}, u32[]{:S(2)}) copy-start(f32[384]{0:T(512)} %param.17) | copy-start | bytes 4612
  0.6 9.6 %copy-start.3 = (bf16[512,384]{1,0:T(8,128)(2,1)S(1)}, bf16[512,384]{1,0:T(8,128)(2,1)}, u32[]{:S(2)}) copy-start(bf16[512,384]{1,0:T(8,128)(2,1)} %param.14) | copy-start | bytes 1179652
  11.7 1.5 %copy-start.4 = (bf16[512,128]{1,0:T(8,128)(2,1)S(1)}, bf16[512,128]{1,0:T(8,128)(2,1)}, u32[]{:S(2)}) copy-start(bf16[512,128]{1,0:T(8,128)(2,1)} %param.16) | copy-start | bytes 393220
  11.7 1.5 %copy-start.6 = (f32[128]{0:T(128)S(1)}, f32[128]{0:T(128)}, u32[]{:S(2)}) copy-start(f32[128]{0:T(128)} %param.19) | copy-start | bytes 1540
  13.2 1.5 copy-start
  13.2 1.5 copy-start.1
  13.3 1.5 copy-start.2
  131.3 11.3 %copy-start.7 = (bf16[4,2,64,5120]{3,2,1,0:T(8,128)(2,1)S(1)}, bf16[4,2,64,5120]{3,2,1,0:T(8,128)(2,1)}, u32[]{:S(2)}) copy-start(bf16[4,2,64,5120]{3,2,1,0:T(8,128)(2,1)} %get-tuple-element.8) | copy-start | bytes 15728644

commit v15 on v13

--- a/solution.py
+++ b/solution.py
@@ -117,6 +117,51 @@
     u_from_zp = send(wu_ref, u_ref.at[z, y], to(zm, y))
     gz = {"y": (send(wg_ref, g_ref.at[z, y], to(zp, y)), send(wg_ref, g_ref.at[z, y], to(zm, y)))}
     uy = {"z": (send(wu_ref, u_ref.at[z, y], to(z, yp)), send(wu_ref, u_ref.at[z, y], to(z, ym)))}
+
+    chunk = prod_v.shape[2]
+
+    def project(k, carry):
+        rows = att_ref[pl.ds(pl.multiple_of(k * chunk, chunk), chunk), :]
+        part = jnp.dot(rows, wout_ref[...], preferred_element_type=jnp.float32)
+        prod_v[k // 2, k % 2] = part.astype(prod_v.dtype)
+        return carry
+
+    lax.fori_loop(0, 2 * xs, project, 0)
+    ar_a = ar_copy(0, prod_v.at[:, 1 - cc], a_buf, core_peer)
+
+    ar_a.wait_recv()
+
+    def add_pair(i, carry):
+        xi = i // tiles
+        cols = pl.ds(pl.multiple_of((i % tiles) * width, width), width)
+        pair = prod_v[xi, cc, :, cols].astype(jnp.float32) + a_buf[xi, :, cols].astype(jnp.float32)
+        b_src[xi, :, cols] = pair.astype(b_src.dtype)
+        return carry
+
+    lax.fori_loop(0, xs * tiles, add_pair, 0)
+    ar_b = [
+        ar_copy(d, b_src.at[(cx + d) % xs], b_buf.at[cx], x_peers[d - 1]) for d in range(1, xs)
+    ]
+
+    g_from_ym.wait_recv()
+    g_far_a = send(g_ref.at[z, ym, low], g_ref.at[z, ym, low], to(z, yp))
+    gz["ym"] = (send(g_ref.at[z, ym], g_ref.at[z, ym], to(zp, y)), send(g_ref.at[z, ym], g_ref.at[z, ym], to(zm, y)))
+    u_from_zm.wait_recv()
+    u_far_a = send(u_ref.at[zm, y, low], u_ref.at[zm, y, low], to(zp, y))
+    uy["zm"] = (send(u_ref.at[zm, y], u_ref.at[zm, y], to(z, yp)), send(u_ref.at[zm, y], u_ref.at[zm, y], to(z, ym)))
+    g_from_yp.wait_recv()
+    g_far_b = send(g_ref.at[z, yp, high], g_ref.at[z, yp, high], to(z, ym))
+    gz["yp"] = (send(g_ref.at[z, yp], g_ref.at[z, yp], to(zp, y)), send(g_ref.at[z, yp], g_ref.at[z, yp], to(zm, y)))
+    u_from_zp.wait_recv()
+    u_far_b = send(u_ref.at[zp, y, high], u_ref.at[zp, y, high], to(zm, y))
+    uy["zp"] = (send(u_ref.at[zp, y], u_ref.at[zp, y], to(z, yp)), send(u_ref.at[zp, y], u_ref.at[zp, y], to(z, ym)))
+
+    g_far_a.wait_recv()
+    g_far_b.wait_recv()
+    gz["y2"] = (send(g_ref.at[z, y2], g_ref.at[z, y2], to(zp, y)), send(g_ref.at[z, y2], g_ref.at[z, y2], to(zm, y)))
+    u_far_a.wait_recv()
+    u_far_b.wait_recv()
+    uy["z2"] = (send(u_ref.at[z2, y], u_ref.at[z2, y], to(z, yp)), send(u_ref.at[z2, y], u_ref.at[z2, y], to(z, ym)))
     kv_copies = []
     own_kv = pltpu.make_async_copy(kv_ref.at[me], kv_out.at[me], local_sems.at[2])
     own_kv.start()
@@ -132,51 +177,6 @@
         )
         c.start()
         kv_copies.append(c)
-
-    chunk = prod_v.shape[2]
-
-    def project(k, carry):
-        rows = att_ref[pl.ds(pl.multiple_of(k * chunk, chunk), chunk), :]
-        part = jnp.dot(rows, wout_ref[...], preferred_element_type=jnp.float32)
-        prod_v[k // 2, k % 2] = part.astype(prod_v.dtype)
-        return carry
-
-    lax.fori_loop(0, 2 * xs, project, 0)
-    ar_a = ar_copy(0, prod_v.at[:, 1 - cc], a_buf, core_peer)
-
-    ar_a.wait_recv()
-
-    def add_pair(i, carry):
-        xi = i // tiles
-        cols = pl.ds(pl.multiple_of((i % tiles) * width, width), width)
-        pair = prod_v[xi, cc, :, cols].astype(jnp.float32) + a_buf[xi, :, cols].astype(jnp.float32)
-        b_src[xi, :, cols] = pair.astype(b_src.dtype)
-        return carry
-
-    lax.fori_loop(0, xs * tiles, add_pair, 0)
-    ar_b = [
-        ar_copy(d, b_src.at[(cx + d) % xs], b_buf.at[cx], x_peers[d - 1]) for d in range(1, xs)
-    ]
-
-    g_from_ym.wait_recv()
-    g_far_a = send(g_ref.at[z, ym, low], g_ref.at[z, ym, low], to(z, yp))
-    gz["ym"] = (send(g_ref.at[z, ym], g_ref.at[z, ym], to(zp, y)), send(g_ref.at[z, ym], g_ref.at[z, ym], to(zm, y)))
-    u_from_zm.wait_recv()
-    u_far_a = send(u_ref.at[zm, y, low], u_ref.at[zm, y, low], to(zp, y))
-    uy["zm"] = (send(u_ref.at[zm, y], u_ref.at[zm, y], to(z, yp)), send(u_ref.at[zm, y], u_ref.at[zm, y], to(z, ym)))
-    g_from_yp.wait_recv()
-    g_far_b = send(g_ref.at[z, yp, high], g_ref.at[z, yp, high], to(z, ym))
-    gz["yp"] = (send(g_ref.at[z, yp], g_ref.at[z, yp], to(zp, y)), send(g_ref.at[z, yp], g_ref.at[z, yp], to(zm, y)))
-    u_from_zp.wait_recv()
-    u_far_b = send(u_ref.at[zp, y, high], u_ref.at[zp, y, high], to(zm, y))
-    uy["zp"] = (send(u_ref.at[zp, y], u_ref.at[zp, y], to(z, yp)), send(u_ref.at[zp, y], u_ref.at[zp, y], to(z, ym)))
-
-    g_far_a.wait_recv()
-    g_far_b.wait_recv()
-    gz["y2"] = (send(g_ref.at[z, y2], g_ref.at[z, y2], to(zp, y)), send(g_ref.at[z, y2], g_ref.at[z, y2], to(zm, y)))
-    u_far_a.wait_recv()
-    u_far_b.wait_recv()
-    uy["z2"] = (send(u_ref.at[z2, y], u_ref.at[z2, y], to(z, yp)), send(u_ref.at[z2, y], u_ref.at[z2, y], to(z, ym)))
 
     for c in ar_b:
         c.wait_recv()

time: 152 us -> 151 us (level)
  no operation moved by 1% of the time
where the time goes in v15:
time: 151 us; the launch traced here: 150 us
  Pallas kernels  116 us (77%)
  matrix products  24.5 us (16%)
  other arithmetic  6.14 us (4%)
  local copies, waits for them, and re-layouts  2.59 us (2%)
    pallas_call x1, Pallas kernels, gather_weights(): pl.pallas_call(gather_kernel, out_shape=(piece, piece, slots, sums), in_s...  116 us
    dot_general x1, matrix products, shards(): gate_acc = jnp.dot(normed, wg_full, preferred_element_type=jnp.float32)  11.3 us
    dot_general x1, matrix products, shards(): up_acc = jnp.dot(normed, wu_full, preferred_element_type=jnp.float32)  9.54 us

profile of v15, /device:TPU:0, one launch (start us, length us, event | category | flops | bytes accessed | tf_op | source)
XLA Modules:
  0.0 150.3 jit_solution(12518252894973179288)
XLA Ops:
  0.7 0.9 fusion.42
  1.6 0.1 copy.50
  1.7 0.2 reduce-window.4
  1.9 0.7 subtract_clamp_fusion
  2.7 0.5 multiply_cosine_fusion.1
  3.2 1.2 copy.39
  4.4 0.8 convert_add_fusion
  5.2 0.1 multiply_subtract_fusion
  5.4 1.2 fusion.27
  6.7 0.2 fusion.15
  6.9 0.8 fusion
  7.7 0.7 fusion.3
  8.5 1.2 fusion.8
  9.7 0.2 copy.43.att_ref
  9.9 0.2 fusion.29
  10.3 0.1 fusion.40
  10.4 0.4 convolution_convert_fusion.1
  10.8 0.6 fusion.33
  11.4 0.3 copy.56.kv_ref
  11.8 116.1 %shard_map.149 = (bf16[4,4,320,864]{3,2,1,0:T(8,128)(2,1)}, bf16[4,4,320,864]{3,2,1,0:T(8,128)(2,1)}, bf16[16,128,256]{2,1,0:T(8,128)(2,1)S(1)}, bf16[4,2,64,5120]{3,2,1,0:T(8,128)(2,1)}) custom-call(bf16[320,864]{1,0:T(8,128)(2,1)S(1)} %copy-done, bf16[320,864]{1,0:T(8,128)(2,1)S(1)} %copy-done.1, bf16[16,128,256]{2,1,0:T(8,128)(2,1)S(1)} %copy.56.kv_ref, ...), custom_call_target="tpu_custom_call" | custom-call | tf_op jit(solution)/shard_map/pallas_call | solution.py:262
  127.9 11.3 %fusion.55 = f32[512,864]{0,1:T(8,128)S(1)} fusion(bf16[512,5120]{1,0:T(8,128)(2,1)} %bitcast.89, bf16[5120,864]{1,0:T(8,128)(2,1)} %bitcast.88), kind=kOutput, calls=%fused_computation.91 | convolution fusion | flops 4529848320 | bytes 15859712 | tf_op jit(solution)/shard_map/dot_general | solution.py:395
  139.2 9.5 %multiply_convert_fusion = bf16[512,864]{0,1:T(8,128)(2,1)} fusion(f32[512,864]{0,1:T(8,128)S(1)} %fusion.55, bf16[512,5120]{1,0:T(8,128)(2,1)S(1)} %bitcast.90, bf16[5120,864]{1,0:T(8,128)(2,1)} %bitcast.87), kind=kOutput, calls=%fused_computation.8 | convolution fusion | flops 4532502528 | bytes 16744448 | tf_op jit(solution)/shard_map/dot_general | solution.py:396
  148.9 0.7 fusion.11
  149.5 0.7 copy.45
  (32 shorter events, 0.4 us)
Async XLA Ops:
  0.6 6.0 %copy-start.5 = (s32[512]{0:T(512)S(1)}, s32[512]{0:T(512)}, u32[]{:S(2)}) copy-start(s32[512]{0:T(512)} %param.20) | copy-start | bytes 6148
  0.6 4.7 %copy-start.3 = (bf16[512,128]{1,0:T(8,128)(2,1)S(1)}, bf16[512,128]{1,0:T(8,128)(2,1)}, u32[]{:S(2)}) copy-start(bf16[512,128]{1,0:T(8,128)(2,1)} %param.15) | copy-start | bytes 393220
  0.7 4.7 %copy-start.7 = (f32[128]{0:T(128)S(1)}, f32[128]{0:T(128)}, u32[]{:S(2)}) copy-start(f32[128]{0:T(128)} %param.18) | copy-start | bytes 1540
  6.9 1.6 %copy-start.4 = (bf16[512,128]{1,0:T(8,128)(2,1)S(1)}, bf16[512,128]{1,0:T(8,128)(2,1)}, u32[]{:S(2)}) copy-start(bf16[512,128]{1,0:T(8,128)(2,1)} %param.16) | copy-start | bytes 393220
  6.9 1.6 %copy-start.8 = (f32[128]{0:T(128)S(1)}, f32[128]{0:T(128)}, u32[]{:S(2)}) copy-start(f32[128]{0:T(128)} %param.19) | copy-start | bytes 1540
  9.7 2.1 %copy-start = (bf16[320,864]{1,0:T(8,128)(2,1)S(1)}, bf16[320,864]{1,0:T(8,128)(2,1)}, u32[]{:S(2)}) copy-start(bf16[320,864]{1,0:T(8,128)(2,1)} %wg_ref.1) | copy-start | bytes 1658884
  9.7 2.1 %copy-start.1 = (bf16[320,864]{1,0:T(8,128)(2,1)S(1)}, bf16[320,864]{1,0:T(8,128)(2,1)}, u32[]{:S(2)}) copy-start(bf16[320,864]{1,0:T(8,128)(2,1)} %wu_ref.1) | copy-start | bytes 1658884
  9.7 2.1 %copy-start.2 = (f32[5120]{0:T(1024)S(1)}, f32[5120]{0:T(1024)}, u32[]{:S(2)}) copy-start(f32[5120]{0:T(1024)} %param.25) | copy-start | bytes 61444
  127.9 11.3 %copy-start.9 = (bf16[4,2,64,5120]{3,2,1,0:T(8,128)(2,1)S(1)}, bf16[4,2,64,5120]{3,2,1,0:T(8,128)(2,1)}, u32[]{:S(2)}) copy-start(bf16[4,2,64,5120]{3,2,1,0:T(8,128)(2,1)} %get-tuple-element.6) | copy-start | bytes 15728644
  139.2 9.6 %copy-start.6 = (s32[16,4]{0,1:T(4,128)S(1)}, s32[16,4]{0,1:T(4,128)}, u32[]{:S(2)}) copy-start(s32[16,4]{0,1:T(4,128)} %param.22) | copy-start | bytes 772

commit v16 on v15

--- a/solution.py
+++ b/solution.py
@@ -162,6 +162,55 @@
     u_far_a.wait_recv()
     u_far_b.wait_recv()
     uy["z2"] = (send(u_ref.at[z2, y], u_ref.at[z2, y], to(z, yp)), send(u_ref.at[z2, y], u_ref.at[z2, y], to(z, ym)))
+
+    for c in ar_b:
+        c.wait_recv()
+
+    r_load.wait()
+    g_load.wait()
+
+    def add_chips(t, squares):
+        cols = pl.ds(pl.multiple_of(t * width, width), width)
+        acc = b_src[cx, :, cols].astype(jnp.float32)
+        for d in range(1, xs):
+            acc = acc + b_buf[(cx + d) % xs, :, cols].astype(jnp.float32)
+        state = acc + r_buf[:, cols].astype(jnp.float32)
+        s_buf[:, cols] = state
+        return squares + jnp.sum(state * state, axis=1, keepdims=True)
+
+    squares = lax.fori_loop(0, tiles, add_chips, jnp.zeros((m_buf.shape[0], 1), jnp.float32))
+    scale = lax.rsqrt(squares / m_buf.shape[1] + EPS)
+
+    def scale_rows(t, carry):
+        cols = pl.ds(pl.multiple_of(t * width, width), width)
+        normed = s_buf[:, cols] * scale * gain_buf[:, cols]
+        m_buf[:, cols] = normed.astype(m_buf.dtype)
+        return carry
+
+    lax.fori_loop(0, tiles, scale_rows, 0)
+    own_sum = pltpu.make_async_copy(m_buf, sum_ref.at[cx, cc], local_sems.at[4])
+    own_sum.start()
+    own_sum.wait()
+    ar_c = [
+        ar_copy(xs - 1 + d, sum_ref.at[cx, cc], sum_ref.at[cx, cc], x_peers[d - 1])
+        for d in range(1, xs)
+    ]
+
+    for (gkey, yy), (ukey, zz) in zip(
+        (("y", y), ("ym", ym), ("yp", yp), ("y2", y2)),
+        (("z", z), ("zm", zm), ("zp", zp), ("z2", z2)),
+    ):
+        from_zm, from_zp = gz[gkey]
+        from_ym, from_yp = uy[ukey]
+        from_zm.wait_recv()
+        send(g_ref.at[zm, yy, low], g_ref.at[zm, yy, low], to(zp, y))
+        from_ym.wait_recv()
+        send(u_ref.at[zz, ym, low], u_ref.at[zz, ym, low], to(z, yp))
+        from_zp.wait_recv()
+        send(g_ref.at[zp, yy, high], g_ref.at[zp, yy, high], to(zm, y))
+        from_yp.wait_recv()
+        send(u_ref.at[zz, yp, high], u_ref.at[zz, yp, high], to(z, ym))
+
     kv_copies = []
     own_kv = pltpu.make_async_copy(kv_ref.at[me], kv_out.at[me], local_sems.at[2])
     own_kv.start()
@@ -177,54 +226,6 @@
         )
         c.start()
         kv_copies.append(c)
-
-    for c in ar_b:
-        c.wait_recv()
-
-    r_load.wait()
-    g_load.wait()
-
-    def add_chips(t, squares):
-        cols = pl.ds(pl.multiple_of(t * width, width), width)
-        acc = b_src[cx, :, cols].astype(jnp.float32)
-        for d in range(1, xs):
-            acc = acc + b_buf[(cx + d) % xs, :, cols].astype(jnp.float32)
-        state = acc + r_buf[:, cols].astype(jnp.float32)
-        s_buf[:, cols] = state
-        return squares + jnp.sum(state * state, axis=1, keepdims=True)
-
-    squares = lax.fori_loop(0, tiles, add_chips, jnp.zeros((m_buf.shape[0], 1), jnp.float32))
-    scale = lax.rsqrt(squares / m_buf.shape[1] + EPS)
-
-    def scale_rows(t, carry):
-        cols = pl.ds(pl.multiple_of(t * width, width), width)
-        normed = s_buf[:, cols] * scale * gain_buf[:, cols]
-        m_buf[:, cols] = normed.astype(m_buf.dtype)
-        return carry
-
-    lax.fori_loop(0, tiles, scale_rows, 0)
-    own_sum = pltpu.make_async_copy(m_buf, sum_ref.at[cx, cc], local_sems.at[4])
-    own_sum.start()
-    own_sum.wait()
-    ar_c = [
-        ar_copy(xs - 1 + d, sum_ref.at[cx, cc], sum_ref.at[cx, cc], x_peers[d - 1])
-        for d in range(1, xs)
-    ]
-
-    for (gkey, yy), (ukey, zz) in zip(
-        (("y", y), ("ym", ym), ("yp", yp), ("y2", y2)),
-        (("z", z), ("zm", zm), ("zp", zp), ("z2", z2)),
-    ):
-        from_zm, from_zp = gz[gkey]
-        from_ym, from_yp = uy[ukey]
-        from_zm.wait_recv()
-        send(g_ref.at[zm, yy, low], g_ref.at[zm, yy, low], to(zp, y))
-        from_ym.wait_recv()
-        send(u_ref.at[zz, ym, low], u_ref.at[zz, ym, low], to(z, yp))
-        from_zp.wait_recv()
-        send(g_ref.at[zp, yy, high], g_ref.at[zp, yy, high], to(zm, y))
-        from_yp.wait_recv()
-        send(u_ref.at[zz, yp, high], u_ref.at[zz, yp, high], to(z, ym))
 
     for c in ar_c:
         c.wait_recv()

time: 151 us -> 151 us (level)
  no operation moved by 1% of the time
where the time goes in v16:
time: 151 us; the launch traced here: 150 us
  Pallas kernels  116 us (77%)
  matrix products  24.5 us (16%)
  other arithmetic  6.14 us (4%)
  local copies, waits for them, and re-layouts  2.59 us (2%)
    pallas_call x1, Pallas kernels, gather_weights(): pl.pallas_call(gather_kernel, out_shape=(piece, piece, slots, sums), in_s...  116 us
    dot_general x1, matrix products, shards(): gate_acc = jnp.dot(normed, wg_full, preferred_element_type=jnp.float32)  11.3 us
    dot_general x1, matrix products, shards(): up_acc = jnp.dot(normed, wu_full, preferred_element_type=jnp.float32)  9.54 us

profile of v16, /device:TPU:0, one launch (start us, length us, event | category | flops | bytes accessed | tf_op | source)
XLA Modules:
  0.0 150.4 jit_solution(18125233138411872753)
XLA Ops:
  0.7 0.9 fusion.42
  1.6 0.1 copy.50
  1.7 0.2 reduce-window.4
  1.9 0.7 subtract_clamp_fusion
  2.7 0.5 multiply_cosine_fusion.1
  3.2 1.2 copy.39
  4.4 0.8 convert_add_fusion
  5.2 0.1 multiply_subtract_fusion
  5.4 1.2 fusion.27
  6.7 0.2 fusion.15
  6.9 0.8 fusion
  7.7 0.7 fusion.3
  8.5 1.2 fusion.8
  9.7 0.2 copy.43.att_ref
  9.9 0.2 fusion.29
  10.3 0.1 fusion.40
  10.4 0.4 convolution_convert_fusion.1
  10.8 0.6 fusion.33
  11.4 0.3 copy.56.kv_ref
  11.8 116.2 %shard_map.149 = (bf16[4,4,320,864]{3,2,1,0:T(8,128)(2,1)}, bf16[4,4,320,864]{3,2,1,0:T(8,128)(2,1)}, bf16[16,128,256]{2,1,0:T(8,128)(2,1)S(1)}, bf16[4,2,64,5120]{3,2,1,0:T(8,128)(2,1)}) custom-call(bf16[320,864]{1,0:T(8,128)(2,1)S(1)} %copy-done, bf16[320,864]{1,0:T(8,128)(2,1)S(1)} %copy-done.1, bf16[16,128,256]{2,1,0:T(8,128)(2,1)S(1)} %copy.56.kv_ref, ...), custom_call_target="tpu_custom_call" | custom-call | tf_op jit(solution)/shard_map/pallas_call | solution.py:263
  128.0 11.3 %fusion.55 = f32[512,864]{0,1:T(8,128)S(1)} fusion(bf16[512,5120]{1,0:T(8,128)(2,1)} %bitcast.89, bf16[5120,864]{1,0:T(8,128)(2,1)} %bitcast.88), kind=kOutput, calls=%fused_computation.91 | convolution fusion | flops 4529848320 | bytes 15859712 | tf_op jit(solution)/shard_map/dot_general | solution.py:396
  139.3 9.5 %multiply_convert_fusion = bf16[512,864]{0,1:T(8,128)(2,1)} fusion(f32[512,864]{0,1:T(8,128)S(1)} %fusion.55, bf16[512,5120]{1,0:T(8,128)(2,1)S(1)} %bitcast.90, bf16[5120,864]{1,0:T(8,128)(2,1)} %bitcast.87), kind=kOutput, calls=%fused_computation.8 | convolution fusion | flops 4532502528 | bytes 16744448 | tf_op jit(solution)/shard_map/dot_general | solution.py:397
  148.9 0.7 fusion.11
  149.6 0.7 copy.45
  (32 shorter events, 0.4 us)
Async XLA Ops:
  0.6 6.0 %copy-start.5 = (s32[512]{0:T(512)S(1)}, s32[512]{0:T(512)}, u32[]{:S(2)}) copy-start(s32[512]{0:T(512)} %param.20) | copy-start | bytes 6148
  0.6 4.7 %copy-start.3 = (bf16[512,128]{1,0:T(8,128)(2,1)S(1)}, bf16[512,128]{1,0:T(8,128)(2,1)}, u32[]{:S(2)}) copy-start(bf16[512,128]{1,0:T(8,128)(2,1)} %param.15) | copy-start | bytes 393220
  0.7 4.7 %copy-start.7 = (f32[128]{0:T(128)S(1)}, f32[128]{0:T(128)}, u32[]{:S(2)}) copy-start(f32[128]{0:T(128)} %param.18) | copy-start | bytes 1540
  6.9 1.6 %copy-start.4 = (bf16[512,128]{1,0:T(8,128)(2,1)S(1)}, bf16[512,128]{1,0:T(8,128)(2,1)}, u32[]{:S(2)}) copy-start(bf16[512,128]{1,0:T(8,128)(2,1)} %param.16) | copy-start | bytes 393220
  6.9 1.6 %copy-start.8 = (f32[128]{0:T(128)S(1)}, f32[128]{0:T(128)}, u32[]{:S(2)}) copy-start(f32[128]{0:T(128)} %param.19) | copy-start | bytes 1540
  9.7 2.1 %copy-start = (bf16[320,864]{1,0:T(8,128)(2,1)S(1)}, bf16[320,864]{1,0:T(8,128)(2,1)}, u32[]{:S(2)}) copy-start(bf16[320,864]{1,0:T(8,128)(2,1)} %wg_ref.1) | copy-start | bytes 1658884
  9.7 2.1 %copy-start.1 = (bf16[320,864]{1,0:T(8,128)(2,1)S(1)}, bf16[320,864]{1,0:T(8,128)(2,1)}, u32[]{:S(2)}) copy-start(bf16[320,864]{1,0:T(8,128)(2,1)} %wu_ref.1) | copy-start | bytes 1658884
  9.7 2.1 %copy-start.2 = (f32[5120]{0:T(1024)S(1)}, f32[5120]{0:T(1024)}, u32[]{:S(2)}) copy-start(f32[5120]{0:T(1024)} %param.25) | copy-start | bytes 61444
  128.0 11.3 %copy-start.9 = (bf16[4,2,64,5120]{3,2,1,0:T(8,128)(2,1)S(1)}, bf16[4,2,64,5120]{3,2,1,0:T(8,128)(2,1)}, u32[]{:S(2)}) copy-start(bf16[4,2,64,5120]{3,2,1,0:T(8,128)(2,1)} %get-tuple-element.6) | copy-start | bytes 15728644
  139.3 9.6 %copy-start.6 = (s32[16,4]{0,1:T(4,128)S(1)}, s32[16,4]{0,1:T(4,128)}, u32[]{:S(2)}) copy-start(s32[16,4]{0,1:T(4,128)} %param.22) | copy-start | bytes 772

commit v17 on v13

--- a/solution.py
+++ b/solution.py
@@ -117,6 +117,27 @@
     u_from_zp = send(wu_ref, u_ref.at[z, y], to(zm, y))
     gz = {"y": (send(wg_ref, g_ref.at[z, y], to(zp, y)), send(wg_ref, g_ref.at[z, y], to(zm, y)))}
     uy = {"z": (send(wu_ref, u_ref.at[z, y], to(z, yp)), send(wu_ref, u_ref.at[z, y], to(z, ym)))}
+
+
+    g_from_ym.wait_recv()
+    g_far_a = send(g_ref.at[z, ym, low], g_ref.at[z, ym, low], to(z, yp))
+    gz["ym"] = (send(g_ref.at[z, ym], g_ref.at[z, ym], to(zp, y)), send(g_ref.at[z, ym], g_ref.at[z, ym], to(zm, y)))
+    u_from_zm.wait_recv()
+    u_far_a = send(u_ref.at[zm, y, low], u_ref.at[zm, y, low], to(zp, y))
+    uy["zm"] = (send(u_ref.at[zm, y], u_ref.at[zm, y], to(z, yp)), send(u_ref.at[zm, y], u_ref.at[zm, y], to(z, ym)))
+    g_from_yp.wait_recv()
+    g_far_b = send(g_ref.at[z, yp, high], g_ref.at[z, yp, high], to(z, ym))
+    gz["yp"] = (send(g_ref.at[z, yp], g_ref.at[z, yp], to(zp, y)), send(g_ref.at[z, yp], g_ref.at[z, yp], to(zm, y)))
+    u_from_zp.wait_recv()
+    u_far_b = send(u_ref.at[zp, y, high], u_ref.at[zp, y, high], to(zm, y))
+    uy["zp"] = (send(u_ref.at[zp, y], u_ref.at[zp, y], to(z, yp)), send(u_ref.at[zp, y], u_ref.at[zp, y], to(z, ym)))
+
+    g_far_a.wait_recv()
+    g_far_b.wait_recv()
+    gz["y2"] = (send(g_ref.at[z, y2], g_ref.at[z, y2], to(zp, y)), send(g_ref.at[z, y2], g_ref.at[z, y2], to(zm, y)))
+    u_far_a.wait_recv()
+    u_far_b.wait_recv()
+    uy["z2"] = (send(u_ref.at[z2, y], u_ref.at[z2, y], to(z, yp)), send(u_ref.at[z2, y], u_ref.at[z2, y], to(z, ym)))
     kv_copies = []
     own_kv = pltpu.make_async_copy(kv_ref.at[me], kv_out.at[me], local_sems.at[2])
     own_kv.start()
@@ -157,26 +178,6 @@
     ar_b = [
         ar_copy(d, b_src.at[(cx + d) % xs], b_buf.at[cx], x_peers[d - 1]) for d in range(1, xs)
     ]
-
-    g_from_ym.wait_recv()
-    g_far_a = send(g_ref.at[z, ym, low], g_ref.at[z, ym, low], to(z, yp))
-    gz["ym"] = (send(g_ref.at[z, ym], g_ref.at[z, ym], to(zp, y)), send(g_ref.at[z, ym], g_ref.at[z, ym], to(zm, y)))
-    u_from_zm.wait_recv()
-    u_far_a = send(u_ref.at[zm, y, low], u_ref.at[zm, y, low], to(zp, y))
-    uy["zm"] = (send(u_ref.at[zm, y], u_ref.at[zm, y], to(z, yp)), send(u_ref.at[zm, y], u_ref.at[zm, y], to(z, ym)))
-    g_from_yp.wait_recv()
-    g_far_b = send(g_ref.at[z, yp, high], g_ref.at[z, yp, high], to(z, ym))
-    gz["yp"] = (send(g_ref.at[z, yp], g_ref.at[z, yp], to(zp, y)), send(g_ref.at[z, yp], g_ref.at[z, yp], to(zm, y)))
-    u_from_zp.wait_recv()
-    u_far_b = send(u_ref.at[zp, y, high], u_ref.at[zp, y, high], to(zm, y))
-    uy["zp"] = (send(u_ref.at[zp, y], u_ref.at[zp, y], to(z, yp)), send(u_ref.at[zp, y], u_ref.at[zp, y], to(z, ym)))
-
-    g_far_a.wait_recv()
-    g_far_b.wait_recv()
-    gz["y2"] = (send(g_ref.at[z, y2], g_ref.at[z, y2], to(zp, y)), send(g_ref.at[z, y2], g_ref.at[z, y2], to(zm, y)))
-    u_far_a.wait_recv()
-    u_far_b.wait_recv()
-    uy["z2"] = (send(u_ref.at[z2, y], u_ref.at[z2, y], to(z, yp)), send(u_ref.at[z2, y], u_ref.at[z2, y], to(z, ym)))
 
     for c in ar_b:
         c.wait_recv()

time: 152 us -> 183 us (1.20)
  Pallas kernels: 117 us -> 147 us
    pallas_call x1, Pallas kernels: 117 us -> 147 us  [gather_weights(): pl.pallas_call(gather_kernel, out_shape=(piece, piece, slots, sums), in_s...]
where the time goes in v17:
time: 183 us; the launch traced here: 181 us
  Pallas kernels  147 us (80%)
  matrix products  24.5 us (13%)
  other arithmetic  6.14 us (3%)
  local copies, waits for them, and re-layouts  2.59 us (1%)
    pallas_call x1, Pallas kernels, gather_weights(): pl.pallas_call(gather_kernel, out_shape=(piece, piece, slots, sums), in_s...  147 us
    dot_general x1, matrix products, shards(): gate_acc = jnp.dot(normed, wg_full, preferred_element_type=jnp.float32)  11.3 us
    dot_general x1, matrix products, shards(): up_acc = jnp.dot(normed, wu_full, preferred_element_type=jnp.float32)  9.55 us

profile of v17, /device:TPU:0, one launch (start us, length us, event | category | flops | bytes accessed | tf_op | source)
XLA Modules:
  0.0 181.3 jit_solution(9462214943778234228)
XLA Ops:
  0.7 0.9 fusion.42
  1.6 0.1 copy.50
  1.7 0.2 reduce-window.4
  1.9 0.7 subtract_clamp_fusion
  2.7 0.5 multiply_cosine_fusion.1
  3.2 1.2 copy.39
  4.4 0.8 convert_add_fusion
  5.2 0.1 multiply_subtract_fusion
  5.4 1.2 fusion.27
  6.7 0.2 fusion.15
  6.9 0.8 fusion
  7.7 0.7 fusion.3
  8.5 1.2 fusion.8
  9.7 0.2 copy.43.att_ref
  9.9 0.2 fusion.29
  10.3 0.1 fusion.40
  10.4 0.4 convolution_convert_fusion.1
  10.8 0.6 fusion.33
  11.4 0.3 copy.56.kv_ref
  11.8 147.2 %shard_map.149 = (bf16[4,4,320,864]{3,2,1,0:T(8,128)(2,1)}, bf16[4,4,320,864]{3,2,1,0:T(8,128)(2,1)}, bf16[16,128,256]{2,1,0:T(8,128)(2,1)S(1)}, bf16[4,2,64,5120]{3,2,1,0:T(8,128)(2,1)}) custom-call(bf16[320,864]{1,0:T(8,128)(2,1)S(1)} %copy-done, bf16[320,864]{1,0:T(8,128)(2,1)S(1)} %copy-done.1, bf16[16,128,256]{2,1,0:T(8,128)(2,1)S(1)} %copy.56.kv_ref, ...), custom_call_target="tpu_custom_call" | custom-call | tf_op jit(solution)/shard_map/pallas_call | solution.py:263
  159.0 11.3 %fusion.55 = f32[512,864]{0,1:T(8,128)S(1)} fusion(bf16[512,5120]{1,0:T(8,128)(2,1)} %bitcast.89, bf16[5120,864]{1,0:T(8,128)(2,1)} %bitcast.88), kind=kOutput, calls=%fused_computation.91 | convolution fusion | flops 4529848320 | bytes 15859712 | tf_op jit(solution)/shard_map/dot_general | solution.py:396
  170.3 9.5 %multiply_convert_fusion = bf16[512,864]{0,1:T(8,128)(2,1)} fusion(f32[512,864]{0,1:T(8,128)S(1)} %fusion.55, bf16[512,5120]{1,0:T(8,128)(2,1)S(1)} %bitcast.90, bf16[5120,864]{1,0:T(8,128)(2,1)} %bitcast.87), kind=kOutput, calls=%fused_computation.8 | convolution fusion | flops 4532502528 | bytes 16744448 | tf_op jit(solution)/shard_map/dot_general | solution.py:397
  179.9 0.7 fusion.11
  180.6 0.7 copy.45
  (32 shorter events, 0.4 us)
Async XLA Ops:
  0.6 6.0 %copy-start.5 = (s32[512]{0:T(512)S(1)}, s32[512]{0:T(512)}, u32[]{:S(2)}) copy-start(s32[512]{0:T(512)} %param.20) | copy-start | bytes 6148
  0.6 4.7 %copy-start.3 = (bf16[512,128]{1,0:T(8,128)(2,1)S(1)}, bf16[512,128]{1,0:T(8,128)(2,1)}, u32[]{:S(2)}) copy-start(bf16[512,128]{1,0:T(8,128)(2,1)} %param.15) | copy-start | bytes 393220
  0.7 4.7 %copy-start.7 = (f32[128]{0:T(128)S(1)}, f32[128]{0:T(128)}, u32[]{:S(2)}) copy-start(f32[128]{0:T(128)} %param.18) | copy-start | bytes 1540
  6.9 1.6 copy-start.4
  6.9 1.6 copy-start.8
  9.7 2.1 %copy-start = (bf16[320,864]{1,0:T(8,128)(2,1)S(1)}, bf16[320,864]{1,0:T(8,128)(2,1)}, u32[]{:S(2)}) copy-start(bf16[320,864]{1,0:T(8,128)(2,1)} %wg_ref.1) | copy-start | bytes 1658884
  9.7 2.1 %copy-start.1 = (bf16[320,864]{1,0:T(8,128)(2,1)S(1)}, bf16[320,864]{1,0:T(8,128)(2,1)}, u32[]{:S(2)}) copy-start(bf16[320,864]{1,0:T(8,128)(2,1)} %wu_ref.1) | copy-start | bytes 1658884
  9.7 2.1 %copy-start.2 = (f32[5120]{0:T(1024)S(1)}, f32[5120]{0:T(1024)}, u32[]{:S(2)}) copy-start(f32[5120]{0:T(1024)} %param.25) | copy-start | bytes 61444
  159.0 11.3 %copy-start.9 = (bf16[4,2,64,5120]{3,2,1,0:T(8,128)(2,1)S(1)}, bf16[4,2,64,5120]{3,2,1,0:T(8,128)(2,1)}, u32[]{:S(2)}) copy-start(bf16[4,2,64,5120]{3,2,1,0:T(8,128)(2,1)} %get-tuple-element.6) | copy-start | bytes 15728644
  170.2 9.6 %copy-start.6 = (s32[16,4]{0,1:T(4,128)S(1)}, s32[16,4]{0,1:T(4,128)}, u32[]{:S(2)}) copy-start(s32[16,4]{0,1:T(4,128)} %param.22) | copy-start | bytes 772

commit v18 on v15

--- a/solution.py
+++ b/solution.py
@@ -12,7 +12,7 @@
 REQS = 4
 RING = 4
 KV_SEMS = 40
-AR_TILE = 512
+AR_TILE = 1024
 
 
 THETA = 1000000.0

time: 151 us -> 151 us (level)
  no operation moved by 1% of the time
where the time goes in v18:
time: 151 us; the launch traced here: 150 us
  Pallas kernels  116 us (77%)
  matrix products  24.5 us (16%)
  other arithmetic  6.14 us (4%)
  local copies, waits for them, and re-layouts  2.59 us (2%)
    pallas_call x1, Pallas kernels, gather_weights(): pl.pallas_call(gather_kernel, out_shape=(piece, piece, slots, sums), in_s...  116 us
    dot_general x1, matrix products, shards(): gate_acc = jnp.dot(normed, wg_full, preferred_element_type=jnp.float32)  11.3 us
    dot_general x1, matrix products, shards(): up_acc = jnp.dot(normed, wu_full, preferred_element_type=jnp.float32)  9.54 us

profile of v18, /device:TPU:0, one launch (start us, length us, event | category | flops | bytes accessed | tf_op | source)
XLA Modules:
  0.0 150.3 jit_solution(1618887514121964676)
XLA Ops:
  0.7 0.9 fusion.42
  1.6 0.1 copy.50
  1.7 0.2 reduce-window.4
  1.9 0.7 subtract_clamp_fusion
  2.7 0.5 multiply_cosine_fusion.1
  3.2 1.2 copy.39
  4.4 0.8 convert_add_fusion
  5.2 0.1 multiply_subtract_fusion
  5.4 1.2 fusion.27
  6.7 0.2 fusion.15
  6.9 0.8 fusion
  7.7 0.7 fusion.3
  8.5 1.2 fusion.8
  9.7 0.2 copy.43.att_ref
  9.9 0.2 fusion.29
  10.3 0.1 fusion.40
  10.4 0.4 convolution_convert_fusion.1
  10.8 0.6 fusion.33
  11.4 0.3 copy.56.kv_ref
  11.8 116.1 %shard_map.149 = (bf16[4,4,320,864]{3,2,1,0:T(8,128)(2,1)}, bf16[4,4,320,864]{3,2,1,0:T(8,128)(2,1)}, bf16[16,128,256]{2,1,0:T(8,128)(2,1)S(1)}, bf16[4,2,64,5120]{3,2,1,0:T(8,128)(2,1)}) custom-call(bf16[320,864]{1,0:T(8,128)(2,1)S(1)} %copy-done, bf16[320,864]{1,0:T(8,128)(2,1)S(1)} %copy-done.1, bf16[16,128,256]{2,1,0:T(8,128)(2,1)S(1)} %copy.56.kv_ref, ...), custom_call_target="tpu_custom_call" | custom-call | tf_op jit(solution)/shard_map/pallas_call | solution.py:262
  127.9 11.3 %fusion.55 = f32[512,864]{0,1:T(8,128)S(1)} fusion(bf16[512,5120]{1,0:T(8,128)(2,1)} %bitcast.89, bf16[5120,864]{1,0:T(8,128)(2,1)} %bitcast.88), kind=kOutput, calls=%fused_computation.91 | convolution fusion | flops 4529848320 | bytes 15859712 | tf_op jit(solution)/shard_map/dot_general | solution.py:395
  139.2 9.5 %multiply_convert_fusion = bf16[512,864]{0,1:T(8,128)(2,1)} fusion(f32[512,864]{0,1:T(8,128)S(1)} %fusion.55, bf16[512,5120]{1,0:T(8,128)(2,1)S(1)} %bitcast.90, bf16[5120,864]{1,0:T(8,128)(2,1)} %bitcast.87), kind=kOutput, calls=%fused_computation.8 | convolution fusion | flops 4532502528 | bytes 16744448 | tf_op jit(solution)/shard_map/dot_general | solution.py:396
  148.9 0.7 fusion.11
  149.5 0.7 copy.45
  (32 shorter events, 0.4 us)
Async XLA Ops:
  0.6 6.0 %copy-start.5 = (s32[512]{0:T(512)S(1)}, s32[512]{0:T(512)}, u32[]{:S(2)}) copy-start(s32[512]{0:T(512)} %param.20) | copy-start | bytes 6148
  0.6 4.7 %copy-start.3 = (bf16[512,128]{1,0:T(8,128)(2,1)S(1)}, bf16[512,128]{1,0:T(8,128)(2,1)}, u32[]{:S(2)}) copy-start(bf16[512,128]{1,0:T(8,128)(2,1)} %param.15) | copy-start | bytes 393220
  0.7 4.7 %copy-start.7 = (f32[128]{0:T(128)S(1)}, f32[128]{0:T(128)}, u32[]{:S(2)}) copy-start(f32[128]{0:T(128)} %param.18) | copy-start | bytes 1540
  6.9 1.6 %copy-start.4 = (bf16[512,128]{1,0:T(8,128)(2,1)S(1)}, bf16[512,128]{1,0:T(8,128)(2,1)}, u32[]{:S(2)}) copy-start(bf16[512,128]{1,0:T(8,128)(2,1)} %param.16) | copy-start | bytes 393220
  6.9 1.6 %copy-start.8 = (f32[128]{0:T(128)S(1)}, f32[128]{0:T(128)}, u32[]{:S(2)}) copy-start(f32[128]{0:T(128)} %param.19) | copy-start | bytes 1540
  9.7 2.1 %copy-start = (bf16[320,864]{1,0:T(8,128)(2,1)S(1)}, bf16[320,864]{1,0:T(8,128)(2,1)}, u32[]{:S(2)}) copy-start(bf16[320,864]{1,0:T(8,128)(2,1)} %wg_ref.1) | copy-start | bytes 1658884
  9.7 2.1 %copy-start.1 = (bf16[320,864]{1,0:T(8,128)(2,1)S(1)}, bf16[320,864]{1,0:T(8,128)(2,1)}, u32[]{:S(2)}) copy-start(bf16[320,864]{1,0:T(8,128)(2,1)} %wu_ref.1) | copy-start | bytes 1658884
  9.7 2.1 %copy-start.2 = (f32[5120]{0:T(1024)S(1)}, f32[5120]{0:T(1024)}, u32[]{:S(2)}) copy-start(f32[5120]{0:T(1024)} %param.25) | copy-start | bytes 61444
  127.9 11.3 %copy-start.9 = (bf16[4,2,64,5120]{3,2,1,0:T(8,128)(2,1)S(1)}, bf16[4,2,64,5120]{3,2,1,0:T(8,128)(2,1)}, u32[]{:S(2)}) copy-start(bf16[4,2,64,5120]{3,2,1,0:T(8,128)(2,1)} %get-tuple-element.6) | copy-start | bytes 15728644
  139.2 9.6 %copy-start.6 = (s32[16,4]{0,1:T(4,128)S(1)}, s32[16,4]{0,1:T(4,128)}, u32[]{:S(2)}) copy-start(s32[16,4]{0,1:T(4,128)} %param.22) | copy-start | bytes 772

commit v19 on v18

--- a/solution.py
+++ b/solution.py
@@ -12,7 +12,7 @@
 REQS = 4
 RING = 4
 KV_SEMS = 40
-AR_TILE = 1024
+AR_TILE = 1280
 
 
 THETA = 1000000.0

time: 151 us -> 151 us (level)
  no operation moved by 1% of the time
where the time goes in v19:
time: 151 us; the launch traced here: 150 us
  Pallas kernels  116 us (77%)
  matrix products  24.5 us (16%)
  other arithmetic  6.14 us (4%)
  local copies, waits for them, and re-layouts  2.59 us (2%)
    pallas_call x1, Pallas kernels, gather_weights(): pl.pallas_call(gather_kernel, out_shape=(piece, piece, slots, sums), in_s...  116 us
    dot_general x1, matrix products, shards(): gate_acc = jnp.dot(normed, wg_full, preferred_element_type=jnp.float32)  11.3 us
    dot_general x1, matrix products, shards(): up_acc = jnp.dot(normed, wu_full, preferred_element_type=jnp.float32)  9.54 us

profile of v19, /device:TPU:0, one launch (start us, length us, event | category | flops | bytes accessed | tf_op | source)
XLA Modules:
  0.0 150.3 jit_solution(18404558853635490880)
XLA Ops:
  0.7 0.9 fusion.42
  1.6 0.1 copy.50
  1.7 0.2 reduce-window.4
  1.9 0.7 subtract_clamp_fusion
  2.7 0.5 multiply_cosine_fusion.1
  3.2 1.2 copy.39
  4.4 0.8 convert_add_fusion
  5.2 0.1 multiply_subtract_fusion
  5.4 1.2 fusion.27
  6.7 0.2 fusion.15
  6.9 0.8 fusion
  7.7 0.7 fusion.3
  8.5 1.2 fusion.8
  9.7 0.2 copy.43.att_ref
  9.9 0.2 fusion.29
  10.3 0.1 fusion.40
  10.4 0.4 convolution_convert_fusion.1
  10.8 0.6 fusion.33
  11.4 0.3 copy.56.kv_ref
  11.8 116.1 %shard_map.149 = (bf16[4,4,320,864]{3,2,1,0:T(8,128)(2,1)}, bf16[4,4,320,864]{3,2,1,0:T(8,128)(2,1)}, bf16[16,128,256]{2,1,0:T(8,128)(2,1)S(1)}, bf16[4,2,64,5120]{3,2,1,0:T(8,128)(2,1)}) custom-call(bf16[320,864]{1,0:T(8,128)(2,1)S(1)} %copy-done, bf16[320,864]{1,0:T(8,128)(2,1)S(1)} %copy-done.1, bf16[16,128,256]{2,1,0:T(8,128)(2,1)S(1)} %copy.56.kv_ref, ...), custom_call_target="tpu_custom_call" | custom-call | tf_op jit(solution)/shard_map/pallas_call | solution.py:262
  127.9 11.3 %fusion.55 = f32[512,864]{0,1:T(8,128)S(1)} fusion(bf16[512,5120]{1,0:T(8,128)(2,1)} %bitcast.89, bf16[5120,864]{1,0:T(8,128)(2,1)} %bitcast.88), kind=kOutput, calls=%fused_computation.91 | convolution fusion | flops 4529848320 | bytes 15859712 | tf_op jit(solution)/shard_map/dot_general | solution.py:395
  139.2 9.5 %multiply_convert_fusion = bf16[512,864]{0,1:T(8,128)(2,1)} fusion(f32[512,864]{0,1:T(8,128)S(1)} %fusion.55, bf16[512,5120]{1,0:T(8,128)(2,1)S(1)} %bitcast.90, bf16[5120,864]{1,0:T(8,128)(2,1)} %bitcast.87), kind=kOutput, calls=%fused_computation.8 | convolution fusion | flops 4532502528 | bytes 16744448 | tf_op jit(solution)/shard_map/dot_general | solution.py:396
  148.9 0.7 fusion.11
  149.5 0.7 copy.45
  (32 shorter events, 0.4 us)
Async XLA Ops:
  0.6 6.0 %copy-start.5 = (s32[512]{0:T(512)S(1)}, s32[512]{0:T(512)}, u32[]{:S(2)}) copy-start(s32[512]{0:T(512)} %param.20) | copy-start | bytes 6148
  0.6 4.7 %copy-start.3 = (bf16[512,128]{1,0:T(8,128)(2,1)S(1)}, bf16[512,128]{1,0:T(8,128)(2,1)}, u32[]{:S(2)}) copy-start(bf16[512,128]{1,0:T(8,128)(2,1)} %param.15) | copy-start | bytes 393220
  0.7 4.7 %copy-start.7 = (f32[128]{0:T(128)S(1)}, f32[128]{0:T(128)}, u32[]{:S(2)}) copy-start(f32[128]{0:T(128)} %param.18) | copy-start | bytes 1540
  6.9 1.6 %copy-start.4 = (bf16[512,128]{1,0:T(8,128)(2,1)S(1)}, bf16[512,128]{1,0:T(8,128)(2,1)}, u32[]{:S(2)}) copy-start(bf16[512,128]{1,0:T(8,128)(2,1)} %param.16) | copy-start | bytes 393220
  6.9 1.6 %copy-start.8 = (f32[128]{0:T(128)S(1)}, f32[128]{0:T(128)}, u32[]{:S(2)}) copy-start(f32[128]{0:T(128)} %param.19) | copy-start | bytes 1540
  9.7 2.1 %copy-start = (bf16[320,864]{1,0:T(8,128)(2,1)S(1)}, bf16[320,864]{1,0:T(8,128)(2,1)}, u32[]{:S(2)}) copy-start(bf16[320,864]{1,0:T(8,128)(2,1)} %wg_ref.1) | copy-start | bytes 1658884
  9.7 2.1 %copy-start.1 = (bf16[320,864]{1,0:T(8,128)(2,1)S(1)}, bf16[320,864]{1,0:T(8,128)(2,1)}, u32[]{:S(2)}) copy-start(bf16[320,864]{1,0:T(8,128)(2,1)} %wu_ref.1) | copy-start | bytes 1658884
  9.7 2.1 %copy-start.2 = (f32[5120]{0:T(1024)S(1)}, f32[5120]{0:T(1024)}, u32[]{:S(2)}) copy-start(f32[5120]{0:T(1024)} %param.25) | copy-start | bytes 61444
  127.9 11.3 %copy-start.9 = (bf16[4,2,64,5120]{3,2,1,0:T(8,128)(2,1)S(1)}, bf16[4,2,64,5120]{3,2,1,0:T(8,128)(2,1)}, u32[]{:S(2)}) copy-start(bf16[4,2,64,5120]{3,2,1,0:T(8,128)(2,1)} %get-tuple-element.6) | copy-start | bytes 15728644
  139.2 9.6 %copy-start.6 = (s32[16,4]{0,1:T(4,128)S(1)}, s32[16,4]{0,1:T(4,128)}, u32[]{:S(2)}) copy-start(s32[16,4]{0,1:T(4,128)} %param.22) | copy-start | bytes 772
